TPU v7x, 768 devices: a whole 4x8x12 slice. The times are simulated.
768 devices in a mesh: lon: 96 (over z, y), lat: 4 (over x_hi, core), rep: 2 (over x_lo).
Axes of the slice: x: 4 (x_hi: 2, x_lo: 2; x = x_hi * 2 + x_lo), y: 8, z: 12, core: 2. Of those that a mesh axis runs over, the one named last changes fastest.
Arguments:
- tokens: bfloat16 [2, 48, 1152, 192], P(None, ('lat', 'rep'), 'lon'), may hold values from -6 to 6
- cotangent: bfloat16 [2, 48, 1152, 192], P(None, ('lat', 'rep'), 'lon'), may hold values from -6 to 6
- region: int32 [2, 48, 1152], P(None, ('lat', 'rep'), 'lon'), may hold values from 0 to 2
- pos_index: int32 [144, 144], replicated, may hold values from 0 to 3311
- w_qkv: bfloat16 [192, 576], replicated, may hold values from -0.4375 to 0.4375
- w_proj: bfloat16 [192, 192], replicated, may hold values from -0.4375 to 0.4375
- bias_table: float32 [3312, 8, 6], P(None, ('lat', 'rep')), may hold values from -4 to 247
Outputs:
- grad_tokens: bfloat16 [2, 48, 1152, 192], P(None, ('lat', 'rep'), 'lon')
- grad_qkv: float32 [192, 576], replicated
- grad_proj: float32 [192, 192], replicated
- grad_bias: float32 [3312, 8, 6], P(None, ('lat', 'rep'))
All inputs are finite; a program needn't handle non-finite values.
Results may differ from a plain program's by a relative error of at most 0.0096.
Values may be sent and summed in bfloat16 or wider, within the bound.
No kernel may reach another device: no remote copies, remote signals or barrier semaphores. Data moves between devices by JAX's collectives and lax.ppermute only.
A program may use at most 64 MiB of HBM per device.

v0:
```python
import jax
import jax.numpy as jnp
from jax import lax
from jax.sharding import PartitionSpec as P


def passed_along(block, axis, distance):
    devices = range(lax.axis_size(axis))
    route = [((i - distance) % len(devices), i) for i in devices]
    return lax.ppermute(block, axis, route)


def contract(form, left, right):
    return jnp.einsum(form, left, right, preferred_element_type=jnp.float32)


def window_grads(shifted, shifted_cot, region, pos_index, w_qkv, w_proj, bias_table):
    levels, lats, lons, width = shifted.shape
    pl_win, lat_win, lon_win = (levels // 2, lats // 6, lons // 12)
    heads = bias_table.shape[2]
    head_dim = width // heads
    scale = head_dim ** (-0.5)

    def windows_of(tensor):
        depth = tensor.shape[-1]
        tensor = tensor.reshape(pl_win, 2, lat_win, 6, lon_win, 12, depth)
        tensor = tensor.transpose(0, 2, 4, 1, 3, 5, 6)
        return tensor.reshape(pl_win, lat_win, lon_win, 144, depth)

    values = shifted.astype(jnp.float32)
    center = values - jnp.mean(values, axis=-1, keepdims=True)
    inv_std = lax.rsqrt(jnp.mean(center * center, axis=-1, keepdims=True) + 1e-05)
    normed = center * inv_std
    hidden = windows_of(normed.astype(jnp.bfloat16))
    projected = contract("pabtc,cf->pabtf", hidden, w_qkv).astype(jnp.bfloat16)
    projected = projected.reshape(pl_win, lat_win, lon_win, 144, 3, heads, head_dim)
    query_rows = projected[:, :, :, :, 0]
    key_rows = projected[:, :, :, :, 1]
    value_rows = projected[:, :, :, :, 2]
    table_rows = bias_table[pos_index].reshape(144, 144, lat_win, pl_win, heads)
    table_rows = table_rows.transpose(3, 2, 4, 0, 1)[:, :, None]
    labels = windows_of(region[..., None])[..., 0]
    same = (labels[..., :, None] == labels[..., None, :])[:, :, :, None]
    scores = contract("pabqhd,pabkhd->pabhqk", query_rows, key_rows) * scale + table_rows
    scores = jnp.where(same, scores, -1000000000.0)
    top = jnp.max(scores, axis=-1, keepdims=True)
    exponent = jnp.exp(scores - top)
    probability = exponent / jnp.sum(exponent, axis=-1, keepdims=True)
    prob_half = probability.astype(jnp.bfloat16)
    attended = contract("pabhqk,pabkhd->pabqhd", prob_half, value_rows).astype(jnp.bfloat16)
    attended = attended.reshape(pl_win, lat_win, lon_win, 144, width)
    cot_win = windows_of(shifted_cot)
    grad_proj = contract("pabtc,pabtf->cf", attended, cot_win)
    grad_att = contract("pabtf,cf->pabtc", cot_win, w_proj).astype(jnp.bfloat16)
    grad_att = grad_att.reshape(pl_win, lat_win, lon_win, 144, heads, head_dim)
    grad_prob = contract("pabqhd,pabkhd->pabhqk", grad_att, value_rows)
    grad_value = contract("pabhqk,pabqhd->pabkhd", prob_half, grad_att)
    grad_scores = probability * (
        grad_prob - jnp.sum(grad_prob * probability, axis=-1, keepdims=True)
    )
    folded = (
        jnp.sum(grad_scores, axis=2)
        .transpose(3, 4, 1, 0, 2)
        .reshape(144 * 144, lat_win * pl_win * heads)
    )
    grad_bias = jax.ops.segment_sum(folded, pos_index.reshape(-1), num_segments=bias_table.shape[0])
    grad_bias = grad_bias.reshape(bias_table.shape)
    scores_half = grad_scores.astype(jnp.bfloat16)
    grad_query = contract("pabhqk,pabkhd->pabqhd", scores_half, key_rows) * scale
    grad_key = contract("pabhqk,pabqhd->pabkhd", scores_half, query_rows) * scale
    grad_in = jnp.stack((grad_query, grad_key, grad_value), axis=4).astype(jnp.bfloat16)
    grad_in = grad_in.reshape(pl_win, lat_win, lon_win, 144, 3 * width)
    grad_qkv = contract("pabtc,pabtf->cf", hidden, grad_in)
    tensor = contract("pabtf,cf->pabtc", grad_in, w_qkv)
    depth = tensor.shape[-1]
    tensor = tensor.reshape(pl_win, lat_win, lon_win, 2, 6, 12, depth)
    tensor = tensor.transpose(0, 3, 1, 4, 2, 5, 6)
    grad_hidden = tensor.reshape(levels, lats, lons, depth)
    grad_norm = inv_std * (
        grad_hidden
        - jnp.mean(grad_hidden, axis=-1, keepdims=True)
        - normed * jnp.mean(grad_hidden * normed, axis=-1, keepdims=True)
    )
    grad_shifted = shifted_cot.astype(jnp.float32) + grad_norm
    return (grad_shifted, grad_qkv, grad_proj, grad_bias)


def roll_lon(stacked, forward):
    half_width = stacked.shape[3] // 2
    if forward:
        kept_part, strip_part, offset = (
            stacked[:, :, :, half_width:],
            stacked[:, :, :, :half_width],
            -1,
        )
    else:
        kept_part, strip_part, offset = (
            stacked[:, :, :, :-half_width],
            stacked[:, :, :, -half_width:],
            1,
        )
    arrived = passed_along(strip_part, "lon", offset)
    if forward:
        return jnp.concatenate((kept_part, arrived), axis=3)
    return jnp.concatenate((arrived, kept_part), axis=3)


def roll_lat(stacked, forward):
    rows_moved = 3
    if forward:
        kept_part, strip_part, offset = (stacked[:, :, rows_moved:], stacked[:, :, :rows_moved], -1)
    else:
        kept_part, strip_part, offset = (
            stacked[:, :, :-rows_moved],
            stacked[:, :, -rows_moved:],
            1,
        )
    arrived = passed_along(strip_part, ("lat", "rep"), offset)
    if forward:
        return jnp.concatenate((kept_part, arrived), axis=2)
    return jnp.concatenate((arrived, kept_part), axis=2)


def local(tokens, cotangent, region, pos_index, w_qkv, w_proj, bias_table):
    stacked = jnp.roll(jnp.stack((tokens, cotangent)), -1, axis=1)
    stacked = roll_lon(stacked, True)
    stacked = roll_lat(stacked, True)
    grad_shifted, grad_qkv, grad_proj, grad_bias = window_grads(
        stacked[0], stacked[1], region, pos_index, w_qkv, w_proj, bias_table
    )
    returned = grad_shifted.astype(jnp.bfloat16)[None]
    returned = roll_lat(returned, False)
    returned = roll_lon(returned, False)
    grad_tokens = jnp.roll(returned[0], 1, axis=0)
    grad_bias = lax.psum(grad_bias, "lon")
    grad_qkv, grad_proj = lax.psum((grad_qkv, grad_proj), ("lon", "lat", "rep"))
    return (grad_tokens, grad_qkv, grad_proj, grad_bias)


def solution(mesh):
    placed = (
        P(None, ("lat", "rep"), "lon", None),
        P(None, ("lat", "rep"), "lon", None),
        P(None, ("lat", "rep"), "lon"),
        P(),
        P(),
        P(),
        P(None, ("lat", "rep"), None),
    )
    return jax.shard_map(
        local,
        mesh=mesh,
        in_specs=placed,
        out_specs=(P(None, ("lat", "rep"), "lon", None), P(), P(), P(None, ("lat", "rep"), None)),
        check_vma=False,
    )
```

profile of v0, /device:TPU:1, one launch (start us, length us, event | category | flops | bytes accessed | tf_op | source)
XLA Modules:
  0.0 946.0 jit_solution(10527690244703705678)
XLA Ops:
  7.2 0.0 copy-start
  7.2 0.0 all-reduce.4.cloned.1.call-start
  7.2 1.0 copy_bitcast_fusion
  8.4 18.0 %collective-permute-start = (bf16[2,2,6,6,192]{4,3,2,1,0:T(8,128)(2,1)S(1)}, bf16[2,2,6,6,192]{4,3,2,1,0:T(8,128)(2,1)S(1)}, u32[]{:S(2)}, u32[]{:S(2)}) collective-permute-start(bf16[2,2,6,6,192]{4,3,2,1,0:T(8,128)(2,1)S(1)} %get-tuple-element.23), channel_id=1, source_target_pairs={{8,0},{16,8},{24,16},{32,24},{40,32},{48,40},{56,48},{64,56},{72,6... | collective-permute-start | bytes 165896 | tf_op jit(solution)/shard_map/ppermute | solution.py:10
  26.4 0.9 compare_select_fusion
  27.3 0.1 reshape.305
  27.5 0.7 copy.28
  28.2 0.1 eq.21
  28.3 0.0 collective-permute-done
  28.3 0.1 fusion.20
  28.4 4.3 collective-permute-start.1
  32.6 0.1 broadcast_compare_fusion
  32.7 1.7 reshape.313
  34.4 1.4 copy.29
  35.8 38.7 %gather_fusion = f32[20736,6]{1,0:T(8,128)} fusion(f32[3312,6]{1,0:T(8,128)S(1)} %bitcast.99, s32[21504]{0:T(1024)S(1)} %pad_clamp_fusion), kind=kCustom, calls=%fused_computation | custom fusion | bytes 1078272 | tf_op jit(solution)/shard_map/gather | solution.py:40
  74.5 11.7 %copy.31 = f32[144,144,1,1,6]{0,1,4,2,3:T(8,128)S(1)} copy(f32[144,144,1,1,6]{4,1,0,3,2:T(8,128)} %bitcast.100) | data formatting | bytes 995328 | tf_op jit(solution)/shard_map/reshape | solution.py:40
  86.2 0.0 collective-permute-done.1
  86.2 0.1 convert_reduce_fusion
  86.3 0.2 multiply_reduce_fusion.2
  86.5 0.1 div.25
  86.7 0.0 copy-start.2
  86.7 0.0 copy-done.5
  86.7 0.0 copy-start.3
  86.7 0.2 convolution_convert_fusion.2
  86.9 0.1 copy.32
  87.0 0.3 copy-done.3
  87.3 0.1 rsqrt.13
  87.4 0.0 copy-done
  87.4 0.3 convolution_convert_fusion
  87.7 0.2 copy.27
  87.9 0.3 fusion.4
  88.2 0.8 fusion.30
  89.0 0.0 copy-start.6
  89.0 0.3 convolution_bitcast_fusion
  89.4 0.3 multiply_reduce_fusion
  89.7 0.1 fusion.9
  89.9 0.2 fusion.5
  90.1 0.2 fusion.6
  90.3 0.8 multiply_convert_fusion
  91.1 0.1 maximum_convert_fusion
  91.2 0.5 copy.36
  91.6 0.6 convert_element_type.99
  92.2 0.0 copy-start.4
  92.2 0.4 fusion.27
  92.6 1.1 fusion.18
  93.7 1.9 collective-permute-start.2
  95.6 0.9 convert_element_type.102
  96.6 1.1 fusion.31
  97.6 1.2 convolution_convert_fusion.1
  98.9 10.4 %copy.49 = f32[144,144,1,1,6]{4,1,0,3,2:T(8,128)} copy(f32[144,144,1,1,6]{0,1,4,2,3:T(8,128)S(1)} %get-tuple-element.18) | data formatting | bytes 995328 | tf_op jit(solution)/shard_map/reshape | solution.py:64
  109.2 113.6 %scatter_custom_fusion = f32[3312,6]{1,0:T(8,128)} fusion(s32[20736]{0:T(1024)} %reshape.313, f32[20736,6]{1,0:T(8,128)} %bitcast.101, f32[]{:T(128)} %constant.8.clone.1), kind=kCustom, calls=%fused_computation.18 | custom fusion | flops 124416 | bytes 80000 | tf_op jit(solution)/shard_map/scatter-add | solution.py:66
  222.9 0.0 all-reduce.4.cloned.1.call-update
  222.9 0.0 all-reduce.6.cloned.1.call-start
  223.0 0.0 collective-permute-done.2
  223.0 1.9 collective-permute-start.3
  224.9 0.8 fusion.32
  225.8 0.0 all-reduce.6.cloned.1.call-update
  225.8 6.0 collective-permute-done.3
  231.9 0.7 copy.40
  232.6 219.2 %all-reduce.4.cloned.1.call-done = f32[3312,1,6]{2,0,1:T(8,128)} async-done(((f32[3312,1,6]{2,0,1:T(8,128)}), f32[3312,1,6]{2,0,1:T(8,128)}) %all-reduce.4.cloned.1.call-update) | async-done | bytes 79504 | tf_op jit(solution)/shard_map/psum | solution.py:135
  451.8 2.6 copy.41
  454.4 481.3 %all-reduce.6.cloned.1.call-done = (f32[192,576]{1,0:T(8,128)}, f32[192,192]{1,0:T(8,128)}) async-done(((f32[192,576]{1,0:T(8,128)}, f32[192,192]{1,0:T(8,128)}), (f32[192,576]{1,0:T(8,128)}, f32[192,192]{1,0:T(8,128)})) %all-reduce.6.cloned.1.call-update) | async-done | bytes 589840 | tf_op jit(solution)/shard_map/psum | solution.py:136
  935.7 1.8 copy.56
  937.5 1.6 copy.57
  (22 shorter events, 0.4 us)
Async XLA Ops:
  7.2 80.3 %copy-start = (bf16[192,576]{1,0:T(8,128)(2,1)S(1)}, bf16[192,576]{1,0:T(8,128)(2,1)}, u32[]{:S(2)}) copy-start(bf16[192,576]{1,0:T(8,128)(2,1)} %param.11) | copy-start | bytes 663556
  7.2 444.7 %all-reduce.4.cloned.1.call-start = ((), (), s32[]{:S(2)}) async-start(), calls=%async_computation | async-start | bytes 3391488 | tf_op jit(solution)/shard_map/psum | solution.py:135
  8.4 19.9 %collective-permute-start = (bf16[2,2,6,6,192]{4,3,2,1,0:T(8,128)(2,1)S(1)}, bf16[2,2,6,6,192]{4,3,2,1,0:T(8,128)(2,1)S(1)}, u32[]{:S(2)}, u32[]{:S(2)}) collective-permute-start(bf16[2,2,6,6,192]{4,3,2,1,0:T(8,128)(2,1)S(1)} %get-tuple-element.23), channel_id=1, source_target_pairs={{8,0},{16,8},{24,16},{32,24},{40,32},{48,40},{56,48},{64,56},{72,6... | collective-permute-start | bytes 165896 | tf_op jit(solution)/shard_map/ppermute | solution.py:10
  28.4 57.8 %collective-permute-start.1 = (bf16[2,2,3,12,192]{4,3,2,1,0:T(8,128)(2,1)S(1)}, bf16[2,2,3,12,192]{4,3,2,1,0:T(8,128)(2,1)S(1)}, u32[]{:S(2)}, u32[]{:S(2)}) collective-permute-start(bf16[2,2,3,12,192]{4,3,2,1,0:T(8,128)(2,1)S(1)} %get-tuple-element.21), channel_id=1, source_target_pairs={{1,0},{2,1},{3,2},{4,3},{5,4},{6,5},{7,6},{0,7},{9,8},{10,9},{11,1... | collective-permute-start | bytes 165896 | tf_op jit(solution)/shard_map/ppermute | solution.py:10
  74.5 12.2 %copy-start.5 = (bf16[192,192]{1,0:T(8,128)(2,1)S(1)}, bf16[192,192]{1,0:T(8,128)(2,1)}, u32[]{:S(2)}) copy-start(bf16[192,192]{1,0:T(8,128)(2,1)} %param.12) | copy-start | bytes 221188
  86.7 1.2 copy-start.2
  86.7 0.6 copy-start.3
  87.9 3.2 copy-start.1
  89.0 2.1 copy-start.6
  92.2 132.7 %copy-start.4 = (bf16[144,192]{1,0:T(8,128)(2,1)S(1)}, bf16[144,192]{1,0:T(8,128)(2,1)}, u32[]{:S(2)}) copy-start(bf16[144,192]{1,0:T(8,128)(2,1)} %copy-done.3) | copy-start | bytes 165892
  93.7 129.3 %collective-permute-start.2 = (bf16[1,2,3,12,192]{4,3,2,1,0:T(8,128)(2,1)S(1)}, bf16[1,2,3,12,192]{4,3,2,1,0:T(8,128)(2,1)S(1)}, u32[]{:S(2)}, u32[]{:S(2)}) collective-permute-start(bf16[1,2,3,12,192]{4,3,2,1,0:T(8,128)(2,1)S(1)} %get-tuple-element.26), channel_id=1, source_target_pairs={{7,0},{0,1},{1,2},{2,3},{3,4},{4,5},{5,6},{6,7},{15,8},{8,9},{9,10... | collective-permute-start | bytes 82952 | tf_op jit(solution)/shard_map/ppermute | solution.py:10
  222.9 712.8 %all-reduce.6.cloned.1.call-start = ((), (), s32[]{:S(2)}) async-start(), calls=%async_computation.1 | async-start | bytes 1376256 | tf_op jit(solution)/shard_map/psum | solution.py:136
  223.0 8.8 collective-permute-start.3
Sparse Core Ops, SparseCore 0:
  223.0 228.7 all-reduce.3
  458.1 477.5 all-reduce.5
where the time goes:
time: 947 us; the launch traced here: 946 us
  waiting for transfers between devices  707 us (75%)
  other arithmetic  118 us (12%)
  local copies, waits for them, and re-layouts  75.3 us (8%)
  starting transfers between devices  26.2 us (3%)
  between operations  14.4 us (2%)
    psum x1, waiting for transfers between devices, local(): grad_qkv, grad_proj = lax.psum((grad_qkv, grad_proj), ('lon', 'lat', 'rep'))  481 us
    psum x1, waiting for transfers between devices, local(): grad_bias = lax.psum(grad_bias, 'lon')  219 us
    scatter-add x1, other arithmetic, window_grads(): jax.ops.segment_sum(folded, pos_index.reshape(-1), num_segments=bias_tabl...  114 us
    gather x1, local copies, waits for them, and re-layouts, window_grads(): table_rows = bias_table[pos_index].reshape(144, 144, lat_win, pl_win, heads)  38.7 us
    ppermute x4, starting transfers between devices, passed_along(): return lax.ppermute(block, axis, route)  26.1 us
  transfers between devices with their start and end apart: 6, of which 3 were waited for; matrix products, arithmetic and copies ran while one was open for 20% of the time, Pallas kernels for 0%

commit v1 on v0

v1 whole, which is shorter than its diff:
```python
import functools

import jax
import jax.numpy as jnp
import numpy as np
from jax import lax
from jax.experimental import pallas as pl
from jax.experimental.pallas import tpu as pltpu
from jax.sharding import PartitionSpec as P

F32 = jnp.float32
BF16 = jnp.bfloat16
T = 144
C = 192
HEADS = 6
HD = 32
ROWS = 3312
BLKS = 26
PACK = 168
QUADS = ((3, 6), (3, 0), (0, 6), (0, 0))
PARAMS = pltpu.CompilerParams(vmem_limit_bytes=48 << 20)


def dot(a, b, ca=1, cb=0):
    return lax.dot_general(a, b, (((ca,), (cb,)), ((), ())), preferred_element_type=F32)


def selections():
    pack = np.zeros((320, 384), np.float32)
    gather = np.zeros((4, 288, 72), np.float32)
    leave = np.zeros((192, 144), np.float32)
    place = np.zeros((4, 192, 36), np.float32)
    for q, (a0, b0) in enumerate(QUADS):
        for p in range(2):
            for a in range(3):
                for b in range(6):
                    row = (p * 3 + a) * 6 + b
                    slab = (((p + 1) % 2) * 6 + a0 + a) * 16 + b0 + b
                    token = (p * 6 + (3 - a0) + a) * 12 + (6 - b0) + b
                    for arr in range(2):
                        pack[q * 80 + arr * 36 + row, arr * 192 + slab] = 1
                        gather[q, arr * 144 + token, arr * 36 + row] = 1
                    leave[q * 48 + row, token] = 1
                    place[q, slab, row] = 1
    return [jnp.asarray(m, BF16) for m in (pack, gather, leave, place)]


def pack_kernel(tok, cot, sel, own, lon, lat, diag, slabs):
    slabs[...] = jnp.zeros_like(slabs)
    for k in range(12):
        slabs[k, 0:12, :] = tok[k // 6, k % 6]
        slabs[12 + k, 0:12, :] = cot[k // 6, k % 6]
    out = dot(sel[...], slabs[...].reshape(384, C)).astype(BF16)
    own[...] = out[0:72]
    lon[...] = out[80:152]
    lat[...] = out[160:232]
    diag[...] = out[240:312]


def unpack_kernel(own, lon, lat, diag, sel, out):
    total = dot(sel[0], own[...])
    for q, ref in enumerate((lon, lat, diag)):
        total = total + dot(sel[q + 1], ref[...])
    slabs = total.astype(BF16).reshape(12, 16, C)
    for k in range(12):
        out[k // 6, k % 6] = slabs[k, 0:12]


def bias_kernel(idx, table, col, row, bias, packed, flat):
    packed[0:T, :] = idx[:, 0:128]
    lane = lax.broadcasted_iota(jnp.int32, (24, 128), 1)
    tail = jnp.zeros((24, 128), jnp.int32)
    for c in range(6):
        part = jnp.concatenate(
            (idx[24 * c : 24 * c + 24, 128:T], jnp.zeros((24, 112), jnp.int32)), axis=1
        )
        part = pltpu.roll(part, 16 * c, 1) if c else part
        tail = jnp.where((lane >= 16 * c) & (lane < 16 * c + 16), part, tail)
    packed[T:PACK, :] = tail

    def block(i, carry):
        at = pl.ds(pl.multiple_of(i * 8, 8), 8)
        position = packed[at, :]
        low = position & 127
        high = position >> 7
        for h in range(HEADS):
            total = jnp.zeros((8, 128), F32)
            for k in range(BLKS):
                r = h * BLKS + k
                values = jnp.broadcast_to(table[r : r + 1, :], (8, 128))
                found = jnp.take_along_axis(values, low, axis=1, mode="promise_in_bounds")
                total = jnp.where(high == k, found, total)
            flat[h, at, :] = total
        return carry

    lax.fori_loop(0, PACK // 8, block, 0)
    same = col[...] == row[...]
    for h in range(HEADS):
        bias[h, :, 0:128] = jnp.where(same[:, 0:128], flat[h, 0:T, :], -1e9)
        tail = flat[h, T:PACK, :]
        for c in range(6):
            part = pltpu.roll(tail, 128 - 16 * c, 1) if c else tail
            at = slice(24 * c, 24 * c + 24)
            bias[h, at, 128:T] = jnp.where(same[at, 128:T], part[:, 0:16], -1e9)


def main_kernel(own, lon, lat, diag, sel, bias, wqkv, wproj, leave,
                ret_own, ret_lon, ret_lat, ret_diag, grads, ds_out, ds_tail):
    scale = HD ** (-0.5)
    both = dot(sel[0], own[...])
    for q, ref in enumerate((lon, lat, diag)):
        both = both + dot(sel[q + 1], ref[...])
    values = both[0:T]
    cot32 = both[T:]
    cot = cot32.astype(BF16)
    center = values - jnp.mean(values, axis=-1, keepdims=True)
    inv_std = lax.rsqrt(jnp.mean(center * center, axis=-1, keepdims=True) + 1e-05)
    normed = center * inv_std
    hidden = normed.astype(BF16)
    proj = dot(hidden, wqkv[...])
    query = proj[:, 0:C]
    query_t = query.T.astype(BF16)
    query = query.astype(BF16)
    key = proj[:, C : 2 * C].astype(BF16)
    value = proj[:, 2 * C :].astype(BF16)
    att = dot(cot, wproj[...], 1, 1)
    att_t = att.T.astype(BF16)
    att = att.astype(BF16)
    head = lax.broadcasted_iota(jnp.int32, (T, C), 1) // HD
    zero = jnp.zeros((T, C), BF16)
    attended = jnp.zeros((T, C), F32)
    grad_query = jnp.zeros((T, C), F32)
    key_t = []
    value_t = []
    lane = lax.broadcasted_iota(jnp.int32, (24, 128), 1)
    for h in range(HEADS):
        mine = head == h
        scores = dot(jnp.where(mine, query, zero), key, 1, 1) * scale + bias[h]
        exponent = jnp.exp(scores - jnp.max(scores, axis=-1, keepdims=True))
        prob = exponent * (1.0 / jnp.sum(exponent, axis=-1, keepdims=True))
        prob_half = prob.astype(BF16)
        attended = attended + dot(prob_half, jnp.where(mine, value, zero))
        grad_prob = dot(jnp.where(mine, att, zero), value, 1, 1)
        value_t.append(dot(att_t[HD * h : HD * h + HD], prob_half))
        ds = prob * (grad_prob - jnp.sum(grad_prob * prob, axis=-1, keepdims=True))
        ds_half = ds.astype(BF16)
        grad_query = grad_query + dot(ds_half, jnp.where(mine, key, zero))
        key_t.append(dot(query_t[HD * h : HD * h + HD], ds_half))
        ds_out[h, 0:T, :] = ds[:, 0:128]
        ds_tail[:, 0:16] = ds[:, 128:T]
        packed = jnp.zeros((24, 128), F32)
        for c in range(6):
            part = ds_tail[24 * c : 24 * c + 24, :]
            part = pltpu.roll(part, 16 * c, 1) if c else part
            packed = jnp.where((lane >= 16 * c) & (lane < 16 * c + 16), part, packed)
        ds_out[h, T:PACK, :] = packed
    grad_key = jnp.concatenate(key_t, axis=0).T
    grad_value = jnp.concatenate(value_t, axis=0).T
    grad_in = jnp.concatenate((grad_query * scale, grad_key * scale, grad_value), axis=1)
    grad_in = grad_in.astype(BF16)
    grad_qkv = dot(hidden, grad_in, 0, 0)
    grad_proj = dot(attended.astype(BF16), cot, 0, 0)
    grads[...] = jnp.concatenate((grad_qkv, grad_proj), axis=1).astype(BF16)
    grad_hidden = dot(grad_in, wqkv[...], 1, 1)
    grad_norm = inv_std * (
        grad_hidden
        - jnp.mean(grad_hidden, axis=-1, keepdims=True)
        - normed * jnp.mean(grad_hidden * normed, axis=-1, keepdims=True)
    )
    returned = (cot32 + grad_norm).astype(BF16)
    parts = dot(leave[...], returned).astype(BF16)
    ret_own[...] = parts[0:36]
    ret_lon[...] = parts[48:84]
    ret_lat[...] = parts[96:132]
    ret_diag[...] = parts[144:180]


def scatter_kernel(idx, ds, out, packed, total):
    packed[0:T, :] = idx[:, 0:128]
    lane = lax.broadcasted_iota(jnp.int32, (24, 128), 1)
    tail = jnp.zeros((24, 128), jnp.int32)
    for c in range(6):
        part = jnp.concatenate(
            (idx[24 * c : 24 * c + 24, 128:T], jnp.zeros((24, 112), jnp.int32)), axis=1
        )
        part = pltpu.roll(part, 16 * c, 1) if c else part
        tail = jnp.where((lane >= 16 * c) & (lane < 16 * c + 16), part, tail)
    packed[T:PACK, :] = tail
    total[...] = jnp.zeros_like(total)
    blocks = lax.broadcasted_iota(jnp.int32, (32, 128), 0)
    lows = lax.broadcasted_iota(jnp.int32, (128, 128), 0)

    def block(i, carry):
        at = pl.ds(pl.multiple_of(i * 8, 8), 8)
        position = packed[at, :]
        low = position & 127
        high = position >> 7
        left = []
        right = []
        for r in range(8):
            right.append(jnp.where(lows == low[r : r + 1], 1.0, 0.0).astype(BF16))
            mine = blocks == high[r : r + 1]
            parts = []
            for h in range(HEADS):
                row = ds[h, at, :][r : r + 1]
                parts.append(jnp.where(mine, row, 0.0).astype(BF16))
            left.append(jnp.concatenate(parts, axis=0))
        total[...] += dot(jnp.concatenate(left, axis=1), jnp.concatenate(right, axis=1), 1, 1)
        return carry

    lax.fori_loop(0, PACK // 8, block, 0)
    out[...] = total[...].astype(BF16)


def call(kernel, shapes, scratch, cost, *args):
    return pl.pallas_call(
        kernel,
        out_shape=[jax.ShapeDtypeStruct(s, d) for s, d in shapes],
        scratch_shapes=[pltpu.VMEM(s, d) for s, d in scratch],
        compiler_params=PARAMS,
        cost_estimate=pl.CostEstimate(flops=cost, bytes_accessed=1 << 20, transcendentals=0),
    )(*args)


def exchange(block, axes, groups=None):
    return lax.all_to_all(block, axes, 0, 0, axis_index_groups=groups, tiled=False)


def summed(parts):
    return jnp.sum(parts.astype(F32), axis=0)


def local(sizes, tokens, cotangent, region, pos_index, w_qkv, w_proj, bias_table):
    n_lon, n_lat, n_y = sizes
    n_z = n_lon // n_y
    pack, gather, leave, place = selections()
    axes = ("lon", "lat", "rep")

    def moved(block, d_lon, d_lat):
        route = []
        for i in range(n_lon):
            for j in range(n_lat):
                source = ((i + d_lon) % n_lon) * n_lat + (j + d_lat) % n_lat
                route.append((source, i * n_lat + j))
        return lax.ppermute(block, axes, route)

    strip = ((72, C), BF16)
    own, lon, lat, diag = call(
        pack_kernel, [strip] * 4, [((24, 16, C), BF16)], 10**8, tokens, cotangent, pack
    )
    lon, lat, diag = moved(lon, 1, 0), moved(lat, 0, 1), moved(diag, 1, 1)

    table = jnp.pad(bias_table.reshape(ROWS, HEADS).T, ((0, 0), (0, BLKS * 128 - ROWS)))
    table = table.reshape(HEADS * BLKS, 128)
    (bias,) = call(
        bias_kernel,
        [((HEADS, T, T), F32)],
        [((PACK, 128), jnp.int32), ((HEADS, PACK, 128), F32)],
        5 * 10**9,
        pos_index,
        table,
        region.reshape(T, 1),
        region.reshape(1, T),
    )
    back = ((36, C), BF16)
    ret_own, ret_lon, ret_lat, ret_diag, grads, ds = call(
        main_kernel,
        [back] * 4 + [((C, 4 * C), BF16), ((HEADS, PACK, 128), F32)],
        [((T, 128), F32)],
        10**10,
        own, lon, lat, diag, gather, bias, w_qkv, w_proj, leave,
    )
    ret_lon, ret_lat, ret_diag = (
        moved(ret_lon, -1, 0), moved(ret_lat, 0, -1), moved(ret_diag, -1, -1),
    )
    across = ("lat", "rep")
    chunk = exchange(grads.reshape(n_lat, C // n_lat, 4 * C), across)
    (scattered,) = call(
        scatter_kernel,
        [((192, 128), BF16)],
        [((PACK, 128), jnp.int32), ((192, 128), F32)],
        5 * 10**9,
        pos_index,
        ds,
    )
    (grad_tokens,) = call(
        unpack_kernel, [((2, 6, 12, C), BF16)], [], 10**8,
        ret_own, ret_lon, ret_lat, ret_diag, place,
    )
    chunk = summed(chunk).astype(BF16)
    rows = chunk.size // 128
    mixed = jnp.concatenate(
        (chunk.reshape(n_y, rows // n_y, 128), scattered.reshape(n_y, 192 // n_y, 128)), axis=1
    )
    rows_y = [[z * n_y + y for y in range(n_y)] for z in range(n_z)]
    rows_z = [[z * n_y + y for z in range(n_z)] for y in range(n_y)]
    mixed = summed(exchange(mixed, "lon", rows_y)).astype(BF16)
    mixed = jnp.broadcast_to(mixed, (n_z,) + mixed.shape)
    mixed = summed(exchange(mixed, "lon", rows_z)).astype(BF16)
    mixed = jnp.broadcast_to(mixed, (n_y,) + mixed.shape)
    mixed = exchange(mixed, "lon", rows_y)
    chunk = mixed[:, : rows // n_y].reshape(C // n_lat, 4 * C)
    scattered = mixed[:, rows // n_y :].reshape(HEADS, 32 * 128)
    grad_bias = scattered[:, :ROWS].astype(F32).T.reshape(ROWS, 1, HEADS)
    grads = exchange(jnp.broadcast_to(chunk, (n_lat,) + chunk.shape), across)
    grads = grads.reshape(C, 4 * C).astype(F32)
    return (grad_tokens, grads[:, : 3 * C], grads[:, 3 * C :], grad_bias)


def solution(mesh):
    n_lon = mesh.shape["lon"]
    n_lat = mesh.shape["lat"] * mesh.shape["rep"]
    n_y = 8 if n_lon % 8 == 0 else 2
    placed = (
        P(None, ("lat", "rep"), "lon", None),
        P(None, ("lat", "rep"), "lon", None),
        P(None, ("lat", "rep"), "lon"),
        P(),
        P(),
        P(),
        P(None, ("lat", "rep"), None),
    )
    return jax.shard_map(
        functools.partial(local, (n_lon, n_lat, n_y)),
        mesh=mesh,
        in_specs=placed,
        out_specs=(P(None, ("lat", "rep"), "lon", None), P(), P(), P(None, ("lat", "rep"), None)),
        check_vma=False,
    )
```

time: 947 us -> 114 us (0.12)
  waiting for transfers between devices: 707 us -> 9.5 us
  other arithmetic: 118 us -> 0.19 us
  local copies, waits for them, and re-layouts: 75.3 us -> 7.63 us
  starting transfers between devices: 26.2 us -> 54.7 us
  blocking collectives: 0 us -> 23.8 us
  Pallas kernels: 0 us -> 16.8 us
  between operations: 14.4 us -> 0.96 us
    psum x2 -> x0, waiting for transfers between devices: 700 us -> none  [the longest x1 481 us: local(): grad_qkv, grad_proj = lax.psum((grad_qkv, grad_proj), ('lon', 'lat', 'rep'))]
    scatter-add x1 -> x0, other arithmetic: 114 us -> none  [window_grads(): jax.ops.segment_sum(folded, pos_index.reshape(-1), num_segments=bias_tabl...]
    gather x1 -> x0, local copies, waits for them, and re-layouts: 38.7 us -> none  [window_grads(): table_rows = bias_table[pos_index].reshape(144, 144, lat_win, pl_win, heads)]
    all_to_all x0 -> x2, blocking collectives: none -> 23.8 us  [exchange(): lax.all_to_all(block, axes, 0, 0, axis_index_groups=groups, tiled=False)]
    reshape x2 -> x7, local copies, waits for them, and re-layouts: 22 us -> 1.08 us  [the longest x1 0.69 us: local(): grad_bias = scattered[:, :ROWS].astype(F32).T.reshape(ROWS, 1, HEADS)]
    pallas_call x0 -> x5, Pallas kernels: none -> 16.8 us  [call(): pl.pallas_call(kernel, out_shape=[jax.ShapeDtypeStruct(s, d) for s, d in...]
    all_to_all x0 -> x3, starting transfers between devices: none -> 15.8 us  [exchange(): lax.all_to_all(block, axes, 0, 0, axis_index_groups=groups, tiled=False)]
    ppermute x4 -> x6, starting transfers between devices: 26.1 us -> 38.9 us  [moved(): return lax.ppermute(block, axes, route)]
  transfers between devices with their start and end apart: 6 -> 9, of which waited for: 3 -> 3; matrix products, arithmetic and copies ran while one was open for 20% -> 1% of each run, Pallas kernels for 0% -> 10%
where the time goes in v1:
time: 114 us
  starting transfers between devices  54.7 us (48%)
  blocking collectives  23.8 us (21%)
  Pallas kernels  16.8 us (15%)
  waiting for transfers between devices  9.5 us (8%)
  local copies, waits for them, and re-layouts  7.63 us (7%)
    ppermute x6, starting transfers between devices, moved(): return lax.ppermute(block, axes, route)  38.9 us
    all_to_all x2, blocking collectives, exchange(): lax.all_to_all(block, axes, 0, 0, axis_index_groups=groups, tiled=False)  23.8 us
    pallas_call x5, Pallas kernels, call(): pl.pallas_call(kernel, out_shape=[jax.ShapeDtypeStruct(s, d) for s, d in...  16.8 us
    all_to_all x3, starting transfers between devices, exchange(): lax.all_to_all(block, axes, 0, 0, axis_index_groups=groups, tiled=False)  15.8 us
    all_to_all x3, waiting for transfers between devices, exchange(): lax.all_to_all(block, axes, 0, 0, axis_index_groups=groups, tiled=False)  6.92 us
    unnamed x23, local copies, waits for them, and re-layouts  3.5 us
    ppermute x6, waiting for transfers between devices, moved(): return lax.ppermute(block, axes, route)  2.58 us
  transfers between devices with their start and end apart: 9, of which 3 were waited for; matrix products, arithmetic and copies ran while one was open for 1% of the time, Pallas kernels for 10%

profile of v1, /device:TPU:1, one launch (start us, length us, event | category | flops | bytes accessed | tf_op | source)
XLA Modules:
  0.0 113.6 jit_solution(4483395730256910217)
XLA Ops:
  0.6 0.0 copy-start
  0.6 0.9 copy.26.tok
  1.6 0.9 copy.27.cot
  2.5 0.0 copy-done
  2.5 0.0 copy-start.8
  2.5 0.3 shard_map.138
  2.8 0.0 copy-start.7
  2.8 18.2 %collective-permute-start = (bf16[72,192]{1,0:T(8,128)(2,1)S(1)}, bf16[72,192]{1,0:T(8,128)(2,1)S(1)}, u32[]{:S(2)}, u32[]{:S(2)}) collective-permute-start(bf16[72,192]{1,0:T(8,128)(2,1)S(1)} %get-tuple-element.15), channel_id=1, source_target_pairs={{8,0},{9,1},{10,2},{11,3},{12,4},{13,5},{14,6},{15,7},{16,8},{17,9... | collective-permute-start | bytes 82952 | tf_op jit(solution)/shard_map/ppermute | solution.py:245
  21.0 4.0 %collective-permute-start.1 = (bf16[72,192]{1,0:T(8,128)(2,1)S(1)}, bf16[72,192]{1,0:T(8,128)(2,1)S(1)}, u32[]{:S(2)}, u32[]{:S(2)}) collective-permute-start(bf16[72,192]{1,0:T(8,128)(2,1)S(1)} %get-tuple-element.16), channel_id=1, source_target_pairs={{1,0},{2,1},{3,2},{4,3},{5,4},{6,5},{7,6},{0,7},{9,8},{10,9},{11,1... | collective-permute-start | bytes 82952 | tf_op jit(solution)/shard_map/ppermute | solution.py:245
  24.9 3.2 %collective-permute-start.2 = (bf16[72,192]{1,0:T(8,128)(2,1)S(1)}, bf16[72,192]{1,0:T(8,128)(2,1)S(1)}, u32[]{:S(2)}, u32[]{:S(2)}) collective-permute-start(bf16[72,192]{1,0:T(8,128)(2,1)S(1)} %get-tuple-element.17), channel_id=1, source_target_pairs={{9,0},{10,1},{11,2},{12,3},{13,4},{14,5},{15,6},{8,7},{17,8},{18,9... | collective-permute-start | bytes 82952 | tf_op jit(solution)/shard_map/ppermute | solution.py:245
  28.2 0.0 copy-done.8
  28.2 0.1 reshape.47.row
  28.3 0.1 reshape.59.col
  28.4 0.0 copy-done.7
  28.4 0.0 copy-start.3
  28.5 0.9 copy-done.3
  29.3 0.0 copy-start.2
  29.3 0.0 copy-start.4
  29.3 0.0 copy-start.5
  29.4 0.0 copy-start.6
  29.4 5.3 %shard_map.139.bias = f32[6,144,144]{2,1,0:T(8,128)S(1)} custom-call(s32[144,144]{1,0:T(8,128)S(1)} %copy-done.3, f32[156,128]{1,0:T(8,128)S(1)} %reshape.45.table, s32[144,1]{1,0:T(8,128)S(1)} %reshape.59.col, s32[1,144]{1,0:T(1,128)S(1)} %reshape.47.row), custom_call_target="tpu_custom_call" | custom-call | flops 5000000000 | bytes 1048576 | tf_op jit(solution)/shard_map/pallas_call | solution.py:216
  34.7 0.0 collective-permute-done.lon
  34.7 0.0 collective-permute-done.1.lat
  34.7 0.0 collective-permute-done.2.diag
  34.7 0.0 copy-done.2
  34.7 0.0 copy-done.4
  34.7 0.0 copy-done.5
  34.7 0.0 copy-done.6
  34.7 5.1 %shard_map.140 = (bf16[36,192]{1,0:T(8,128)(2,1)S(1)}, bf16[36,192]{1,0:T(8,128)(2,1)S(1)}, bf16[36,192]{1,0:T(8,128)(2,1)S(1)}, bf16[36,192]{1,0:T(8,128)(2,1)S...) custom-call(bf16[72,192]{1,0:T(8,128)(2,1)S(1)} %get-tuple-element.14.own, ...), custom_call_target="tpu_custom_call" | custom-call | flops 10000000000 | bytes 1048576 | tf_op jit(solution)/shard_map/pallas_call | solution.py:216
  39.9 4.4 %all-to-all-start = ((bf16[8,24,768]{2,1,0:T(8,128)(2,1)}), bf16[8,24,768]{2,1,0:T(8,128)(2,1)S(1)}, u32[]{:S(2)}, u32[]{:S(2)}) async-start(bf16[8,24,768]{2,1,0:T(8,128)(2,1)} %bitcast.1), calls=%async_computation | async-start | bytes 589824 | tf_op jit(solution)/shard_map/all_to_all | solution.py:226
  44.3 5.8 %shard_map.142 = bf16[192,128]{1,0:T(8,128)(2,1)S(1)} custom-call(s32[144,144]{1,0:T(8,128)S(1)} %copy-done.3, f32[6,168,128]{2,1,0:T(8,128)S(1)} %get-tuple-element.23.ds), custom_call_target="tpu_custom_call" | custom-call | flops 5000000000 | bytes 1048576 | tf_op jit(solution)/shard_map/pallas_call | solution.py:216
  50.1 0.9 all-to-all-done
  51.0 0.1 reshape.49
  51.1 10.1 %all_to_all.25 = bf16[8,42,128]{2,1,0:T(8,128)(2,1)S(1)} all-to-all(bf16[8,42,128]{2,1,0:T(8,128)(2,1)S(1)} %pad_maximum_fusion), channel_id=1, replica_groups={{0,8,16,24,32,40,48,56},{64,72,80,88,96,104,112,120},{128,136,144,152,1..., dimensions={0} | all-to-all | bytes 172032 | tf_op jit(solution)/shard_map/all_to_all | solution.py:226
  61.3 13.8 %all_to_all.26 = bf16[12,42,128]{2,1,0:T(8,128)(2,1)S(1)} all-to-all(bf16[12,42,128]{2,1,0:T(8,128)(2,1)S(1)} %broadcast_in_dim.9), channel_id=1, replica_groups={{0,64,128,192,256,320,384,448,512,576,640,704},{8,72,136,200,264,328,39..., dimensions={0} | all-to-all | bytes 258048 | tf_op jit(solution)/shard_map/all_to_all | solution.py:226
  75.0 0.0 copy-start.1
  75.1 0.7 broadcast_in_dim.10
  75.7 3.4 %all-to-all-start.3 = ((bf16[8,42,128]{2,1,0:T(8,128)(2,1)}), bf16[8,42,128]{2,1,0:T(8,128)(2,1)S(1)}, u32[]{:S(2)}, u32[]{:S(2)}) async-start(bf16[8,42,128]{2,1,0:T(8,128)(2,1)} %broadcast_in_dim.10), calls=%async_computation.3 | async-start | bytes 196608 | tf_op jit(solution)/shard_map/all_to_all | solution.py:226
  79.1 3.3 %collective-permute-start.3 = (bf16[36,192]{1,0:T(8,128)(2,1)S(1)}, bf16[36,192]{1,0:T(8,128)(2,1)S(1)}, u32[]{:S(2)}, u32[]{:S(2)}) collective-permute-start(bf16[36,192]{1,0:T(8,128)(2,1)S(1)} %get-tuple-element.19), channel_id=1, source_target_pairs={{760,0},{761,1},{762,2},{763,3},{764,4},{765,5},{766,6},{767,7},{0... | collective-permute-start | bytes 41480 | tf_op jit(solution)/shard_map/ppermute | solution.py:245
  82.3 2.5 %collective-permute-start.4 = (bf16[36,192]{1,0:T(8,128)(2,1)S(1)}, bf16[36,192]{1,0:T(8,128)(2,1)S(1)}, u32[]{:S(2)}, u32[]{:S(2)}) collective-permute-start(bf16[36,192]{1,0:T(8,128)(2,1)S(1)} %get-tuple-element.20), channel_id=1, source_target_pairs={{7,0},{0,1},{1,2},{2,3},{3,4},{4,5},{5,6},{6,7},{15,8},{8,9},{9,10... | collective-permute-start | bytes 41480 | tf_op jit(solution)/shard_map/ppermute | solution.py:245
  84.9 7.8 %collective-permute-start.5 = (bf16[36,192]{1,0:T(8,128)(2,1)S(1)}, bf16[36,192]{1,0:T(8,128)(2,1)S(1)}, u32[]{:S(2)}, u32[]{:S(2)}) collective-permute-start(bf16[36,192]{1,0:T(8,128)(2,1)S(1)} %get-tuple-element.21), channel_id=1, source_target_pairs={{767,0},{760,1},{761,2},{762,3},{763,4},{764,5},{765,6},{766,7},{7... | collective-permute-start | bytes 41480 | tf_op jit(solution)/shard_map/ppermute | solution.py:245
  92.7 0.0 collective-permute-done.3.lon
  92.7 0.0 collective-permute-done.4.lat
  92.7 2.6 %collective-permute-done.5.diag = bf16[36,192]{1,0:T(8,128)(2,1)S(1)} collective-permute-done((bf16[36,192]{1,0:T(8,128)(2,1)S(1)}, bf16[36,192]{1,0:T(8,128)(2,1)S(1)}, u32[]{:S(2)}, u32[]{:S(2)}) %collective-permute-start.5) | collective-permute-done | bytes 13856 | tf_op jit(solution)/shard_map/ppermute | solution.py:245
  95.3 0.0 copy-done.1
  95.3 0.2 shard_map.141
  95.5 0.7 copy.31
  96.2 0.0 all-to-all-done.3
  96.2 0.1 reshape.51
  96.3 0.1 reshape.52
  96.4 0.7 broadcast_in_dim.11
  97.2 8.0 %all-to-all-start.4 = ((bf16[8,24,768]{2,1,0:T(8,128)(2,1)}), bf16[8,24,768]{2,1,0:T(8,128)(2,1)S(1)}, u32[]{:S(2)}, u32[]{:S(2)}) async-start(bf16[8,24,768]{2,1,0:T(8,128)(2,1)} %broadcast_in_dim.11), calls=%async_computation.4 | async-start | bytes 589824 | tf_op jit(solution)/shard_map/all_to_all | solution.py:226
  105.2 0.7 reshape.57
  105.9 6.0 %all-to-all-done.4 = bf16[8,24,768]{2,1,0:T(8,128)(2,1)S(1)} async-done(((bf16[8,24,768]{2,1,0:T(8,128)(2,1)}), bf16[8,24,768]{2,1,0:T(8,128)(2,1)S(1)}, u32[]{:S(2)}, u32[]{:S(2)}) %all-to-all-start.4) | async-done | bytes 294944 | tf_op jit(solution)/shard_map/all_to_all | solution.py:226
  111.9 0.1 bitcast_convert_fusion
  112.0 0.8 slice.22
  112.8 0.8 slice.21
  (12 shorter events, 0.2 us)
Async XLA Ops:
  0.6 1.9 %copy-start = (bf16[320,384]{1,0:T(8,128)(2,1)S(1)}, bf16[320,384]{1,0:T(8,128)(2,1)}, u32[]{:S(2)}) copy-start(bf16[320,384]{1,0:T(8,128)(2,1)} %constant.16.clone.sel) | copy-start | bytes 737284
  2.5 25.7 %copy-start.8 = (s32[2,6,12]{2,0,1:T(2,128)S(1)}, s32[2,6,12]{2,0,1:T(2,128)}, u32[]{:S(2)}) copy-start(s32[2,6,12]{2,0,1:T(2,128)} %param.13) | copy-start | bytes 1732
  2.8 25.6 %copy-start.7 = (f32[3312,1,6]{0,1,2:T(1,128)S(1)}, f32[3312,1,6]{0,1,2:T(1,128)}, u32[]{:S(2)}) copy-start(f32[3312,1,6]{0,1,2:T(1,128)} %param.17) | copy-start | bytes 238468
  2.8 31.9 %collective-permute-start = (bf16[72,192]{1,0:T(8,128)(2,1)S(1)}, bf16[72,192]{1,0:T(8,128)(2,1)S(1)}, u32[]{:S(2)}, u32[]{:S(2)}) collective-permute-start(bf16[72,192]{1,0:T(8,128)(2,1)S(1)} %get-tuple-element.15), channel_id=1, source_target_pairs={{8,0},{9,1},{10,2},{11,3},{12,4},{13,5},{14,6},{15,7},{16,8},{17,9... | collective-permute-start | bytes 82952 | tf_op jit(solution)/shard_map/ppermute | solution.py:245
  21.0 13.7 %collective-permute-start.1 = (bf16[72,192]{1,0:T(8,128)(2,1)S(1)}, bf16[72,192]{1,0:T(8,128)(2,1)S(1)}, u32[]{:S(2)}, u32[]{:S(2)}) collective-permute-start(bf16[72,192]{1,0:T(8,128)(2,1)S(1)} %get-tuple-element.16), channel_id=1, source_target_pairs={{1,0},{2,1},{3,2},{4,3},{5,4},{6,5},{7,6},{0,7},{9,8},{10,9},{11,1... | collective-permute-start | bytes 82952 | tf_op jit(solution)/shard_map/ppermute | solution.py:245
  24.9 9.7 %collective-permute-start.2 = (bf16[72,192]{1,0:T(8,128)(2,1)S(1)}, bf16[72,192]{1,0:T(8,128)(2,1)S(1)}, u32[]{:S(2)}, u32[]{:S(2)}) collective-permute-start(bf16[72,192]{1,0:T(8,128)(2,1)S(1)} %get-tuple-element.17), channel_id=1, source_target_pairs={{9,0},{10,1},{11,2},{12,3},{13,4},{14,5},{15,6},{8,7},{17,8},{18,9... | collective-permute-start | bytes 82952 | tf_op jit(solution)/shard_map/ppermute | solution.py:245
  28.4 0.9 copy-start.3
  29.3 5.3 %copy-start.2 = (bf16[192,576]{1,0:T(8,128)(2,1)S(1)}, bf16[192,576]{1,0:T(8,128)(2,1)}, u32[]{:S(2)}) copy-start(bf16[192,576]{1,0:T(8,128)(2,1)} %wqkv.1) | copy-start | bytes 663556
  29.3 5.4 %copy-start.4 = (bf16[192,192]{1,0:T(8,128)(2,1)S(1)}, bf16[192,192]{1,0:T(8,128)(2,1)}, u32[]{:S(2)}) copy-start(bf16[192,192]{1,0:T(8,128)(2,1)} %wproj.1) | copy-start | bytes 221188
  29.3 5.4 %copy-start.5 = (bf16[4,288,72]{2,1,0:T(8,128)(2,1)S(1)}, bf16[4,288,72]{2,1,0:T(8,128)(2,1)}, u32[]{:S(2)}) copy-start(bf16[4,288,72]{2,1,0:T(8,128)(2,1)} %constant.17.clone.sel) | copy-start | bytes 497668
  29.4 5.4 %copy-start.6 = (bf16[192,144]{1,0:T(8,128)(2,1)S(1)}, bf16[192,144]{1,0:T(8,128)(2,1)}, u32[]{:S(2)}) copy-start(bf16[192,144]{1,0:T(8,128)(2,1)} %constant.18.clone.leave) | copy-start | bytes 165892
  39.9 11.1 %all-to-all-start = ((bf16[8,24,768]{2,1,0:T(8,128)(2,1)}), bf16[8,24,768]{2,1,0:T(8,128)(2,1)S(1)}, u32[]{:S(2)}, u32[]{:S(2)}) async-start(bf16[8,24,768]{2,1,0:T(8,128)(2,1)} %bitcast.1), calls=%async_computation | async-start | bytes 589824 | tf_op jit(solution)/shard_map/all_to_all | solution.py:226
  75.0 20.2 %copy-start.1 = (bf16[4,192,36]{2,1,0:T(8,128)(2,1)S(1)}, bf16[4,192,36]{2,1,0:T(8,128)(2,1)}, u32[]{:S(2)}) copy-start(bf16[4,192,36]{2,1,0:T(8,128)(2,1)} %constant.19.clone.sel) | copy-start | bytes 165892
  75.7 20.5 %all-to-all-start.3 = ((bf16[8,42,128]{2,1,0:T(8,128)(2,1)}), bf16[8,42,128]{2,1,0:T(8,128)(2,1)S(1)}, u32[]{:S(2)}, u32[]{:S(2)}) async-start(bf16[8,42,128]{2,1,0:T(8,128)(2,1)} %broadcast_in_dim.10), calls=%async_computation.3 | async-start | bytes 196608 | tf_op jit(solution)/shard_map/all_to_all | solution.py:226
  79.1 13.6 %collective-permute-start.3 = (bf16[36,192]{1,0:T(8,128)(2,1)S(1)}, bf16[36,192]{1,0:T(8,128)(2,1)S(1)}, u32[]{:S(2)}, u32[]{:S(2)}) collective-permute-start(bf16[36,192]{1,0:T(8,128)(2,1)S(1)} %get-tuple-element.19), channel_id=1, source_target_pairs={{760,0},{761,1},{762,2},{763,3},{764,4},{765,5},{766,6},{767,7},{0... | collective-permute-start | bytes 41480 | tf_op jit(solution)/shard_map/ppermute | solution.py:245
  82.3 10.4 %collective-permute-start.4 = (bf16[36,192]{1,0:T(8,128)(2,1)S(1)}, bf16[36,192]{1,0:T(8,128)(2,1)S(1)}, u32[]{:S(2)}, u32[]{:S(2)}) collective-permute-start(bf16[36,192]{1,0:T(8,128)(2,1)S(1)} %get-tuple-element.20), channel_id=1, source_target_pairs={{7,0},{0,1},{1,2},{2,3},{3,4},{4,5},{5,6},{6,7},{15,8},{8,9},{9,10... | collective-permute-start | bytes 41480 | tf_op jit(solution)/shard_map/ppermute | solution.py:245
  84.9 10.4 %collective-permute-start.5 = (bf16[36,192]{1,0:T(8,128)(2,1)S(1)}, bf16[36,192]{1,0:T(8,128)(2,1)S(1)}, u32[]{:S(2)}, u32[]{:S(2)}) collective-permute-start(bf16[36,192]{1,0:T(8,128)(2,1)S(1)} %get-tuple-element.21), channel_id=1, source_target_pairs={{767,0},{760,1},{761,2},{762,3},{763,4},{764,5},{765,6},{766,7},{7... | collective-permute-start | bytes 41480 | tf_op jit(solution)/shard_map/ppermute | solution.py:245
  97.2 14.7 %all-to-all-start.4 = ((bf16[8,24,768]{2,1,0:T(8,128)(2,1)}), bf16[8,24,768]{2,1,0:T(8,128)(2,1)S(1)}, u32[]{:S(2)}, u32[]{:S(2)}) async-start(bf16[8,24,768]{2,1,0:T(8,128)(2,1)} %broadcast_in_dim.11), calls=%async_computation.4 | async-start | bytes 589824 | tf_op jit(solution)/shard_map/all_to_all | solution.py:226

commit v2 on v1

--- a/solution.py
+++ b/solution.py
@@ -17,7 +17,7 @@
 ROWS = 3312
 BLKS = 26
 PACK = 168
-QUADS = ((3, 6), (3, 0), (0, 6), (0, 0))
+HALF = HEADS // 2
 PARAMS = pltpu.CompilerParams(vmem_limit_bytes=48 << 20)
 
 
@@ -26,47 +26,68 @@
 
 
 def selections():
-    pack = np.zeros((320, 384), np.float32)
-    gather = np.zeros((4, 288, 72), np.float32)
-    leave = np.zeros((192, 144), np.float32)
-    place = np.zeros((4, 192, 36), np.float32)
-    for q, (a0, b0) in enumerate(QUADS):
-        for p in range(2):
-            for a in range(3):
-                for b in range(6):
-                    row = (p * 3 + a) * 6 + b
-                    slab = (((p + 1) % 2) * 6 + a0 + a) * 16 + b0 + b
-                    token = (p * 6 + (3 - a0) + a) * 12 + (6 - b0) + b
+    first = np.zeros((288, 384), np.float32)
+    second = np.zeros((2, 144, 144), np.float32)
+    gather = np.zeros((3, 288, 144), np.float32)
+    leave = np.zeros((160, 144), np.float32)
+    place = np.zeros((4, 192, 40), np.float32)
+    for p in range(2):
+        for a in range(6):
+            for b in range(12):
+                slab = (((p + 1) % 2) * 6 + a) * 16 + b
+                half = (p * 6 + a) * 6 + b % 6
+                wide = (p * 3 + a % 3) * 12 + (b + 6) % 12
+                for arr in range(2):
+                    first[(0 if b < 6 else 144) + arr * 72 + half, arr * 192 + slab] = 1
+                    source = 1 if b < 6 else 0
+                    if a < 3:
+                        second[source, arr * 72 + wide, arr * 72 + half] = 1
+                    else:
+                        token = (p * 6 + a - 3) * 12 + (b + 6) % 12
+                        gather[source, arr * 144 + token, arr * 72 + half] = 1
+                token = (p * 6 + a) * 12 + b
+                if a >= 3:
                     for arr in range(2):
-                        pack[q * 80 + arr * 36 + row, arr * 192 + slab] = 1
-                        gather[q, arr * 144 + token, arr * 36 + row] = 1
-                    leave[q * 48 + row, token] = 1
-                    place[q, slab, row] = 1
-    return [jnp.asarray(m, BF16) for m in (pack, gather, leave, place)]
-
-
-def pack_kernel(tok, cot, sel, own, lon, lat, diag, slabs):
+                        row = (p * 3 + a - 3) * 12 + b
+                        gather[2, arr * 144 + token, arr * 72 + row] = 1
+                row = (p * 3 + a % 3) * 6 + b % 6
+                leave[(80 if a >= 3 else 0) + (40 if b >= 6 else 0) + row, token] = 1
+                home = (((p + 1) % 2) * 6 + (a + 3) % 6) * 16 + (b + 6) % 12
+                place[(2 if b >= 6 else 0) + (1 if a >= 3 else 0), home, row] = 1
+    return [jnp.asarray(m, BF16) for m in (first, second, gather, leave, place)]
+
+
+def pack_kernel(tok, cot, sel, strip, kept, slabs):
     slabs[...] = jnp.zeros_like(slabs)
     for k in range(12):
         slabs[k, 0:12, :] = tok[k // 6, k % 6]
         slabs[12 + k, 0:12, :] = cot[k // 6, k % 6]
     out = dot(sel[...], slabs[...].reshape(384, C)).astype(BF16)
-    own[...] = out[0:72]
-    lon[...] = out[80:152]
-    lat[...] = out[160:232]
-    diag[...] = out[240:312]
-
-
-def unpack_kernel(own, lon, lat, diag, sel, out):
-    total = dot(sel[0], own[...])
-    for q, ref in enumerate((lon, lat, diag)):
-        total = total + dot(sel[q + 1], ref[...])
+    strip[...] = out[0:T]
+    kept[...] = out[T:]
+
+
+def repack_kernel(kept, arrived, sel, strip):
+    strip[...] = (dot(sel[0], kept[...]) + dot(sel[1], arrived[...])).astype(BF16)
+
+
+def unpack_kernel(kept, first, second, sel, out):
+    total = dot(sel[0], kept[0]) + dot(sel[1], first[0])
+    total = total + dot(sel[2], second[0]) + dot(sel[3], second[1])
     slabs = total.astype(BF16).reshape(12, 16, C)
     for k in range(12):
         out[k // 6, k % 6] = slabs[k, 0:12]
 
 
-def bias_kernel(idx, table, col, row, bias, packed, flat):
+def finish_kernel(parts, qkv, proj):
+    n, rows, _ = parts.shape
+    for k in range(n):
+        part = parts[k].astype(F32)
+        qkv[rows * k : rows * k + rows, :] = part[:, : 3 * C]
+        proj[rows * k : rows * k + rows, :] = part[:, 3 * C :]
+
+
+def bias_kernel(first, idx, table, col, row, bias, packed, flat):
     packed[0:T, :] = idx[:, 0:128]
     lane = lax.broadcasted_iota(jnp.int32, (24, 128), 1)
     tail = jnp.zeros((24, 128), jnp.int32)
@@ -83,10 +104,10 @@
         position = packed[at, :]
         low = position & 127
         high = position >> 7
-        for h in range(HEADS):
+        for h in range(HALF):
             total = jnp.zeros((8, 128), F32)
             for k in range(BLKS):
-                r = h * BLKS + k
+                r = (first + h) * BLKS + k
                 values = jnp.broadcast_to(table[r : r + 1, :], (8, 128))
                 found = jnp.take_along_axis(values, low, axis=1, mode="promise_in_bounds")
                 total = jnp.where(high == k, found, total)
@@ -95,7 +116,7 @@
 
     lax.fori_loop(0, PACK // 8, block, 0)
     same = col[...] == row[...]
-    for h in range(HEADS):
+    for h in range(HALF):
         bias[h, :, 0:128] = jnp.where(same[:, 0:128], flat[h, 0:T, :], -1e9)
         tail = flat[h, T:PACK, :]
         for c in range(6):
@@ -104,12 +125,10 @@
             bias[h, at, 128:T] = jnp.where(same[at, 128:T], part[:, 0:16], -1e9)
 
 
-def main_kernel(own, lon, lat, diag, sel, bias, wqkv, wproj, leave,
-                ret_own, ret_lon, ret_lat, ret_diag, grads, ds_out, ds_tail):
+def main_kernel(kept, lon, lat, sel, bias_a, bias_b, wqkv, wproj, leave,
+                ret_kept, ret_strip, grads, ds_out, ds_tail):
     scale = HD ** (-0.5)
-    both = dot(sel[0], own[...])
-    for q, ref in enumerate((lon, lat, diag)):
-        both = both + dot(sel[q + 1], ref[...])
+    both = dot(sel[0], kept[...]) + dot(sel[1], lon[...]) + dot(sel[2], lat[...])
     values = both[0:T]
     cot32 = both[T:]
     cot = cot32.astype(BF16)
@@ -135,7 +154,8 @@
     lane = lax.broadcasted_iota(jnp.int32, (24, 128), 1)
     for h in range(HEADS):
         mine = head == h
-        scores = dot(jnp.where(mine, query, zero), key, 1, 1) * scale + bias[h]
+        scores = dot(jnp.where(mine, query, zero), key, 1, 1) * scale
+        scores = scores + (bias_a[h] if h < HALF else bias_b[h - HALF])
         exponent = jnp.exp(scores - jnp.max(scores, axis=-1, keepdims=True))
         prob = exponent * (1.0 / jnp.sum(exponent, axis=-1, keepdims=True))
         prob_half = prob.astype(BF16)
@@ -169,10 +189,9 @@
     )
     returned = (cot32 + grad_norm).astype(BF16)
     parts = dot(leave[...], returned).astype(BF16)
-    ret_own[...] = parts[0:36]
-    ret_lon[...] = parts[48:84]
-    ret_lat[...] = parts[96:132]
-    ret_diag[...] = parts[144:180]
+    for k in range(2):
+        ret_kept[k] = parts[40 * k : 40 * k + 40]
+        ret_strip[k] = parts[80 + 40 * k : 120 + 40 * k]
 
 
 def scatter_kernel(idx, ds, out, packed, total):
@@ -233,47 +252,46 @@
 def local(sizes, tokens, cotangent, region, pos_index, w_qkv, w_proj, bias_table):
     n_lon, n_lat, n_y = sizes
     n_z = n_lon // n_y
-    pack, gather, leave, place = selections()
-    axes = ("lon", "lat", "rep")
-
-    def moved(block, d_lon, d_lat):
-        route = []
-        for i in range(n_lon):
-            for j in range(n_lat):
-                source = ((i + d_lon) % n_lon) * n_lat + (j + d_lat) % n_lat
-                route.append((source, i * n_lat + j))
-        return lax.ppermute(block, axes, route)
-
-    strip = ((72, C), BF16)
-    own, lon, lat, diag = call(
-        pack_kernel, [strip] * 4, [((24, 16, C), BF16)], 10**8, tokens, cotangent, pack
-    )
-    lon, lat, diag = moved(lon, 1, 0), moved(lat, 0, 1), moved(diag, 1, 1)
+    first, second, gather, leave, place = selections()
+    across = ("lat", "rep")
+
+    def moved(block, axes, n, distance):
+        return lax.ppermute(block, axes, [((i + distance) % n, i) for i in range(n)])
 
     table = jnp.pad(bias_table.reshape(ROWS, HEADS).T, ((0, 0), (0, BLKS * 128 - ROWS)))
     table = table.reshape(HEADS * BLKS, 128)
-    (bias,) = call(
-        bias_kernel,
-        [((HEADS, T, T), F32)],
-        [((PACK, 128), jnp.int32), ((HEADS, PACK, 128), F32)],
-        5 * 10**9,
-        pos_index,
-        table,
-        region.reshape(T, 1),
-        region.reshape(1, T),
-    )
-    back = ((36, C), BF16)
-    ret_own, ret_lon, ret_lat, ret_diag, grads, ds = call(
+
+    def bias_of(head, index):
+        (bias,) = call(
+            functools.partial(bias_kernel, head),
+            [((HALF, T, T), F32)],
+            [((PACK, 128), jnp.int32), ((HALF, PACK, 128), F32)],
+            3 * 10**9,
+            index,
+            table,
+            region.reshape(T, 1),
+            region.reshape(1, T),
+        )
+        return bias
+
+    block = ((T, C), BF16)
+    strip, kept = call(
+        pack_kernel, [block] * 2, [((24, 16, C), BF16)], 10**8, tokens, cotangent, first
+    )
+    lon = moved(strip, "lon", n_lon, 1)
+    bias_a = bias_of(0, pos_index)
+    (strip,) = call(repack_kernel, [block], [], 10**8, kept, lon, second)
+    strip, late_index = lax.optimization_barrier((strip, pos_index))
+    lat = moved(strip, across, n_lat, 1)
+    bias_b = bias_of(HALF, late_index)
+    quarter = ((2, 40, C), BF16)
+    ret_kept, ret_strip, grads, ds = call(
         main_kernel,
-        [back] * 4 + [((C, 4 * C), BF16), ((HEADS, PACK, 128), F32)],
+        [quarter] * 2 + [((C, 4 * C), BF16), ((HEADS, PACK, 128), F32)],
         [((T, 128), F32)],
         10**10,
-        own, lon, lat, diag, gather, bias, w_qkv, w_proj, leave,
-    )
-    ret_lon, ret_lat, ret_diag = (
-        moved(ret_lon, -1, 0), moved(ret_lat, 0, -1), moved(ret_diag, -1, -1),
-    )
-    across = ("lat", "rep")
+        kept, lon, lat, gather, bias_a, bias_b, w_qkv, w_proj, leave,
+    )
     chunk = exchange(grads.reshape(n_lat, C // n_lat, 4 * C), across)
     (scattered,) = call(
         scatter_kernel,
@@ -283,10 +301,6 @@
         pos_index,
         ds,
     )
-    (grad_tokens,) = call(
-        unpack_kernel, [((2, 6, 12, C), BF16)], [], 10**8,
-        ret_own, ret_lon, ret_lat, ret_diag, place,
-    )
     chunk = summed(chunk).astype(BF16)
     rows = chunk.size // 128
     mixed = jnp.concatenate(
@@ -294,17 +308,27 @@
     )
     rows_y = [[z * n_y + y for y in range(n_y)] for z in range(n_z)]
     rows_z = [[z * n_y + y for z in range(n_z)] for y in range(n_y)]
+    mixed, ret_strip = lax.optimization_barrier((mixed, ret_strip))
+    ret_first = moved(ret_strip, across, n_lat, -1)
     mixed = summed(exchange(mixed, "lon", rows_y)).astype(BF16)
     mixed = jnp.broadcast_to(mixed, (n_z,) + mixed.shape)
+    mixed, ret_first = lax.optimization_barrier((mixed, ret_first))
+    ret_second = moved(jnp.stack((ret_kept[1], ret_first[1])), "lon", n_lon, -1)
     mixed = summed(exchange(mixed, "lon", rows_z)).astype(BF16)
     mixed = jnp.broadcast_to(mixed, (n_y,) + mixed.shape)
+    mixed, ret_second = lax.optimization_barrier((mixed, ret_second))
+    (grad_tokens,) = call(
+        unpack_kernel, [((2, 6, 12, C), BF16)], [], 10**8, ret_kept, ret_first, ret_second, place,
+    )
     mixed = exchange(mixed, "lon", rows_y)
     chunk = mixed[:, : rows // n_y].reshape(C // n_lat, 4 * C)
     scattered = mixed[:, rows // n_y :].reshape(HEADS, 32 * 128)
+    grads = exchange(jnp.broadcast_to(chunk, (n_lat,) + chunk.shape), across)
+    grad_qkv, grad_proj = call(
+        finish_kernel, [((C, 3 * C), F32), ((C, C), F32)], [], 10**7, grads
+    )
     grad_bias = scattered[:, :ROWS].astype(F32).T.reshape(ROWS, 1, HEADS)
-    grads = exchange(jnp.broadcast_to(chunk, (n_lat,) + chunk.shape), across)
-    grads = grads.reshape(C, 4 * C).astype(F32)
-    return (grad_tokens, grads[:, : 3 * C], grads[:, 3 * C :], grad_bias)
+    return (grad_tokens, grad_qkv, grad_proj, grad_bias)
 
 
 def solution(mesh):

time: 114 us -> 107 us (0.939)
  blocking collectives: 23.8 us -> 0 us
  waiting for transfers between devices: 9.5 us -> 27.5 us
  starting transfers between devices: 54.7 us -> 50.7 us
  Pallas kernels: 16.8 us -> 19.1 us
    all_to_all x2 -> x0, blocking collectives: 23.8 us -> none  [exchange(): lax.all_to_all(block, axes, 0, 0, axis_index_groups=groups, tiled=False)]
    all_to_all x3 -> x5, waiting for transfers between devices: 6.92 us -> 27.5 us  [exchange(): lax.all_to_all(block, axes, 0, 0, axis_index_groups=groups, tiled=False)]
    ppermute x6 -> x4, starting transfers between devices: 38.9 us -> 27 us  [moved(): lax.ppermute(block, axes, [((i + distance) % n, i) for i in range(n)])]
    all_to_all x3 -> x5, starting transfers between devices: 15.8 us -> 23.7 us  [exchange(): lax.all_to_all(block, axes, 0, 0, axis_index_groups=groups, tiled=False)]
    ppermute x6 -> x4, waiting for transfers between devices: 2.58 us -> 0.01 us  [moved(): lax.ppermute(block, axes, [((i + distance) % n, i) for i in range(n)])]
    pallas_call x5 -> x8, Pallas kernels: 16.8 us -> 19.1 us  [call(): pl.pallas_call(kernel, out_shape=[jax.ShapeDtypeStruct(s, d) for s, d in...]
    slice x2, local copies, waits for them, and re-layouts: 1.61 us -> 0.01 us  [local(): ret_second = moved(jnp.stack((ret_kept[1], ret_first[1])), 'lon', n_lon, -1)]
    unnamed x23 -> x25, local copies, waits for them, and re-layouts: 3.5 us -> 3.51 us
  transfers between devices with their start and end apart: 9 -> 9, of which waited for: 3 -> 5; matrix products, arithmetic and copies ran while one was open for 1% -> 2% of each run, Pallas kernels for 10% -> 12%
where the time goes in v2:
time: 107 us; the launch traced here: 106 us
  starting transfers between devices  50.7 us (47%)
  waiting for transfers between devices  27.5 us (26%)
  Pallas kernels  19.1 us (18%)
  local copies, waits for them, and re-layouts  6.7 us (6%)
    all_to_all x5, waiting for transfers between devices, exchange(): lax.all_to_all(block, axes, 0, 0, axis_index_groups=groups, tiled=False)  27.5 us
    ppermute x4, starting transfers between devices, moved(): lax.ppermute(block, axes, [((i + distance) % n, i) for i in range(n)])  27 us
    all_to_all x5, starting transfers between devices, exchange(): lax.all_to_all(block, axes, 0, 0, axis_index_groups=groups, tiled=False)  23.7 us
    pallas_call x8, Pallas kernels, call(): pl.pallas_call(kernel, out_shape=[jax.ShapeDtypeStruct(s, d) for s, d in...  19.1 us
    unnamed x25, local copies, waits for them, and re-layouts  3.51 us
  transfers between devices with their start and end apart: 9, of which 5 were waited for; matrix products, arithmetic and copies ran while one was open for 2% of the time, Pallas kernels for 12%

profile of v2, /device:TPU:1, one launch (start us, length us, event | category | flops | bytes accessed | tf_op | source)
XLA Modules:
  0.0 105.7 jit_solution(13797040124376180226)
XLA Ops:
  0.6 0.0 copy-start
  0.6 0.9 copy.28.tok
  1.6 0.9 copy.29.cot
  2.5 0.0 copy-done
  2.5 0.0 copy-start.9
  2.5 0.3 shard_map.147
  2.8 0.0 copy-start.8
  2.8 18.2 %collective-permute-start = (bf16[144,192]{1,0:T(8,128)(2,1)S(1)}, bf16[144,192]{1,0:T(8,128)(2,1)S(1)}, u32[]{:S(2)}, u32[]{:S(2)}) collective-permute-start(bf16[144,192]{1,0:T(8,128)(2,1)S(1)} %get-tuple-element.21), channel_id=1, source_target_pairs={{8,0},{16,8},{24,16},{32,24},{40,32},{48,40},{56,48},{64,56},{72,6... | collective-permute-start | bytes 165896 | tf_op jit(solution)/shard_map/ppermute | solution.py:259
  21.0 0.0 copy-done.9
  21.0 0.1 reshape.46.row
  21.1 0.1 reshape.57.col
  21.2 0.0 copy-done.8
  21.2 0.0 copy-start.3
  21.3 0.9 copy-done.3
  22.1 0.0 copy-start.6
  22.1 3.5 %shard_map.149.bias_a = f32[3,144,144]{2,1,0:T(8,128)S(1)} custom-call(s32[144,144]{1,0:T(8,128)S(1)} %copy-done.3, f32[156,128]{1,0:T(8,128)S(1)} %reshape.44.table, s32[144,1]{1,0:T(8,128)S(1)} %reshape.57.col, s32[1,144]{1,0:T(1,128)S(1)} %reshape.46.row), custom_call_target="tpu_custom_call" | custom-call | flops 3000000000 | bytes 1048576 | tf_op jit(solution)/shard_map/pallas_call | solution.py:235
  25.7 0.0 collective-permute-done.arrived.lon
  25.7 0.0 copy-done.6
  25.7 0.2 shard_map.148
  25.9 0.0 copy-start.2
  25.9 0.0 copy-start.4
  25.9 0.0 copy-start.5
  25.9 0.0 copy-start.7
  25.9 4.1 %collective-permute-start.1 = (bf16[144,192]{1,0:T(8,128)(2,1)S(1)}, bf16[144,192]{1,0:T(8,128)(2,1)S(1)}, u32[]{:S(2)}, u32[]{:S(2)}) collective-permute-start(bf16[144,192]{1,0:T(8,128)(2,1)S(1)} %shard_map.148), channel_id=1, source_target_pairs={{1,0},{2,1},{3,2},{4,3},{5,4},{6,5},{7,6},{0,7},{9,8},{10,9},{11,1... | collective-permute-start | bytes 165896 | tf_op jit(solution)/shard_map/ppermute | solution.py:259
  30.0 3.5 %shard_map.150.bias_b = f32[3,144,144]{2,1,0:T(8,128)S(1)} custom-call(s32[144,144]{1,0:T(8,128)S(1)} %copy-done.3, f32[156,128]{1,0:T(8,128)S(1)} %reshape.44.table, s32[144,1]{1,0:T(8,128)S(1)} %reshape.57.col, s32[1,144]{1,0:T(1,128)S(1)} %reshape.46.row), custom_call_target="tpu_custom_call" | custom-call | flops 3000000000 | bytes 1048576 | tf_op jit(solution)/shard_map/pallas_call | solution.py:235
  33.5 0.0 collective-permute-done.1.lat
  33.5 0.0 copy-done.2
  33.6 0.0 copy-done.4
  33.6 0.0 copy-done.5
  33.6 0.0 copy-done.7
  33.6 4.6 %shard_map.151 = (bf16[2,40,192]{2,1,0:T(8,128)(2,1)S(1)}, bf16[2,40,192]{2,1,0:T(8,128)(2,1)S(1)}, bf16[192,768]{1,0:T(8,128)(2,1)}, f32[6,168,128]{2,1,0:T(8,128)S(1)}) custom-call(bf16[144,192]{1,0:T(8,128)(2,1)S(1)} %get-tuple-element.20.kept, bf16[144,192]{1,0:T(8,128)(2,1)S(1)} %collective-permute-done.arrived.lon, ...), custom_call_target="tpu_custom_call" | custom-call | flops 10000000000 | bytes 1048576 | tf_op jit(solution)/shard_map/pallas_call | solution.py:235
  38.2 4.1 %all-to-all-start = ((bf16[8,24,768]{2,1,0:T(8,128)(2,1)}), bf16[8,24,768]{2,1,0:T(8,128)(2,1)S(1)}, u32[]{:S(2)}, u32[]{:S(2)}) async-start(bf16[8,24,768]{2,1,0:T(8,128)(2,1)} %bitcast.1), calls=%async_computation | async-start | bytes 589824 | tf_op jit(solution)/shard_map/all_to_all | solution.py:245
  42.4 5.8 %shard_map.152 = bf16[192,128]{1,0:T(8,128)(2,1)S(1)} custom-call(s32[144,144]{1,0:T(8,128)S(1)} %copy-done.3, f32[6,168,128]{2,1,0:T(8,128)S(1)} %get-tuple-element.26.ds), custom_call_target="tpu_custom_call" | custom-call | flops 5000000000 | bytes 1048576 | tf_op jit(solution)/shard_map/pallas_call | solution.py:235
  48.2 0.9 all-to-all-done
  49.1 0.1 reshape.48
  49.2 0.7 pad_maximum_fusion
  49.9 3.4 %all-to-all-start.1 = ((bf16[8,42,128]{2,1,0:T(8,128)(2,1)}), bf16[8,42,128]{2,1,0:T(8,128)(2,1)S(1)}, u32[]{:S(2)}, u32[]{:S(2)}) async-start(bf16[8,42,128]{2,1,0:T(8,128)(2,1)} %pad_maximum_fusion), calls=%async_computation.1 | async-start | bytes 196608 | tf_op jit(solution)/shard_map/all_to_all | solution.py:245
  53.3 2.4 %collective-permute-start.2 = (bf16[2,40,192]{2,1,0:T(8,128)(2,1)S(1)}, bf16[2,40,192]{2,1,0:T(8,128)(2,1)S(1)}, u32[]{:S(2)}, u32[]{:S(2)}) collective-permute-start(bf16[2,40,192]{2,1,0:T(8,128)(2,1)S(1)} %get-tuple-element.29), channel_id=1, source_target_pairs={{7,0},{0,1},{1,2},{2,3},{3,4},{4,5},{5,6},{6,7},{15,8},{8,9},{9,10... | collective-permute-start | bytes 92168 | tf_op jit(solution)/shard_map/ppermute | solution.py:259
  55.7 5.2 %all-to-all-done.1 = bf16[8,42,128]{2,1,0:T(8,128)(2,1)S(1)} async-done(((bf16[8,42,128]{2,1,0:T(8,128)(2,1)}), bf16[8,42,128]{2,1,0:T(8,128)(2,1)S(1)}, u32[]{:S(2)}, u32[]{:S(2)}) %all-to-all-start.1) | async-done | bytes 86048 | tf_op jit(solution)/shard_map/all_to_all | solution.py:245
  60.9 0.0 collective-permute-done.2.first
  60.9 0.7 broadcast_in_dim.9
  61.6 3.5 %all-to-all-start.2 = ((bf16[12,42,128]{2,1,0:T(8,128)(2,1)}), bf16[12,42,128]{2,1,0:T(8,128)(2,1)S(1)}, u32[]{:S(2)}, u32[]{:S(2)}) async-start(bf16[12,42,128]{2,1,0:T(8,128)(2,1)} %broadcast_in_dim.9), calls=%async_computation.2 | async-start | bytes 294912 | tf_op jit(solution)/shard_map/all_to_all | solution.py:245
  65.1 0.0 copy-start.1
  65.1 2.4 %collective-permute-start.3 = (bf16[2,40,192]{2,1,0:T(8,128)(2,1)S(1)}, bf16[2,40,192]{2,1,0:T(8,128)(2,1)S(1)}, u32[]{:S(2)}, u32[]{:S(2)}) collective-permute-start(bf16[2,40,192]{2,1,0:T(8,128)(2,1)S(1)} %pad_maximum_fusion.1), channel_id=1, source_target_pairs={{760,0},{0,8},{8,16},{16,24},{24,32},{32,40},{40,48},{48,56},{56,6... | collective-permute-start | bytes 92168 | tf_op jit(solution)/shard_map/ppermute | solution.py:259
  67.5 8.8 %all-to-all-done.2 = bf16[12,42,128]{2,1,0:T(8,128)(2,1)S(1)} async-done(((bf16[12,42,128]{2,1,0:T(8,128)(2,1)}), bf16[12,42,128]{2,1,0:T(8,128)(2,1)S(1)}, u32[]{:S(2)}, u32[]{:S(2)}) %all-to-all-start.2) | async-done | bytes 129056 | tf_op jit(solution)/shard_map/all_to_all | solution.py:245
  76.3 0.0 collective-permute-done.3.second
  76.3 0.7 broadcast_in_dim.10
  77.0 3.9 %all-to-all-start.3 = ((bf16[8,42,128]{2,1,0:T(8,128)(2,1)}), bf16[8,42,128]{2,1,0:T(8,128)(2,1)S(1)}, u32[]{:S(2)}, u32[]{:S(2)}) async-start(bf16[8,42,128]{2,1,0:T(8,128)(2,1)} %broadcast_in_dim.10), calls=%async_computation.3 | async-start | bytes 196608 | tf_op jit(solution)/shard_map/all_to_all | solution.py:245
  80.8 0.0 copy-done.1
  80.8 0.2 shard_map.153
  81.1 0.7 copy.34
  81.8 6.6 %all-to-all-done.3 = bf16[8,42,128]{2,1,0:T(8,128)(2,1)S(1)} async-done(((bf16[8,42,128]{2,1,0:T(8,128)(2,1)}), bf16[8,42,128]{2,1,0:T(8,128)(2,1)S(1)}, u32[]{:S(2)}, u32[]{:S(2)}) %all-to-all-start.3) | async-done | bytes 86048 | tf_op jit(solution)/shard_map/all_to_all | solution.py:245
  88.4 0.1 reshape.50
  88.5 0.1 reshape.51
  88.6 0.7 broadcast_in_dim.11
  89.3 8.8 %all-to-all-start.4 = ((bf16[8,24,768]{2,1,0:T(8,128)(2,1)}), bf16[8,24,768]{2,1,0:T(8,128)(2,1)S(1)}, u32[]{:S(2)}, u32[]{:S(2)}) async-start(bf16[8,24,768]{2,1,0:T(8,128)(2,1)} %broadcast_in_dim.11), calls=%async_computation.4 | async-start | bytes 589824 | tf_op jit(solution)/shard_map/all_to_all | solution.py:245
  98.1 0.7 reshape.55
  98.8 6.0 %all-to-all-done.4.parts = bf16[8,24,768]{2,1,0:T(8,128)(2,1)S(1)} async-done(((bf16[8,24,768]{2,1,0:T(8,128)(2,1)}), bf16[8,24,768]{2,1,0:T(8,128)(2,1)S(1)}, u32[]{:S(2)}, u32[]{:S(2)}) %all-to-all-start.4) | async-done | bytes 294944 | tf_op jit(solution)/shard_map/all_to_all | solution.py:245
  104.8 0.9 shard_map.154
  (13 shorter events, 0.2 us)
Async XLA Ops:
  0.6 1.9 %copy-start = (bf16[288,384]{1,0:T(8,128)(2,1)S(1)}, bf16[288,384]{1,0:T(8,128)(2,1)}, u32[]{:S(2)}) copy-start(bf16[288,384]{1,0:T(8,128)(2,1)} %constant.18.clone.sel) | copy-start | bytes 663556
  2.5 18.5 %copy-start.9 = (s32[2,6,12]{2,0,1:T(2,128)S(1)}, s32[2,6,12]{2,0,1:T(2,128)}, u32[]{:S(2)}) copy-start(s32[2,6,12]{2,0,1:T(2,128)} %param.14) | copy-start | bytes 1732
  2.8 18.4 %copy-start.8 = (f32[3312,1,6]{0,1,2:T(1,128)S(1)}, f32[3312,1,6]{0,1,2:T(1,128)}, u32[]{:S(2)}) copy-start(f32[3312,1,6]{0,1,2:T(1,128)} %param.18) | copy-start | bytes 238468
  2.8 22.9 %collective-permute-start = (bf16[144,192]{1,0:T(8,128)(2,1)S(1)}, bf16[144,192]{1,0:T(8,128)(2,1)S(1)}, u32[]{:S(2)}, u32[]{:S(2)}) collective-permute-start(bf16[144,192]{1,0:T(8,128)(2,1)S(1)} %get-tuple-element.21), channel_id=1, source_target_pairs={{8,0},{16,8},{24,16},{32,24},{40,32},{48,40},{56,48},{64,56},{72,6... | collective-permute-start | bytes 165896 | tf_op jit(solution)/shard_map/ppermute | solution.py:259
  21.2 0.9 copy-start.3
  22.1 3.5 %copy-start.6 = (bf16[2,144,144]{2,1,0:T(8,128)(2,1)S(1)}, bf16[2,144,144]{2,1,0:T(8,128)(2,1)}, u32[]{:S(2)}) copy-start(bf16[2,144,144]{2,1,0:T(8,128)(2,1)} %constant.19.clone.sel) | copy-start | bytes 248836
  25.9 7.7 %copy-start.2 = (bf16[192,576]{1,0:T(8,128)(2,1)S(1)}, bf16[192,576]{1,0:T(8,128)(2,1)}, u32[]{:S(2)}) copy-start(bf16[192,576]{1,0:T(8,128)(2,1)} %wqkv.1) | copy-start | bytes 663556
  25.9 7.7 %copy-start.4 = (bf16[192,192]{1,0:T(8,128)(2,1)S(1)}, bf16[192,192]{1,0:T(8,128)(2,1)}, u32[]{:S(2)}) copy-start(bf16[192,192]{1,0:T(8,128)(2,1)} %wproj.1) | copy-start | bytes 221188
  25.9 7.7 %copy-start.5 = (bf16[3,288,144]{2,1,0:T(8,128)(2,1)S(1)}, bf16[3,288,144]{2,1,0:T(8,128)(2,1)}, u32[]{:S(2)}) copy-start(bf16[3,288,144]{2,1,0:T(8,128)(2,1)} %constant.20.clone.sel) | copy-start | bytes 746500
  25.9 7.7 %copy-start.7 = (bf16[160,144]{1,0:T(8,128)(2,1)S(1)}, bf16[160,144]{1,0:T(8,128)(2,1)}, u32[]{:S(2)}) copy-start(bf16[160,144]{1,0:T(8,128)(2,1)} %constant.21.clone.leave) | copy-start | bytes 138244
  25.9 7.6 %collective-permute-start.1 = (bf16[144,192]{1,0:T(8,128)(2,1)S(1)}, bf16[144,192]{1,0:T(8,128)(2,1)S(1)}, u32[]{:S(2)}, u32[]{:S(2)}) collective-permute-start(bf16[144,192]{1,0:T(8,128)(2,1)S(1)} %shard_map.148), channel_id=1, source_target_pairs={{1,0},{2,1},{3,2},{4,3},{5,4},{6,5},{7,6},{0,7},{9,8},{10,9},{11,1... | collective-permute-start | bytes 165896 | tf_op jit(solution)/shard_map/ppermute | solution.py:259
  38.2 10.9 %all-to-all-start = ((bf16[8,24,768]{2,1,0:T(8,128)(2,1)}), bf16[8,24,768]{2,1,0:T(8,128)(2,1)S(1)}, u32[]{:S(2)}, u32[]{:S(2)}) async-start(bf16[8,24,768]{2,1,0:T(8,128)(2,1)} %bitcast.1), calls=%async_computation | async-start | bytes 589824 | tf_op jit(solution)/shard_map/all_to_all | solution.py:245
  49.9 11.0 %all-to-all-start.1 = ((bf16[8,42,128]{2,1,0:T(8,128)(2,1)}), bf16[8,42,128]{2,1,0:T(8,128)(2,1)S(1)}, u32[]{:S(2)}, u32[]{:S(2)}) async-start(bf16[8,42,128]{2,1,0:T(8,128)(2,1)} %pad_maximum_fusion), calls=%async_computation.1 | async-start | bytes 196608 | tf_op jit(solution)/shard_map/all_to_all | solution.py:245
  53.3 7.6 %collective-permute-start.2 = (bf16[2,40,192]{2,1,0:T(8,128)(2,1)S(1)}, bf16[2,40,192]{2,1,0:T(8,128)(2,1)S(1)}, u32[]{:S(2)}, u32[]{:S(2)}) collective-permute-start(bf16[2,40,192]{2,1,0:T(8,128)(2,1)S(1)} %get-tuple-element.29), channel_id=1, source_target_pairs={{7,0},{0,1},{1,2},{2,3},{3,4},{4,5},{5,6},{6,7},{15,8},{8,9},{9,10... | collective-permute-start | bytes 92168 | tf_op jit(solution)/shard_map/ppermute | solution.py:259
  61.6 14.7 %all-to-all-start.2 = ((bf16[12,42,128]{2,1,0:T(8,128)(2,1)}), bf16[12,42,128]{2,1,0:T(8,128)(2,1)S(1)}, u32[]{:S(2)}, u32[]{:S(2)}) async-start(bf16[12,42,128]{2,1,0:T(8,128)(2,1)} %broadcast_in_dim.9), calls=%async_computation.2 | async-start | bytes 294912 | tf_op jit(solution)/shard_map/all_to_all | solution.py:245
  65.1 15.7 %copy-start.1 = (bf16[4,192,40]{2,1,0:T(8,128)(2,1)S(1)}, bf16[4,192,40]{2,1,0:T(8,128)(2,1)}, u32[]{:S(2)}) copy-start(bf16[4,192,40]{2,1,0:T(8,128)(2,1)} %constant.22.clone.sel) | copy-start | bytes 184324
  65.1 11.2 %collective-permute-start.3 = (bf16[2,40,192]{2,1,0:T(8,128)(2,1)S(1)}, bf16[2,40,192]{2,1,0:T(8,128)(2,1)S(1)}, u32[]{:S(2)}, u32[]{:S(2)}) collective-permute-start(bf16[2,40,192]{2,1,0:T(8,128)(2,1)S(1)} %pad_maximum_fusion.1), channel_id=1, source_target_pairs={{760,0},{0,8},{8,16},{16,24},{24,32},{32,40},{40,48},{48,56},{56,6... | collective-permute-start | bytes 92168 | tf_op jit(solution)/shard_map/ppermute | solution.py:259
  77.0 11.4 %all-to-all-start.3 = ((bf16[8,42,128]{2,1,0:T(8,128)(2,1)}), bf16[8,42,128]{2,1,0:T(8,128)(2,1)S(1)}, u32[]{:S(2)}, u32[]{:S(2)}) async-start(bf16[8,42,128]{2,1,0:T(8,128)(2,1)} %broadcast_in_dim.10), calls=%async_computation.3 | async-start | bytes 196608 | tf_op jit(solution)/shard_map/all_to_all | solution.py:245
  89.3 15.5 %all-to-all-start.4 = ((bf16[8,24,768]{2,1,0:T(8,128)(2,1)}), bf16[8,24,768]{2,1,0:T(8,128)(2,1)S(1)}, u32[]{:S(2)}, u32[]{:S(2)}) async-start(bf16[8,24,768]{2,1,0:T(8,128)(2,1)} %broadcast_in_dim.11), calls=%async_computation.4 | async-start | bytes 589824 | tf_op jit(solution)/shard_map/all_to_all | solution.py:245

commit v3 on v2

--- a/solution.py
+++ b/solution.py
@@ -26,19 +26,19 @@
 
 
 def selections():
-    first = np.zeros((288, 384), np.float32)
+    first = np.zeros((288, 288), np.float32)
     second = np.zeros((2, 144, 144), np.float32)
     gather = np.zeros((3, 288, 144), np.float32)
     leave = np.zeros((160, 144), np.float32)
-    place = np.zeros((4, 192, 40), np.float32)
+    place = np.zeros((4, T, 40), np.float32)
     for p in range(2):
         for a in range(6):
             for b in range(12):
-                slab = (((p + 1) % 2) * 6 + a) * 16 + b
+                slab = (a * 12 + b) * 2 + (p + 1) % 2
                 half = (p * 6 + a) * 6 + b % 6
                 wide = (p * 3 + a % 3) * 12 + (b + 6) % 12
                 for arr in range(2):
-                    first[(0 if b < 6 else 144) + arr * 72 + half, arr * 192 + slab] = 1
+                    first[(0 if b < 6 else 144) + arr * 72 + half, arr * T + slab] = 1
                     source = 1 if b < 6 else 0
                     if a < 3:
                         second[source, arr * 72 + wide, arr * 72 + half] = 1
@@ -52,17 +52,17 @@
                         gather[2, arr * 144 + token, arr * 72 + row] = 1
                 row = (p * 3 + a % 3) * 6 + b % 6
                 leave[(80 if a >= 3 else 0) + (40 if b >= 6 else 0) + row, token] = 1
-                home = (((p + 1) % 2) * 6 + (a + 3) % 6) * 16 + (b + 6) % 12
+                home = (((a + 3) % 6) * 12 + (b + 6) % 12) * 2 + (p + 1) % 2
                 place[(2 if b >= 6 else 0) + (1 if a >= 3 else 0), home, row] = 1
     return [jnp.asarray(m, BF16) for m in (first, second, gather, leave, place)]
 
 
-def pack_kernel(tok, cot, sel, strip, kept, slabs):
-    slabs[...] = jnp.zeros_like(slabs)
-    for k in range(12):
-        slabs[k, 0:12, :] = tok[k // 6, k % 6]
-        slabs[12 + k, 0:12, :] = cot[k // 6, k % 6]
-    out = dot(sel[...], slabs[...].reshape(384, C)).astype(BF16)
+def pack_kernel(tok, cot, sel, strip, kept, rows):
+    for arr, ref in enumerate((tok, cot)):
+        for k in range(72):
+            at = arr * T + 2 * k
+            rows[at : at + 2, :] = ref[k // 12, k % 12].astype(F32)
+    out = dot(sel[...], rows[...].astype(BF16)).astype(BF16)
     strip[...] = out[0:T]
     kept[...] = out[T:]
 
@@ -71,24 +71,53 @@
     strip[...] = (dot(sel[0], kept[...]) + dot(sel[1], arrived[...])).astype(BF16)
 
 
-def unpack_kernel(kept, first, second, sel, out):
+def unpack_kernel(kept, first, second, sel, out, rows):
     total = dot(sel[0], kept[0]) + dot(sel[1], first[0])
-    total = total + dot(sel[2], second[0]) + dot(sel[3], second[1])
-    slabs = total.astype(BF16).reshape(12, 16, C)
-    for k in range(12):
-        out[k // 6, k % 6] = slabs[k, 0:12]
-
-
-def finish_kernel(parts, qkv, proj):
-    n, rows, _ = parts.shape
+    rows[...] = total + dot(sel[2], second[0]) + dot(sel[3], second[1])
+    for k in range(72):
+        out[k // 12, k % 12] = rows[2 * k : 2 * k + 2, :].astype(BF16)
+
+
+def mix_kernel(parts, scattered, out, wide):
+    n, rows, _ = out.shape
+    bias_rows = scattered.shape[0] // n
+    rows = rows - bias_rows
+    wide[...] = jnp.sum(parts[...].astype(F32), axis=0)
+    for k in range(n):
+        mine = wide[rows * k : rows * k + rows, :]
+        theirs = scattered[bias_rows * k : bias_rows * k + bias_rows, :]
+        out[k] = jnp.concatenate((mine, theirs), axis=0).astype(BF16)
+
+
+def sum_kernel(parts, out):
+    total = jnp.sum(parts[...].astype(F32), axis=0).astype(BF16)
+    for k in range(out.shape[0]):
+        out[k] = total
+
+
+def split_kernel(parts, out, scattered, wide):
+    n = parts.shape[0]
+    bias_rows = scattered.shape[0] // n
+    rows = parts.shape[1] - bias_rows
     for k in range(n):
         part = parts[k].astype(F32)
-        qkv[rows * k : rows * k + rows, :] = part[:, : 3 * C]
-        proj[rows * k : rows * k + rows, :] = part[:, 3 * C :]
-
-
-def bias_kernel(first, idx, table, col, row, bias, packed, flat):
-    packed[0:T, :] = idx[:, 0:128]
+        wide[rows * k : rows * k + rows, :] = part[0:rows]
+        scattered[bias_rows * k : bias_rows * k + bias_rows, :] = part[rows:]
+    total = wide[...].astype(BF16)
+    for k in range(out.shape[0]):
+        out[k] = total
+
+
+def finish_kernel(parts, qkv, proj):
+    wide = parts[...].reshape(6 * C, 128).astype(F32)
+    for k in range(4):
+        qkv[:, 128 * k : 128 * k + 128] = wide[C * k : C * k + C]
+    qkv[:, 512:576] = wide[4 * C : 5 * C, 0:64]
+    proj[:, 0:64] = wide[4 * C : 5 * C, 64:128]
+    proj[:, 64:C] = wide[5 * C : 6 * C]
+
+
+def packed_rows(idx):
     lane = lax.broadcasted_iota(jnp.int32, (24, 128), 1)
     tail = jnp.zeros((24, 128), jnp.int32)
     for c in range(6):
@@ -97,21 +126,25 @@
         )
         part = pltpu.roll(part, 16 * c, 1) if c else part
         tail = jnp.where((lane >= 16 * c) & (lane < 16 * c + 16), part, tail)
-    packed[T:PACK, :] = tail
-
+    return tail
+
+
+def bias_body(first, table, col, row, packed, bias, flat):
     def block(i, carry):
         at = pl.ds(pl.multiple_of(i * 8, 8), 8)
         position = packed[at, :]
         low = position & 127
         high = position >> 7
-        for h in range(HALF):
-            total = jnp.zeros((8, 128), F32)
-            for k in range(BLKS):
+        totals = [jnp.zeros((8, 128), F32)] * HALF
+        for k in range(BLKS):
+            here = high == k
+            for h in range(HALF):
                 r = (first + h) * BLKS + k
                 values = jnp.broadcast_to(table[r : r + 1, :], (8, 128))
                 found = jnp.take_along_axis(values, low, axis=1, mode="promise_in_bounds")
-                total = jnp.where(high == k, found, total)
-            flat[h, at, :] = total
+                totals[h] = jnp.where(here, found, totals[h])
+        for h in range(HALF):
+            flat[h, at, :] = totals[h]
         return carry
 
     lax.fori_loop(0, PACK // 8, block, 0)
@@ -125,13 +158,22 @@
             bias[h, at, 128:T] = jnp.where(same[at, 128:T], part[:, 0:16], -1e9)
 
 
-def main_kernel(kept, lon, lat, sel, bias_a, bias_b, wqkv, wproj, leave,
-                ret_kept, ret_strip, grads, ds_out, ds_tail):
+def bias_first_kernel(idx, table, col, row, bias, packed, flat):
+    packed[0:T, :] = idx[:, 0:128]
+    packed[T:PACK, :] = packed_rows(idx)
+    bias_body(0, table, col, row, packed, bias, flat)
+
+
+def bias_second_kernel(packed, table, col, row, bias, flat):
+    bias_body(HALF, table, col, row, packed, bias, flat)
+
+
+def main_kernel(kept, lon, lat, sel, bias_a, bias_b, wqkv, wproj,
+                grads, ds_out, grad_in_out, normed_out, inv_std_out, cot_out, ds_tail):
     scale = HD ** (-0.5)
     both = dot(sel[0], kept[...]) + dot(sel[1], lon[...]) + dot(sel[2], lat[...])
     values = both[0:T]
-    cot32 = both[T:]
-    cot = cot32.astype(BF16)
+    cot = both[T:].astype(BF16)
     center = values - jnp.mean(values, axis=-1, keepdims=True)
     inv_std = lax.rsqrt(jnp.mean(center * center, axis=-1, keepdims=True) + 1e-05)
     normed = center * inv_std
@@ -180,31 +222,31 @@
     grad_in = grad_in.astype(BF16)
     grad_qkv = dot(hidden, grad_in, 0, 0)
     grad_proj = dot(attended.astype(BF16), cot, 0, 0)
-    grads[...] = jnp.concatenate((grad_qkv, grad_proj), axis=1).astype(BF16)
-    grad_hidden = dot(grad_in, wqkv[...], 1, 1)
-    grad_norm = inv_std * (
+    both = jnp.concatenate((grad_qkv, grad_proj), axis=1).astype(BF16)
+    for k in range(6):
+        grads[C * k : C * k + C, :] = both[:, 128 * k : 128 * k + 128]
+    grad_in_out[...] = grad_in
+    normed_out[...] = normed
+    inv_std_out[...] = inv_std
+    cot_out[...] = cot
+
+
+def norm_kernel(grad_in, normed_ref, inv_std, cot, wqkv, leave, ret_kept, ret_strip):
+    normed = normed_ref[...]
+    grad_hidden = dot(grad_in[...], wqkv[...], 1, 1)
+    grad_norm = inv_std[...] * (
         grad_hidden
         - jnp.mean(grad_hidden, axis=-1, keepdims=True)
         - normed * jnp.mean(grad_hidden * normed, axis=-1, keepdims=True)
     )
-    returned = (cot32 + grad_norm).astype(BF16)
+    returned = (cot[...].astype(F32) + grad_norm).astype(BF16)
     parts = dot(leave[...], returned).astype(BF16)
     for k in range(2):
         ret_kept[k] = parts[40 * k : 40 * k + 40]
         ret_strip[k] = parts[80 + 40 * k : 120 + 40 * k]
 
 
-def scatter_kernel(idx, ds, out, packed, total):
-    packed[0:T, :] = idx[:, 0:128]
-    lane = lax.broadcasted_iota(jnp.int32, (24, 128), 1)
-    tail = jnp.zeros((24, 128), jnp.int32)
-    for c in range(6):
-        part = jnp.concatenate(
-            (idx[24 * c : 24 * c + 24, 128:T], jnp.zeros((24, 112), jnp.int32)), axis=1
-        )
-        part = pltpu.roll(part, 16 * c, 1) if c else part
-        tail = jnp.where((lane >= 16 * c) & (lane < 16 * c + 16), part, tail)
-    packed[T:PACK, :] = tail
+def scatter_kernel(packed, ds, out, total):
     total[...] = jnp.zeros_like(total)
     blocks = lax.broadcasted_iota(jnp.int32, (32, 128), 0)
     lows = lax.broadcasted_iota(jnp.int32, (128, 128), 0)
@@ -228,7 +270,7 @@
         return carry
 
     lax.fori_loop(0, PACK // 8, block, 0)
-    out[...] = total[...].astype(BF16)
+    out[...] = total[...]
 
 
 def call(kernel, shapes, scratch, cost, *args):
@@ -245,10 +287,6 @@
     return lax.all_to_all(block, axes, 0, 0, axis_index_groups=groups, tiled=False)
 
 
-def summed(parts):
-    return jnp.sum(parts.astype(F32), axis=0)
-
-
 def local(sizes, tokens, cotangent, region, pos_index, w_qkv, w_proj, bias_table):
     n_lon, n_lat, n_y = sizes
     n_z = n_lon // n_y
@@ -261,74 +299,80 @@
     table = jnp.pad(bias_table.reshape(ROWS, HEADS).T, ((0, 0), (0, BLKS * 128 - ROWS)))
     table = table.reshape(HEADS * BLKS, 128)
 
-    def bias_of(head, index):
-        (bias,) = call(
-            functools.partial(bias_kernel, head),
-            [((HALF, T, T), F32)],
-            [((PACK, 128), jnp.int32), ((HALF, PACK, 128), F32)],
-            3 * 10**9,
-            index,
-            table,
-            region.reshape(T, 1),
-            region.reshape(1, T),
-        )
-        return bias
-
+    col, row = region.reshape(T, 1), region.reshape(1, T)
+    bias_shape = ((HALF, T, T), F32)
+    bias_scratch = [((HALF, PACK, 128), F32)]
     block = ((T, C), BF16)
+    order = (1, 2, 0, 3)
     strip, kept = call(
-        pack_kernel, [block] * 2, [((24, 16, C), BF16)], 10**8, tokens, cotangent, first
+        pack_kernel, [block] * 2, [((2 * T, C), F32)], 10**8,
+        tokens.transpose(order), cotangent.transpose(order), first,
     )
     lon = moved(strip, "lon", n_lon, 1)
-    bias_a = bias_of(0, pos_index)
+    bias_a, packed = call(
+        bias_first_kernel, [bias_shape, ((PACK, 128), jnp.int32)], bias_scratch, 3 * 10**9,
+        pos_index, table, col, row,
+    )
     (strip,) = call(repack_kernel, [block], [], 10**8, kept, lon, second)
-    strip, late_index = lax.optimization_barrier((strip, pos_index))
+    strip, late_packed = lax.optimization_barrier((strip, packed))
     lat = moved(strip, across, n_lat, 1)
-    bias_b = bias_of(HALF, late_index)
-    quarter = ((2, 40, C), BF16)
-    ret_kept, ret_strip, grads, ds = call(
+    (bias_b,) = call(
+        bias_second_kernel, [bias_shape], bias_scratch, 3 * 10**9, late_packed, table, col, row
+    )
+    grads, ds, grad_in, normed, inv_std, cot = call(
         main_kernel,
-        [quarter] * 2 + [((C, 4 * C), BF16), ((HEADS, PACK, 128), F32)],
+        [
+            ((6 * C, 128), BF16),
+            ((HEADS, PACK, 128), F32),
+            ((T, 3 * C), BF16),
+            ((T, C), F32),
+            ((T, 1), F32),
+            block,
+        ],
         [((T, 128), F32)],
         10**10,
-        kept, lon, lat, gather, bias_a, bias_b, w_qkv, w_proj, leave,
-    )
-    chunk = exchange(grads.reshape(n_lat, C // n_lat, 4 * C), across)
-    (scattered,) = call(
-        scatter_kernel,
-        [((192, 128), BF16)],
-        [((PACK, 128), jnp.int32), ((192, 128), F32)],
-        5 * 10**9,
-        pos_index,
-        ds,
-    )
-    chunk = summed(chunk).astype(BF16)
-    rows = chunk.size // 128
-    mixed = jnp.concatenate(
-        (chunk.reshape(n_y, rows // n_y, 128), scattered.reshape(n_y, 192 // n_y, 128)), axis=1
+        kept, lon, lat, gather, bias_a, bias_b, w_qkv, w_proj,
     )
     rows_y = [[z * n_y + y for y in range(n_y)] for z in range(n_z)]
     rows_z = [[z * n_y + y for z in range(n_z)] for y in range(n_y)]
-    mixed, ret_strip = lax.optimization_barrier((mixed, ret_strip))
+    rows = 6 * C // n_lat
+    grads = exchange(grads.reshape(n_lat, rows, 128), across)
+    (scattered,) = call(
+        scatter_kernel, [((192, 128), F32)], [((192, 128), F32)], 5 * 10**9, packed, ds
+    )
+    mixed_rows = (rows + 192) // n_y
+    wide = [((rows, 128), F32)]
+    (mixed,) = call(
+        mix_kernel, [((n_y, mixed_rows, 128), BF16)], wide, 10**7, grads, scattered
+    )
+    mixed, grad_in = lax.optimization_barrier((mixed, grad_in))
+    quarter = ((2, 40, C), BF16)
+    ret_kept, ret_strip = call(
+        norm_kernel, [quarter] * 2, [], 10**8, grad_in, normed, inv_std, cot, w_qkv, leave
+    )
     ret_first = moved(ret_strip, across, n_lat, -1)
-    mixed = summed(exchange(mixed, "lon", rows_y)).astype(BF16)
-    mixed = jnp.broadcast_to(mixed, (n_z,) + mixed.shape)
+    mixed = exchange(mixed, "lon", rows_y)
+    (mixed,) = call(sum_kernel, [((n_z, mixed_rows, 128), BF16)], [], 10**7, mixed)
+    mixed = exchange(mixed, "lon", rows_z)
+    (mixed,) = call(sum_kernel, [((n_y, mixed_rows, 128), BF16)], [], 10**7, mixed)
     mixed, ret_first = lax.optimization_barrier((mixed, ret_first))
     ret_second = moved(jnp.stack((ret_kept[1], ret_first[1])), "lon", n_lon, -1)
-    mixed = summed(exchange(mixed, "lon", rows_z)).astype(BF16)
-    mixed = jnp.broadcast_to(mixed, (n_y,) + mixed.shape)
-    mixed, ret_second = lax.optimization_barrier((mixed, ret_second))
+    mixed = exchange(mixed, "lon", rows_y)
+    grads, scattered = call(
+        split_kernel, [((n_lat, rows, 128), BF16), ((192, 128), F32)], wide, 10**7, mixed
+    )
+    grads, ret_second = lax.optimization_barrier((grads, ret_second))
+    grads = exchange(grads, across)
     (grad_tokens,) = call(
-        unpack_kernel, [((2, 6, 12, C), BF16)], [], 10**8, ret_kept, ret_first, ret_second, place,
-    )
-    mixed = exchange(mixed, "lon", rows_y)
-    chunk = mixed[:, : rows // n_y].reshape(C // n_lat, 4 * C)
-    scattered = mixed[:, rows // n_y :].reshape(HEADS, 32 * 128)
-    grads = exchange(jnp.broadcast_to(chunk, (n_lat,) + chunk.shape), across)
+        unpack_kernel, [((6, 12, 2, C), BF16)], [((T, C), F32)], 10**8,
+        ret_kept, ret_first, ret_second, place,
+    )
+    scattered = scattered.reshape(HEADS, 32 * 128)
+    grad_bias = scattered[:, :ROWS].T.reshape(ROWS, 1, HEADS)
     grad_qkv, grad_proj = call(
         finish_kernel, [((C, 3 * C), F32), ((C, C), F32)], [], 10**7, grads
     )
-    grad_bias = scattered[:, :ROWS].astype(F32).T.reshape(ROWS, 1, HEADS)
-    return (grad_tokens, grad_qkv, grad_proj, grad_bias)
+    return (grad_tokens.transpose(2, 0, 1, 3), grad_qkv, grad_proj, grad_bias)
 
 
 def solution(mesh):

time: 107 us -> 104 us (0.972)
  blocking collectives: 0 us -> 10.1 us
  waiting for transfers between devices: 27.5 us -> 18.1 us
  starting transfers between devices: 50.7 us -> 47.7 us
  Pallas kernels: 19.1 us -> 21.9 us
  local copies, waits for them, and re-layouts: 6.7 us -> 4.75 us
    all_to_all x0 -> x1, blocking collectives: none -> 10.1 us  [exchange(): lax.all_to_all(block, axes, 0, 0, axis_index_groups=groups, tiled=False)]
    all_to_all x5 -> x4, waiting for transfers between devices: 27.5 us -> 18.1 us  [exchange(): lax.all_to_all(block, axes, 0, 0, axis_index_groups=groups, tiled=False)]
    all_to_all x5 -> x4, starting transfers between devices: 23.7 us -> 19.9 us  [exchange(): lax.all_to_all(block, axes, 0, 0, axis_index_groups=groups, tiled=False)]
    pallas_call x8 -> x13, Pallas kernels: 19.1 us -> 21.9 us  [call(): pl.pallas_call(kernel, out_shape=[jax.ShapeDtypeStruct(s, d) for s, d in...]
    broadcast_in_dim x3 -> x0, local copies, waits for them, and re-layouts: 2.07 us -> none  [the longest x1 0.73 us: local(): grads = exchange(jnp.broadcast_to(chunk, (n_lat,) + chunk.shape), across)]
    unnamed x25 -> x26, local copies, waits for them, and re-layouts: 3.51 us -> 3.83 us
  transfers between devices with their start and end apart: 9 -> 8, of which waited for: 5 -> 4; matrix products, arithmetic and copies ran while one was open for 2% -> 1% of each run, Pallas kernels for 12% -> 15%
where the time goes in v3:
time: 104 us; the launch traced here: 103 us
  starting transfers between devices  47.7 us (46%)
  Pallas kernels  21.9 us (21%)
  waiting for transfers between devices  18.1 us (17%)
  blocking collectives  10.1 us (10%)
  local copies, waits for them, and re-layouts  4.75 us (5%)
    ppermute x4, starting transfers between devices, moved(): lax.ppermute(block, axes, [((i + distance) % n, i) for i in range(n)])  27.8 us
    pallas_call x13, Pallas kernels, call(): pl.pallas_call(kernel, out_shape=[jax.ShapeDtypeStruct(s, d) for s, d in...  21.9 us
    all_to_all x4, starting transfers between devices, exchange(): lax.all_to_all(block, axes, 0, 0, axis_index_groups=groups, tiled=False)  19.9 us
    all_to_all x4, waiting for transfers between devices, exchange(): lax.all_to_all(block, axes, 0, 0, axis_index_groups=groups, tiled=False)  18.1 us
    all_to_all x1, blocking collectives, exchange(): lax.all_to_all(block, axes, 0, 0, axis_index_groups=groups, tiled=False)  10.1 us
    unnamed x26, local copies, waits for them, and re-layouts  3.83 us
  transfers between devices with their start and end apart: 8, of which 4 were waited for; matrix products, arithmetic and copies ran while one was open for 1% of the time, Pallas kernels for 15%

profile of v3, /device:TPU:1, one launch (start us, length us, event | category | flops | bytes accessed | tf_op | source)
XLA Modules:
  0.0 103.4 jit_solution(17909066364601307039)
XLA Ops:
  0.6 0.0 copy-start.4
  0.6 0.9 copy-done.4
  1.5 0.0 copy-start.5
  1.5 0.9 copy-done.5
  2.4 0.0 copy-start.7
  2.4 0.9 copy-done.7
  3.3 0.0 copy-start.11
  3.3 0.3 shard_map.147
  3.7 0.0 copy-start.10
  3.7 18.2 %collective-permute-start = (bf16[144,192]{1,0:T(8,128)(2,1)S(1)}, bf16[144,192]{1,0:T(8,128)(2,1)S(1)}, u32[]{:S(2)}, u32[]{:S(2)}) collective-permute-start(bf16[144,192]{1,0:T(8,128)(2,1)S(1)} %get-tuple-element.29), channel_id=1, source_target_pairs={{8,0},{16,8},{24,16},{32,24},{40,32},{48,40},{56,48},{64,56},{72,6... | collective-permute-start | bytes 165896 | tf_op jit(solution)/shard_map/ppermute | solution.py:297
  21.9 0.0 copy-done.11
  21.9 0.1 reshape.32.row
  22.0 0.1 reshape.36.col
  22.1 0.0 copy-done.10
  22.1 0.0 copy-start.2
  22.2 0.9 copy-done.2
  23.0 0.0 copy-start.8
  23.0 3.5 %shard_map.149 = (f32[3,144,144]{2,1,0:T(8,128)S(1)}, s32[168,128]{1,0:T(8,128)S(1)}) custom-call(s32[144,144]{1,0:T(8,128)S(1)} %copy-done.2, f32[156,128]{1,0:T(8,128)S(1)} %reshape.30.table, s32[144,1]{1,0:T(8,128)S(1)} %reshape.36.col, s32[1,144]{1,0:T(1,128)S(1)} %reshape.32.row), custom_call_target="tpu_custom_call" | custom-call | flops 3000000000 | bytes 1048576 | tf_op jit(solution)/shard_map/pallas_call | solution.py:277
  26.5 0.0 collective-permute-done.arrived.lon
  26.6 0.0 copy-done.8
  26.6 0.2 shard_map.148
  26.7 0.0 copy-start
  26.8 0.0 copy-start.3
  26.8 0.0 copy-start.6
  26.8 4.1 %collective-permute-start.1 = (bf16[144,192]{1,0:T(8,128)(2,1)S(1)}, bf16[144,192]{1,0:T(8,128)(2,1)S(1)}, u32[]{:S(2)}, u32[]{:S(2)}) collective-permute-start(bf16[144,192]{1,0:T(8,128)(2,1)S(1)} %shard_map.148), channel_id=1, source_target_pairs={{1,0},{2,1},{3,2},{4,3},{5,4},{6,5},{7,6},{0,7},{9,8},{10,9},{11,1... | collective-permute-start | bytes 165896 | tf_op jit(solution)/shard_map/ppermute | solution.py:297
  30.9 3.4 %shard_map.150.bias_b = f32[3,144,144]{2,1,0:T(8,128)S(1)} custom-call(s32[168,128]{1,0:T(8,128)S(1)} %get-tuple-element.33.packed, f32[156,128]{1,0:T(8,128)S(1)} %reshape.30.table, s32[144,1]{1,0:T(8,128)S(1)} %reshape.36.col, s32[1,144]{1,0:T(1,128)S(1)} %reshape.32.row), custom_call_target="tpu_custom_call" | custom-call | flops 3000000000 | bytes 1048576 | tf_op jit(solution)/shard_map/pallas_call | solution.py:277
  34.3 0.0 collective-permute-done.1.lat
  34.3 0.0 copy-done
  34.3 0.0 copy-done.3
  34.3 0.0 copy-done.6
  34.3 4.4 %shard_map.151 = (bf16[1152,128]{1,0:T(8,128)(2,1)}, f32[6,168,128]{2,1,0:T(8,128)S(1)}, bf16[144,576]{1,0:T(8,128)(2,1)S(1)}, f32[144,192]{1,0:T(8,128)S(1)}, f...) custom-call(bf16[144,192]{1,0:T(8,128)(2,1)S(1)} %get-tuple-element.28.kept, ...), custom_call_target="tpu_custom_call" | custom-call | flops 10000000000 | bytes 1048576 | tf_op jit(solution)/shard_map/pallas_call | solution.py:277
  38.7 4.2 %all-to-all-start = ((bf16[8,144,128]{2,1,0:T(8,128)(2,1)}), bf16[8,144,128]{2,1,0:T(8,128)(2,1)S(1)}, u32[]{:S(2)}, u32[]{:S(2)}) async-start(bf16[8,144,128]{2,1,0:T(8,128)(2,1)} %bitcast.3), calls=%async_computation | async-start | bytes 589824 | tf_op jit(solution)/shard_map/all_to_all | solution.py:287
  42.9 5.7 %shard_map.152.scattered = f32[192,128]{1,0:T(8,128)S(1)} custom-call(s32[168,128]{1,0:T(8,128)S(1)} %get-tuple-element.33.packed, f32[6,168,128]{2,1,0:T(8,128)S(1)} %get-tuple-element.35.ds), custom_call_target="tpu_custom_call" | custom-call | flops 5000000000 | bytes 1048576 | tf_op jit(solution)/shard_map/pallas_call | solution.py:277
  48.5 1.1 %all-to-all-done.parts = bf16[8,144,128]{2,1,0:T(8,128)(2,1)S(1)} async-done(((bf16[8,144,128]{2,1,0:T(8,128)(2,1)}), bf16[8,144,128]{2,1,0:T(8,128)(2,1)S(1)}, u32[]{:S(2)}, u32[]{:S(2)}) %all-to-all-start) | async-done | bytes 294944 | tf_op jit(solution)/shard_map/all_to_all | solution.py:287
  49.6 0.1 shard_map.153
  49.7 10.1 %all_to_all.25.parts = bf16[8,42,128]{2,1,0:T(8,128)(2,1)S(1)} all-to-all(bf16[8,42,128]{2,1,0:T(8,128)(2,1)S(1)} %shard_map.153), channel_id=1, replica_groups={{0,8,16,24,32,40,48,56},{64,72,80,88,96,104,112,120},{128,136,144,152,1..., dimensions={0} | all-to-all | bytes 172032 | tf_op jit(solution)/shard_map/all_to_all | solution.py:287
  59.7 0.7 shard_map.155
  60.4 0.0 copy-start.1
  60.4 4.2 %all-to-all-start.2 = ((bf16[12,42,128]{2,1,0:T(8,128)(2,1)}), bf16[12,42,128]{2,1,0:T(8,128)(2,1)S(1)}, u32[]{:S(2)}, u32[]{:S(2)}) async-start(bf16[12,42,128]{2,1,0:T(8,128)(2,1)} %shard_map.155), calls=%async_computation.2 | async-start | bytes 294912 | tf_op jit(solution)/shard_map/all_to_all | solution.py:287
  64.6 0.0 copy-done.1
  64.6 0.5 shard_map.154
  65.1 2.3 %collective-permute-start.2 = (bf16[2,40,192]{2,1,0:T(8,128)(2,1)S(1)}, bf16[2,40,192]{2,1,0:T(8,128)(2,1)S(1)}, u32[]{:S(2)}, u32[]{:S(2)}) collective-permute-start(bf16[2,40,192]{2,1,0:T(8,128)(2,1)S(1)} %get-tuple-element.43), channel_id=1, source_target_pairs={{7,0},{0,1},{1,2},{2,3},{3,4},{4,5},{5,6},{6,7},{15,8},{8,9},{9,10... | collective-permute-start | bytes 92168 | tf_op jit(solution)/shard_map/ppermute | solution.py:297
  67.4 7.9 %all-to-all-done.2.parts = bf16[12,42,128]{2,1,0:T(8,128)(2,1)S(1)} async-done(((bf16[12,42,128]{2,1,0:T(8,128)(2,1)}), bf16[12,42,128]{2,1,0:T(8,128)(2,1)S(1)}, u32[]{:S(2)}, u32[]{:S(2)}) %all-to-all-start.2) | async-done | bytes 129056 | tf_op jit(solution)/shard_map/all_to_all | solution.py:287
  75.3 0.7 shard_map.156
  76.0 0.0 collective-permute-done.2.first
  76.0 3.4 %all-to-all-start.3 = ((bf16[8,42,128]{2,1,0:T(8,128)(2,1)}), bf16[8,42,128]{2,1,0:T(8,128)(2,1)S(1)}, u32[]{:S(2)}, u32[]{:S(2)}) async-start(bf16[8,42,128]{2,1,0:T(8,128)(2,1)} %shard_map.156), calls=%async_computation.3 | async-start | bytes 196608 | tf_op jit(solution)/shard_map/all_to_all | solution.py:287
  79.4 3.3 %collective-permute-start.3 = (bf16[2,40,192]{2,1,0:T(8,128)(2,1)S(1)}, bf16[2,40,192]{2,1,0:T(8,128)(2,1)S(1)}, u32[]{:S(2)}, u32[]{:S(2)}) collective-permute-start(bf16[2,40,192]{2,1,0:T(8,128)(2,1)S(1)} %pad_maximum_fusion), channel_id=1, source_target_pairs={{760,0},{0,8},{8,16},{16,24},{24,32},{32,40},{40,48},{48,56},{56,6... | collective-permute-start | bytes 92168 | tf_op jit(solution)/shard_map/ppermute | solution.py:297
  82.7 4.2 %all-to-all-done.3.parts = bf16[8,42,128]{2,1,0:T(8,128)(2,1)S(1)} async-done(((bf16[8,42,128]{2,1,0:T(8,128)(2,1)}), bf16[8,42,128]{2,1,0:T(8,128)(2,1)S(1)}, u32[]{:S(2)}, u32[]{:S(2)}) %all-to-all-start.3) | async-done | bytes 86048 | tf_op jit(solution)/shard_map/all_to_all | solution.py:287
  86.8 0.8 shard_map.157
  87.6 0.0 collective-permute-done.3.second
  87.6 8.2 %all-to-all-start.4 = ((bf16[8,144,128]{2,1,0:T(8,128)(2,1)}), bf16[8,144,128]{2,1,0:T(8,128)(2,1)S(1)}, u32[]{:S(2)}, u32[]{:S(2)}) async-start(bf16[8,144,128]{2,1,0:T(8,128)(2,1)} %get-tuple-element.48), calls=%async_computation.4 | async-start | bytes 589824 | tf_op jit(solution)/shard_map/all_to_all | solution.py:287
  95.8 0.0 copy-start.9
  95.9 0.7 reshape.35
  96.6 0.2 copy-done.9
  96.8 0.9 shard_map.158
  97.6 4.9 %all-to-all-done.4.parts = bf16[8,144,128]{2,1,0:T(8,128)(2,1)S(1)} async-done(((bf16[8,144,128]{2,1,0:T(8,128)(2,1)}), bf16[8,144,128]{2,1,0:T(8,128)(2,1)S(1)}, u32[]{:S(2)}, u32[]{:S(2)}) %all-to-all-start.4) | async-done | bytes 294944 | tf_op jit(solution)/shard_map/all_to_all | solution.py:287
  102.6 0.9 shard_map.159
  (9 shorter events, 0.1 us)
Async XLA Ops:
  0.6 0.9 copy-start.4
  1.5 0.9 copy-start.5
  2.4 0.9 copy-start.7
  3.3 18.5 %copy-start.11 = (s32[2,6,12]{2,0,1:T(2,128)S(1)}, s32[2,6,12]{2,0,1:T(2,128)}, u32[]{:S(2)}) copy-start(s32[2,6,12]{2,0,1:T(2,128)} %param.14) | copy-start | bytes 1732
  3.7 18.4 %copy-start.10 = (f32[3312,1,6]{0,1,2:T(1,128)S(1)}, f32[3312,1,6]{0,1,2:T(1,128)}, u32[]{:S(2)}) copy-start(f32[3312,1,6]{0,1,2:T(1,128)} %param.18) | copy-start | bytes 238468
  3.7 22.9 %collective-permute-start = (bf16[144,192]{1,0:T(8,128)(2,1)S(1)}, bf16[144,192]{1,0:T(8,128)(2,1)S(1)}, u32[]{:S(2)}, u32[]{:S(2)}) collective-permute-start(bf16[144,192]{1,0:T(8,128)(2,1)S(1)} %get-tuple-element.29), channel_id=1, source_target_pairs={{8,0},{16,8},{24,16},{32,24},{40,32},{48,40},{56,48},{64,56},{72,6... | collective-permute-start | bytes 165896 | tf_op jit(solution)/shard_map/ppermute | solution.py:297
  22.1 0.9 copy-start.2
  23.0 3.5 %copy-start.8 = (bf16[2,144,144]{2,1,0:T(8,128)(2,1)S(1)}, bf16[2,144,144]{2,1,0:T(8,128)(2,1)}, u32[]{:S(2)}) copy-start(bf16[2,144,144]{2,1,0:T(8,128)(2,1)} %constant.14.clone.sel) | copy-start | bytes 248836
  26.7 7.5 %copy-start = (bf16[192,576]{1,0:T(8,128)(2,1)S(1)}, bf16[192,576]{1,0:T(8,128)(2,1)}, u32[]{:S(2)}) copy-start(bf16[192,576]{1,0:T(8,128)(2,1)} %wqkv.3) | copy-start | bytes 663556
  26.8 7.5 %copy-start.3 = (bf16[192,192]{1,0:T(8,128)(2,1)S(1)}, bf16[192,192]{1,0:T(8,128)(2,1)}, u32[]{:S(2)}) copy-start(bf16[192,192]{1,0:T(8,128)(2,1)} %wproj.1) | copy-start | bytes 221188
  26.8 7.5 %copy-start.6 = (bf16[3,288,144]{2,1,0:T(8,128)(2,1)S(1)}, bf16[3,288,144]{2,1,0:T(8,128)(2,1)}, u32[]{:S(2)}) copy-start(bf16[3,288,144]{2,1,0:T(8,128)(2,1)} %constant.15.clone.sel) | copy-start | bytes 746500
  26.8 7.5 %collective-permute-start.1 = (bf16[144,192]{1,0:T(8,128)(2,1)S(1)}, bf16[144,192]{1,0:T(8,128)(2,1)S(1)}, u32[]{:S(2)}, u32[]{:S(2)}) collective-permute-start(bf16[144,192]{1,0:T(8,128)(2,1)S(1)} %shard_map.148), channel_id=1, source_target_pairs={{1,0},{2,1},{3,2},{4,3},{5,4},{6,5},{7,6},{0,7},{9,8},{10,9},{11,1... | collective-permute-start | bytes 165896 | tf_op jit(solution)/shard_map/ppermute | solution.py:297
  38.7 10.9 %all-to-all-start = ((bf16[8,144,128]{2,1,0:T(8,128)(2,1)}), bf16[8,144,128]{2,1,0:T(8,128)(2,1)S(1)}, u32[]{:S(2)}, u32[]{:S(2)}) async-start(bf16[8,144,128]{2,1,0:T(8,128)(2,1)} %bitcast.3), calls=%async_computation | async-start | bytes 589824 | tf_op jit(solution)/shard_map/all_to_all | solution.py:287
  60.4 4.2 %copy-start.1 = (bf16[160,144]{1,0:T(8,128)(2,1)S(1)}, bf16[160,144]{1,0:T(8,128)(2,1)}, u32[]{:S(2)}) copy-start(bf16[160,144]{1,0:T(8,128)(2,1)} %constant.16.clone.leave) | copy-start | bytes 138244
  60.4 14.9 %all-to-all-start.2 = ((bf16[12,42,128]{2,1,0:T(8,128)(2,1)}), bf16[12,42,128]{2,1,0:T(8,128)(2,1)S(1)}, u32[]{:S(2)}, u32[]{:S(2)}) async-start(bf16[12,42,128]{2,1,0:T(8,128)(2,1)} %shard_map.155), calls=%async_computation.2 | async-start | bytes 294912 | tf_op jit(solution)/shard_map/all_to_all | solution.py:287
  65.1 10.9 %collective-permute-start.2 = (bf16[2,40,192]{2,1,0:T(8,128)(2,1)S(1)}, bf16[2,40,192]{2,1,0:T(8,128)(2,1)S(1)}, u32[]{:S(2)}, u32[]{:S(2)}) collective-permute-start(bf16[2,40,192]{2,1,0:T(8,128)(2,1)S(1)} %get-tuple-element.43), channel_id=1, source_target_pairs={{7,0},{0,1},{1,2},{2,3},{3,4},{4,5},{5,6},{6,7},{15,8},{8,9},{9,10... | collective-permute-start | bytes 92168 | tf_op jit(solution)/shard_map/ppermute | solution.py:297
  76.0 10.9 %all-to-all-start.3 = ((bf16[8,42,128]{2,1,0:T(8,128)(2,1)}), bf16[8,42,128]{2,1,0:T(8,128)(2,1)S(1)}, u32[]{:S(2)}, u32[]{:S(2)}) async-start(bf16[8,42,128]{2,1,0:T(8,128)(2,1)} %shard_map.156), calls=%async_computation.3 | async-start | bytes 196608 | tf_op jit(solution)/shard_map/all_to_all | solution.py:287
  79.4 8.2 %collective-permute-start.3 = (bf16[2,40,192]{2,1,0:T(8,128)(2,1)S(1)}, bf16[2,40,192]{2,1,0:T(8,128)(2,1)S(1)}, u32[]{:S(2)}, u32[]{:S(2)}) collective-permute-start(bf16[2,40,192]{2,1,0:T(8,128)(2,1)S(1)} %pad_maximum_fusion), channel_id=1, source_target_pairs={{760,0},{0,8},{8,16},{16,24},{24,32},{32,40},{40,48},{48,56},{56,6... | collective-permute-start | bytes 92168 | tf_op jit(solution)/shard_map/ppermute | solution.py:297
  87.6 15.0 %all-to-all-start.4 = ((bf16[8,144,128]{2,1,0:T(8,128)(2,1)}), bf16[8,144,128]{2,1,0:T(8,128)(2,1)S(1)}, u32[]{:S(2)}, u32[]{:S(2)}) async-start(bf16[8,144,128]{2,1,0:T(8,128)(2,1)} %get-tuple-element.48), calls=%async_computation.4 | async-start | bytes 589824 | tf_op jit(solution)/shard_map/all_to_all | solution.py:287
  95.8 0.9 copy-start.9

commit v4 on v3

--- a/solution.py
+++ b/solution.py
@@ -18,7 +18,6 @@
 BLKS = 26
 PACK = 168
 HALF = HEADS // 2
-PARAMS = pltpu.CompilerParams(vmem_limit_bytes=48 << 20)
 
 
 def dot(a, b, ca=1, cb=0):
@@ -57,14 +56,27 @@
     return [jnp.asarray(m, BF16) for m in (first, second, gather, leave, place)]
 
 
-def pack_kernel(tok, cot, sel, strip, kept, rows):
-    for arr, ref in enumerate((tok, cot)):
+def pack_kernel(tok, cot, sel, idx, strip, kept, packed, tok_in, cot_in, sel_in, idx_in, rows, sems):
+    copies = [
+        pltpu.make_async_copy(src, dst, sems.at[k])
+        for k, (src, dst) in enumerate(
+            ((tok, tok_in), (cot, cot_in), (sel, sel_in), (idx, idx_in))
+        )
+    ]
+    for copy in copies:
+        copy.start()
+    for arr, ref in enumerate((tok_in, cot_in)):
+        copies[arr].wait()
         for k in range(72):
             at = arr * T + 2 * k
             rows[at : at + 2, :] = ref[k // 12, k % 12].astype(F32)
-    out = dot(sel[...], rows[...].astype(BF16)).astype(BF16)
+    copies[2].wait()
+    out = dot(sel_in[...], rows[...].astype(BF16)).astype(BF16)
     strip[...] = out[0:T]
     kept[...] = out[T:]
+    copies[3].wait()
+    packed[0:T, :] = idx_in[:, 0:128]
+    packed[T:PACK, :] = packed_rows(idx_in)
 
 
 def repack_kernel(kept, arrived, sel, strip):
@@ -158,9 +170,7 @@
             bias[h, at, 128:T] = jnp.where(same[at, 128:T], part[:, 0:16], -1e9)
 
 
-def bias_first_kernel(idx, table, col, row, bias, packed, flat):
-    packed[0:T, :] = idx[:, 0:128]
-    packed[T:PACK, :] = packed_rows(idx)
+def bias_first_kernel(packed, table, col, row, bias, flat):
     bias_body(0, table, col, row, packed, bias, flat)
 
 
@@ -273,13 +283,19 @@
     out[...] = total[...]
 
 
-def call(kernel, shapes, scratch, cost, *args):
+def call(kernel, shapes, scratch, cost, *args, copies=0):
+    scratch = [pltpu.VMEM(s, d) for s, d in scratch]
+    specs = {}
+    if copies:
+        scratch.append(pltpu.SemaphoreType.DMA((copies,)))
+        specs["in_specs"] = [pl.BlockSpec(memory_space=pltpu.MemorySpace.HBM)] * copies
     return pl.pallas_call(
         kernel,
         out_shape=[jax.ShapeDtypeStruct(s, d) for s, d in shapes],
-        scratch_shapes=[pltpu.VMEM(s, d) for s, d in scratch],
-        compiler_params=PARAMS,
+        scratch_shapes=scratch,
+        compiler_params=pltpu.CompilerParams(vmem_limit_bytes=(56 if copies else 48) << 20),
         cost_estimate=pl.CostEstimate(flops=cost, bytes_accessed=1 << 20, transcendentals=0),
+        **specs,
     )(*args)
 
 
@@ -304,14 +320,18 @@
     bias_scratch = [((HALF, PACK, 128), F32)]
     block = ((T, C), BF16)
     order = (1, 2, 0, 3)
-    strip, kept = call(
-        pack_kernel, [block] * 2, [((2 * T, C), F32)], 10**8,
-        tokens.transpose(order), cotangent.transpose(order), first,
+    stored = ((6, 12, 2, C), BF16)
+    strip, kept, packed = call(
+        pack_kernel,
+        [block] * 2 + [((PACK, 128), jnp.int32)],
+        [stored, stored, ((2 * T, 2 * T), BF16), ((T, T), jnp.int32), ((2 * T, C), F32)],
+        10**8,
+        tokens.transpose(order), cotangent.transpose(order), first, pos_index,
+        copies=4,
     )
     lon = moved(strip, "lon", n_lon, 1)
-    bias_a, packed = call(
-        bias_first_kernel, [bias_shape, ((PACK, 128), jnp.int32)], bias_scratch, 3 * 10**9,
-        pos_index, table, col, row,
+    (bias_a,) = call(
+        bias_first_kernel, [bias_shape], bias_scratch, 3 * 10**9, packed, table, col, row
     )
     (strip,) = call(repack_kernel, [block], [], 10**8, kept, lon, second)
     strip, late_packed = lax.optimization_barrier((strip, packed))

time: 104 us -> 103 us (level)
  local copies, waits for them, and re-layouts: 4.75 us -> 2.04 us
  Pallas kernels: 21.9 us -> 23.5 us
    unnamed x26 -> x22, local copies, waits for them, and re-layouts: 3.83 us -> 1.12 us
    pallas_call x13, Pallas kernels: 21.9 us -> 23.5 us  [call(): pl.pallas_call(kernel, out_shape=[jax.ShapeDtypeStruct(s, d) for s, d in...]
where the time goes in v4:
time: 103 us
  starting transfers between devices  48.1 us (47%)
  Pallas kernels  23.5 us (23%)
  waiting for transfers between devices  18 us (17%)
  blocking collectives  10.1 us (10%)
  local copies, waits for them, and re-layouts  2.04 us (2%)
    ppermute x4, starting transfers between devices, moved(): lax.ppermute(block, axes, [((i + distance) % n, i) for i in range(n)])  27.9 us
    pallas_call x13, Pallas kernels, call(): pl.pallas_call(kernel, out_shape=[jax.ShapeDtypeStruct(s, d) for s, d in...  23.5 us
    all_to_all x4, starting transfers between devices, exchange(): lax.all_to_all(block, axes, 0, 0, axis_index_groups=groups, tiled=False)  20.3 us
    all_to_all x4, waiting for transfers between devices, exchange(): lax.all_to_all(block, axes, 0, 0, axis_index_groups=groups, tiled=False)  18 us
    all_to_all x1, blocking collectives, exchange(): lax.all_to_all(block, axes, 0, 0, axis_index_groups=groups, tiled=False)  10.1 us
  transfers between devices with their start and end apart: 8, of which 4 were waited for; matrix products, arithmetic and copies ran while one was open for 1% of the time, Pallas kernels for 15%

profile of v4, /device:TPU:1, one launch (start us, length us, event | category | flops | bytes accessed | tf_op | source)
XLA Modules:
  0.0 102.6 jit_solution(18408330393366388297)
XLA Ops:
  0.6 0.0 copy-start.9
  0.6 2.0 %shard_map.147 = (bf16[144,192]{1,0:T(8,128)(2,1)}, bf16[144,192]{1,0:T(8,128)(2,1)}, s32[168,128]{1,0:T(8,128)}) custom-call(bf16[6,12,2,192]{3,2,1,0:T(2,128)(2,1)} %bitcast.14, bf16[6,12,2,192]{3,2,1,0:T(2,128)(2,1)} %bitcast.15, bf16[288,288]{1,0:T(8,128)(2,1)} %constant.13.clone.sel, s32[144,144]{1,0:T(8,128)} %idx.1), custom_call_target="tpu_custom_call" | custom-call | flops 100000000 | bytes 1048576 | tf_op jit(solution)/shard_map/pallas_call | solution.py:292
  2.7 0.0 copy-start.8
  2.7 18.2 %collective-permute-start = (bf16[144,192]{1,0:T(8,128)(2,1)}, bf16[144,192]{1,0:T(8,128)(2,1)S(1)}, u32[]{:S(2)}, u32[]{:S(2)}) collective-permute-start(bf16[144,192]{1,0:T(8,128)(2,1)} %get-tuple-element.28), channel_id=1, source_target_pairs={{8,0},{16,8},{24,16},{32,24},{40,32},{48,40},{56,48},{64,56},{72,6... | collective-permute-start | bytes 165896 | tf_op jit(solution)/shard_map/ppermute | solution.py:313
  20.8 0.0 copy-done.9
  20.9 0.1 reshape.32.row
  20.9 0.1 reshape.36.col
  21.0 0.0 copy-done.8
  21.1 0.0 copy-start.3
  21.1 0.9 copy-done.3
  22.0 0.0 copy-start.4
  22.0 0.0 copy-start.6
  22.0 3.4 %shard_map.149.bias_a = f32[3,144,144]{2,1,0:T(8,128)S(1)} custom-call(s32[168,128]{1,0:T(8,128)S(1)} %copy-done.3, f32[156,128]{1,0:T(8,128)S(1)} %reshape.30.table, s32[144,1]{1,0:T(8,128)S(1)} %reshape.36.col, s32[1,144]{1,0:T(1,128)S(1)} %reshape.32.row), custom_call_target="tpu_custom_call" | custom-call | flops 3000000000 | bytes 1048576 | tf_op jit(solution)/shard_map/pallas_call | solution.py:292
  25.4 0.0 collective-permute-done.arrived.lon
  25.4 0.0 copy-done.4
  25.4 0.0 copy-done.6
  25.4 0.2 shard_map.148
  25.6 0.0 copy-start
  25.6 0.0 copy-start.2
  25.6 0.0 copy-start.5
  25.6 4.1 %collective-permute-start.1 = (bf16[144,192]{1,0:T(8,128)(2,1)S(1)}, bf16[144,192]{1,0:T(8,128)(2,1)S(1)}, u32[]{:S(2)}, u32[]{:S(2)}) collective-permute-start(bf16[144,192]{1,0:T(8,128)(2,1)S(1)} %shard_map.148), channel_id=1, source_target_pairs={{1,0},{2,1},{3,2},{4,3},{5,4},{6,5},{7,6},{0,7},{9,8},{10,9},{11,1... | collective-permute-start | bytes 165896 | tf_op jit(solution)/shard_map/ppermute | solution.py:313
  29.7 3.4 %shard_map.150.bias_b = f32[3,144,144]{2,1,0:T(8,128)S(1)} custom-call(s32[168,128]{1,0:T(8,128)S(1)} %copy-done.3, f32[156,128]{1,0:T(8,128)S(1)} %reshape.30.table, s32[144,1]{1,0:T(8,128)S(1)} %reshape.36.col, s32[1,144]{1,0:T(1,128)S(1)} %reshape.32.row), custom_call_target="tpu_custom_call" | custom-call | flops 3000000000 | bytes 1048576 | tf_op jit(solution)/shard_map/pallas_call | solution.py:292
  33.1 0.0 collective-permute-done.1.lat
  33.1 0.0 copy-done
  33.1 0.0 copy-done.2
  33.1 0.0 copy-done.5
  33.1 4.4 %shard_map.151 = (bf16[1152,128]{1,0:T(8,128)(2,1)}, f32[6,168,128]{2,1,0:T(8,128)S(1)}, bf16[144,576]{1,0:T(8,128)(2,1)S(1)}, f32[144,192]{1,0:T(8,128)S(1)}, f...) custom-call(bf16[144,192]{1,0:T(8,128)(2,1)S(1)} %copy-done.4, bf16[144,192]{1,0:T(8,128)(2,1)S(1)} %collective-permute-done.arrived.lon, ...), custom_call_target="tpu_custom_call" | custom-call | flops 10000000000 | bytes 1048576 | tf_op jit(solution)/shard_map/pallas_call | solution.py:292
  37.5 4.1 %all-to-all-start = ((bf16[8,144,128]{2,1,0:T(8,128)(2,1)}), bf16[8,144,128]{2,1,0:T(8,128)(2,1)S(1)}, u32[]{:S(2)}, u32[]{:S(2)}) async-start(bf16[8,144,128]{2,1,0:T(8,128)(2,1)} %bitcast.3), calls=%async_computation | async-start | bytes 589824 | tf_op jit(solution)/shard_map/all_to_all | solution.py:303
  41.7 5.7 %shard_map.152.scattered = f32[192,128]{1,0:T(8,128)S(1)} custom-call(s32[168,128]{1,0:T(8,128)S(1)} %copy-done.3, f32[6,168,128]{2,1,0:T(8,128)S(1)} %get-tuple-element.33.ds), custom_call_target="tpu_custom_call" | custom-call | flops 5000000000 | bytes 1048576 | tf_op jit(solution)/shard_map/pallas_call | solution.py:292
  47.4 1.0 all-to-all-done.parts
  48.4 0.1 shard_map.153
  48.5 10.1 %all_to_all.25.parts = bf16[8,42,128]{2,1,0:T(8,128)(2,1)S(1)} all-to-all(bf16[8,42,128]{2,1,0:T(8,128)(2,1)S(1)} %shard_map.153), channel_id=1, replica_groups={{0,8,16,24,32,40,48,56},{64,72,80,88,96,104,112,120},{128,136,144,152,1..., dimensions={0} | all-to-all | bytes 172032 | tf_op jit(solution)/shard_map/all_to_all | solution.py:303
  58.5 0.7 shard_map.155
  59.2 0.0 copy-start.1
  59.2 4.5 %all-to-all-start.2 = ((bf16[12,42,128]{2,1,0:T(8,128)(2,1)}), bf16[12,42,128]{2,1,0:T(8,128)(2,1)S(1)}, u32[]{:S(2)}, u32[]{:S(2)}) async-start(bf16[12,42,128]{2,1,0:T(8,128)(2,1)} %shard_map.155), calls=%async_computation.2 | async-start | bytes 294912 | tf_op jit(solution)/shard_map/all_to_all | solution.py:303
  63.8 0.0 copy-done.1
  63.8 0.5 shard_map.154
  64.3 2.3 %collective-permute-start.2 = (bf16[2,40,192]{2,1,0:T(8,128)(2,1)S(1)}, bf16[2,40,192]{2,1,0:T(8,128)(2,1)S(1)}, u32[]{:S(2)}, u32[]{:S(2)}) collective-permute-start(bf16[2,40,192]{2,1,0:T(8,128)(2,1)S(1)} %get-tuple-element.41), channel_id=1, source_target_pairs={{7,0},{0,1},{1,2},{2,3},{3,4},{4,5},{5,6},{6,7},{15,8},{8,9},{9,10... | collective-permute-start | bytes 92168 | tf_op jit(solution)/shard_map/ppermute | solution.py:313
  66.6 7.9 %all-to-all-done.2.parts = bf16[12,42,128]{2,1,0:T(8,128)(2,1)S(1)} async-done(((bf16[12,42,128]{2,1,0:T(8,128)(2,1)}), bf16[12,42,128]{2,1,0:T(8,128)(2,1)S(1)}, u32[]{:S(2)}, u32[]{:S(2)}) %all-to-all-start.2) | async-done | bytes 129056 | tf_op jit(solution)/shard_map/all_to_all | solution.py:303
  74.5 0.7 shard_map.156
  75.2 0.0 collective-permute-done.2.first
  75.2 3.4 %all-to-all-start.3 = ((bf16[8,42,128]{2,1,0:T(8,128)(2,1)}), bf16[8,42,128]{2,1,0:T(8,128)(2,1)S(1)}, u32[]{:S(2)}, u32[]{:S(2)}) async-start(bf16[8,42,128]{2,1,0:T(8,128)(2,1)} %shard_map.156), calls=%async_computation.3 | async-start | bytes 196608 | tf_op jit(solution)/shard_map/all_to_all | solution.py:303
  78.6 3.3 %collective-permute-start.3 = (bf16[2,40,192]{2,1,0:T(8,128)(2,1)S(1)}, bf16[2,40,192]{2,1,0:T(8,128)(2,1)S(1)}, u32[]{:S(2)}, u32[]{:S(2)}) collective-permute-start(bf16[2,40,192]{2,1,0:T(8,128)(2,1)S(1)} %pad_maximum_fusion), channel_id=1, source_target_pairs={{760,0},{0,8},{8,16},{16,24},{24,32},{32,40},{40,48},{48,56},{56,6... | collective-permute-start | bytes 92168 | tf_op jit(solution)/shard_map/ppermute | solution.py:313
  81.8 4.2 %all-to-all-done.3.parts = bf16[8,42,128]{2,1,0:T(8,128)(2,1)S(1)} async-done(((bf16[8,42,128]{2,1,0:T(8,128)(2,1)}), bf16[8,42,128]{2,1,0:T(8,128)(2,1)S(1)}, u32[]{:S(2)}, u32[]{:S(2)}) %all-to-all-start.3) | async-done | bytes 86048 | tf_op jit(solution)/shard_map/all_to_all | solution.py:303
  86.0 0.8 shard_map.157
  86.8 0.0 collective-permute-done.3.second
  86.8 8.2 %all-to-all-start.4 = ((bf16[8,144,128]{2,1,0:T(8,128)(2,1)}), bf16[8,144,128]{2,1,0:T(8,128)(2,1)S(1)}, u32[]{:S(2)}, u32[]{:S(2)}) async-start(bf16[8,144,128]{2,1,0:T(8,128)(2,1)} %get-tuple-element.46), calls=%async_computation.4 | async-start | bytes 589824 | tf_op jit(solution)/shard_map/all_to_all | solution.py:303
  95.0 0.0 copy-start.7
  95.1 0.7 reshape.35
  95.8 0.2 copy-done.7
  95.9 0.9 shard_map.158
  96.8 4.9 %all-to-all-done.4.parts = bf16[8,144,128]{2,1,0:T(8,128)(2,1)S(1)} async-done(((bf16[8,144,128]{2,1,0:T(8,128)(2,1)}), bf16[8,144,128]{2,1,0:T(8,128)(2,1)S(1)}, u32[]{:S(2)}, u32[]{:S(2)}) %all-to-all-start.4) | async-done | bytes 294944 | tf_op jit(solution)/shard_map/all_to_all | solution.py:303
  101.8 0.9 shard_map.159
  (9 shorter events, 0.1 us)
Async XLA Ops:
  0.6 20.2 %copy-start.9 = (s32[2,6,12]{2,0,1:T(2,128)S(1)}, s32[2,6,12]{2,0,1:T(2,128)}, u32[]{:S(2)}) copy-start(s32[2,6,12]{2,0,1:T(2,128)} %param.14) | copy-start | bytes 1732
  2.7 18.4 %copy-start.8 = (f32[3312,1,6]{0,1,2:T(1,128)S(1)}, f32[3312,1,6]{0,1,2:T(1,128)}, u32[]{:S(2)}) copy-start(f32[3312,1,6]{0,1,2:T(1,128)} %param.18) | copy-start | bytes 238468
  2.7 22.7 %collective-permute-start = (bf16[144,192]{1,0:T(8,128)(2,1)}, bf16[144,192]{1,0:T(8,128)(2,1)S(1)}, u32[]{:S(2)}, u32[]{:S(2)}) collective-permute-start(bf16[144,192]{1,0:T(8,128)(2,1)} %get-tuple-element.28), channel_id=1, source_target_pairs={{8,0},{16,8},{24,16},{32,24},{40,32},{48,40},{56,48},{64,56},{72,6... | collective-permute-start | bytes 165896 | tf_op jit(solution)/shard_map/ppermute | solution.py:313
  21.1 0.9 copy-start.3
  22.0 3.4 %copy-start.4 = (bf16[144,192]{1,0:T(8,128)(2,1)S(1)}, bf16[144,192]{1,0:T(8,128)(2,1)}, u32[]{:S(2)}) copy-start(bf16[144,192]{1,0:T(8,128)(2,1)} %get-tuple-element.27.kept) | copy-start | bytes 165892
  22.0 3.4 %copy-start.6 = (bf16[2,144,144]{2,1,0:T(8,128)(2,1)S(1)}, bf16[2,144,144]{2,1,0:T(8,128)(2,1)}, u32[]{:S(2)}) copy-start(bf16[2,144,144]{2,1,0:T(8,128)(2,1)} %constant.14.clone.sel) | copy-start | bytes 248836
  25.6 7.5 %copy-start = (bf16[192,576]{1,0:T(8,128)(2,1)S(1)}, bf16[192,576]{1,0:T(8,128)(2,1)}, u32[]{:S(2)}) copy-start(bf16[192,576]{1,0:T(8,128)(2,1)} %wqkv.3) | copy-start | bytes 663556
  25.6 7.5 %copy-start.2 = (bf16[192,192]{1,0:T(8,128)(2,1)S(1)}, bf16[192,192]{1,0:T(8,128)(2,1)}, u32[]{:S(2)}) copy-start(bf16[192,192]{1,0:T(8,128)(2,1)} %wproj.1) | copy-start | bytes 221188
  25.6 7.5 %copy-start.5 = (bf16[3,288,144]{2,1,0:T(8,128)(2,1)S(1)}, bf16[3,288,144]{2,1,0:T(8,128)(2,1)}, u32[]{:S(2)}) copy-start(bf16[3,288,144]{2,1,0:T(8,128)(2,1)} %constant.15.clone.sel) | copy-start | bytes 746500
  25.6 7.5 %collective-permute-start.1 = (bf16[144,192]{1,0:T(8,128)(2,1)S(1)}, bf16[144,192]{1,0:T(8,128)(2,1)S(1)}, u32[]{:S(2)}, u32[]{:S(2)}) collective-permute-start(bf16[144,192]{1,0:T(8,128)(2,1)S(1)} %shard_map.148), channel_id=1, source_target_pairs={{1,0},{2,1},{3,2},{4,3},{5,4},{6,5},{7,6},{0,7},{9,8},{10,9},{11,1... | collective-permute-start | bytes 165896 | tf_op jit(solution)/shard_map/ppermute | solution.py:313
  37.5 10.9 %all-to-all-start = ((bf16[8,144,128]{2,1,0:T(8,128)(2,1)}), bf16[8,144,128]{2,1,0:T(8,128)(2,1)S(1)}, u32[]{:S(2)}, u32[]{:S(2)}) async-start(bf16[8,144,128]{2,1,0:T(8,128)(2,1)} %bitcast.3), calls=%async_computation | async-start | bytes 589824 | tf_op jit(solution)/shard_map/all_to_all | solution.py:303
  59.2 4.5 %copy-start.1 = (bf16[160,144]{1,0:T(8,128)(2,1)S(1)}, bf16[160,144]{1,0:T(8,128)(2,1)}, u32[]{:S(2)}) copy-start(bf16[160,144]{1,0:T(8,128)(2,1)} %constant.16.clone.leave) | copy-start | bytes 138244
  59.2 15.3 %all-to-all-start.2 = ((bf16[12,42,128]{2,1,0:T(8,128)(2,1)}), bf16[12,42,128]{2,1,0:T(8,128)(2,1)S(1)}, u32[]{:S(2)}, u32[]{:S(2)}) async-start(bf16[12,42,128]{2,1,0:T(8,128)(2,1)} %shard_map.155), calls=%async_computation.2 | async-start | bytes 294912 | tf_op jit(solution)/shard_map/all_to_all | solution.py:303
  64.3 10.9 %collective-permute-start.2 = (bf16[2,40,192]{2,1,0:T(8,128)(2,1)S(1)}, bf16[2,40,192]{2,1,0:T(8,128)(2,1)S(1)}, u32[]{:S(2)}, u32[]{:S(2)}) collective-permute-start(bf16[2,40,192]{2,1,0:T(8,128)(2,1)S(1)} %get-tuple-element.41), channel_id=1, source_target_pairs={{7,0},{0,1},{1,2},{2,3},{3,4},{4,5},{5,6},{6,7},{15,8},{8,9},{9,10... | collective-permute-start | bytes 92168 | tf_op jit(solution)/shard_map/ppermute | solution.py:313
  75.2 10.9 %all-to-all-start.3 = ((bf16[8,42,128]{2,1,0:T(8,128)(2,1)}), bf16[8,42,128]{2,1,0:T(8,128)(2,1)S(1)}, u32[]{:S(2)}, u32[]{:S(2)}) async-start(bf16[8,42,128]{2,1,0:T(8,128)(2,1)} %shard_map.156), calls=%async_computation.3 | async-start | bytes 196608 | tf_op jit(solution)/shard_map/all_to_all | solution.py:303
  78.6 8.2 %collective-permute-start.3 = (bf16[2,40,192]{2,1,0:T(8,128)(2,1)S(1)}, bf16[2,40,192]{2,1,0:T(8,128)(2,1)S(1)}, u32[]{:S(2)}, u32[]{:S(2)}) collective-permute-start(bf16[2,40,192]{2,1,0:T(8,128)(2,1)S(1)} %pad_maximum_fusion), channel_id=1, source_target_pairs={{760,0},{0,8},{8,16},{16,24},{24,32},{32,40},{40,48},{48,56},{56,6... | collective-permute-start | bytes 92168 | tf_op jit(solution)/shard_map/ppermute | solution.py:313
  86.8 15.0 %all-to-all-start.4 = ((bf16[8,144,128]{2,1,0:T(8,128)(2,1)}), bf16[8,144,128]{2,1,0:T(8,128)(2,1)S(1)}, u32[]{:S(2)}, u32[]{:S(2)}) async-start(bf16[8,144,128]{2,1,0:T(8,128)(2,1)} %get-tuple-element.46), calls=%async_computation.4 | async-start | bytes 589824 | tf_op jit(solution)/shard_map/all_to_all | solution.py:303
  95.0 0.9 copy-start.7

commit v5 on v4

--- a/solution.py
+++ b/solution.py
@@ -289,11 +289,13 @@
     if copies:
         scratch.append(pltpu.SemaphoreType.DMA((copies,)))
         specs["in_specs"] = [pl.BlockSpec(memory_space=pltpu.MemorySpace.HBM)] * copies
+    if copies:
+        args = [pltpu.with_memory_space_constraint(a, pltpu.MemorySpace.HBM) for a in args]
     return pl.pallas_call(
         kernel,
         out_shape=[jax.ShapeDtypeStruct(s, d) for s, d in shapes],
         scratch_shapes=scratch,
-        compiler_params=pltpu.CompilerParams(vmem_limit_bytes=(56 if copies else 48) << 20),
+        compiler_params=pltpu.CompilerParams(vmem_limit_bytes=(48 if copies else 48) << 20),
         cost_estimate=pl.CostEstimate(flops=cost, bytes_accessed=1 << 20, transcendentals=0),
         **specs,
     )(*args)
@@ -365,6 +367,10 @@
     (mixed,) = call(
         mix_kernel, [((n_y, mixed_rows, 128), BF16)], wide, 10**7, grads, scattered
     )
+    mixed = exchange(mixed, "lon", rows_y)
+    (mixed,) = call(sum_kernel, [((n_z, mixed_rows, 128), BF16)], [], 10**7, mixed)
+    mixed = exchange(mixed, "lon", rows_z)
+    (mixed,) = call(sum_kernel, [((n_y, mixed_rows, 128), BF16)], [], 10**7, mixed)
     mixed, grad_in = lax.optimization_barrier((mixed, grad_in))
     quarter = ((2, 40, C), BF16)
     ret_kept, ret_strip = call(
@@ -372,16 +378,11 @@
     )
     ret_first = moved(ret_strip, across, n_lat, -1)
     mixed = exchange(mixed, "lon", rows_y)
-    (mixed,) = call(sum_kernel, [((n_z, mixed_rows, 128), BF16)], [], 10**7, mixed)
-    mixed = exchange(mixed, "lon", rows_z)
-    (mixed,) = call(sum_kernel, [((n_y, mixed_rows, 128), BF16)], [], 10**7, mixed)
-    mixed, ret_first = lax.optimization_barrier((mixed, ret_first))
-    ret_second = moved(jnp.stack((ret_kept[1], ret_first[1])), "lon", n_lon, -1)
-    mixed = exchange(mixed, "lon", rows_y)
     grads, scattered = call(
         split_kernel, [((n_lat, rows, 128), BF16), ((192, 128), F32)], wide, 10**7, mixed
     )
-    grads, ret_second = lax.optimization_barrier((grads, ret_second))
+    grads, ret_first = lax.optimization_barrier((grads, ret_first))
+    ret_second = moved(jnp.stack((ret_kept[1], ret_first[1])), "lon", n_lon, -1)
     grads = exchange(grads, across)
     (grad_tokens,) = call(
         unpack_kernel, [((6, 12, 2, C), BF16)], [((T, C), F32)], 10**8,

time: 103 us -> 104 us (level)
  blocking collectives: 10.1 us -> 25.6 us
  waiting for transfers between devices: 18 us -> 10.9 us
  starting transfers between devices: 48.1 us -> 42.5 us
  Pallas kernels: 23.5 us -> 22.2 us
  local copies, waits for them, and re-layouts: 2.04 us -> 0.98 us
    all_to_all x1 -> x2, blocking collectives: 10.1 us -> 25.6 us  [exchange(): lax.all_to_all(block, axes, 0, 0, axis_index_groups=groups, tiled=False)]
    all_to_all x4 -> x3, waiting for transfers between devices: 18 us -> 5.59 us  [exchange(): lax.all_to_all(block, axes, 0, 0, axis_index_groups=groups, tiled=False)]
    ppermute x4, waiting for transfers between devices: 0.01 us -> 5.34 us  [moved(): lax.ppermute(block, axes, [((i + distance) % n, i) for i in range(n)])]
    all_to_all x4 -> x3, starting transfers between devices: 20.3 us -> 15.7 us  [exchange(): lax.all_to_all(block, axes, 0, 0, axis_index_groups=groups, tiled=False)]
    pallas_call x13, Pallas kernels: 23.5 us -> 22.2 us  [call(): pl.pallas_call(kernel, out_shape=[jax.ShapeDtypeStruct(s, d) for s, d in...]
    unnamed x22 -> x18, local copies, waits for them, and re-layouts: 1.12 us -> 0.07 us
  transfers between devices with their start and end apart: 8 -> 7, of which waited for: 4 -> 4; matrix products, arithmetic and copies ran while one was open for 1% -> 1% of each run, Pallas kernels for 15% -> 14%
where the time goes in v5:
time: 104 us; the launch traced here: 103 us
  starting transfers between devices  42.5 us (41%)
  blocking collectives  25.6 us (25%)
  Pallas kernels  22.2 us (21%)
  waiting for transfers between devices  10.9 us (10%)
    ppermute x4, starting transfers between devices, moved(): lax.ppermute(block, axes, [((i + distance) % n, i) for i in range(n)])  26.8 us
    all_to_all x2, blocking collectives, exchange(): lax.all_to_all(block, axes, 0, 0, axis_index_groups=groups, tiled=False)  25.6 us
    pallas_call x13, Pallas kernels, call(): pl.pallas_call(kernel, out_shape=[jax.ShapeDtypeStruct(s, d) for s, d in...  22.2 us
    all_to_all x3, starting transfers between devices, exchange(): lax.all_to_all(block, axes, 0, 0, axis_index_groups=groups, tiled=False)  15.7 us
    all_to_all x3, waiting for transfers between devices, exchange(): lax.all_to_all(block, axes, 0, 0, axis_index_groups=groups, tiled=False)  5.59 us
    ppermute x4, waiting for transfers between devices, moved(): lax.ppermute(block, axes, [((i + distance) % n, i) for i in range(n)])  5.34 us
  transfers between devices with their start and end apart: 7, of which 4 were waited for; matrix products, arithmetic and copies ran while one was open for 1% of the time, Pallas kernels for 14%

profile of v5, /device:TPU:1, one launch (start us, length us, event | category | flops | bytes accessed | tf_op | source)
XLA Modules:
  0.0 103.2 jit_solution(4898885705757153458)
XLA Ops:
  0.6 0.0 copy-start.7
  0.6 1.4 %shard_map.147 = (bf16[144,192]{1,0:T(8,128)(2,1)S(1)}, bf16[144,192]{1,0:T(8,128)(2,1)S(1)}, s32[168,128]{1,0:T(8,128)S(1)}) custom-call(bf16[6,12,2,192]{3,2,1,0:T(2,128)(2,1)} %bitcast.14, bf16[6,12,2,192]{3,2,1,0:T(2,128)(2,1)} %bitcast.15, bf16[288,288]{1,0:T(8,128)(2,1)} %constant.13.clone.sel, s32[144,144]{1,0:T(8,128)} %idx.1), custom_call_target="tpu_custom_call" | custom-call | flops 100000000 | bytes 1048576 | tf_op jit(solution)/shard_map/pallas_call | solution.py:294
  2.0 0.0 copy-start.6
  2.0 18.2 %collective-permute-start = (bf16[144,192]{1,0:T(8,128)(2,1)S(1)}, bf16[144,192]{1,0:T(8,128)(2,1)S(1)}, u32[]{:S(2)}, u32[]{:S(2)}) collective-permute-start(bf16[144,192]{1,0:T(8,128)(2,1)S(1)} %get-tuple-element.26), channel_id=1, source_target_pairs={{8,0},{16,8},{24,16},{32,24},{40,32},{48,40},{56,48},{64,56},{72,6... | collective-permute-start | bytes 165896 | tf_op jit(solution)/shard_map/ppermute | solution.py:315
  20.2 0.0 copy-done.7
  20.2 0.1 reshape.32.row
  20.3 0.1 reshape.36.col
  20.4 0.0 copy-done.6
  20.5 0.0 copy-start.4
  20.5 3.4 %shard_map.149.bias_a = f32[3,144,144]{2,1,0:T(8,128)S(1)} custom-call(s32[168,128]{1,0:T(8,128)S(1)} %get-tuple-element.29.packed, f32[156,128]{1,0:T(8,128)S(1)} %reshape.30.table, s32[144,1]{1,0:T(8,128)S(1)} %reshape.36.col, s32[1,144]{1,0:T(1,128)S(1)} %reshape.32.row), custom_call_target="tpu_custom_call" | custom-call | flops 3000000000 | bytes 1048576 | tf_op jit(solution)/shard_map/pallas_call | solution.py:294
  23.9 0.0 collective-permute-done.arrived.lon
  23.9 0.0 copy-done.4
  23.9 0.2 shard_map.148
  24.1 0.0 copy-start
  24.1 0.0 copy-start.2
  24.1 0.0 copy-start.3
  24.1 4.1 %collective-permute-start.1 = (bf16[144,192]{1,0:T(8,128)(2,1)S(1)}, bf16[144,192]{1,0:T(8,128)(2,1)S(1)}, u32[]{:S(2)}, u32[]{:S(2)}) collective-permute-start(bf16[144,192]{1,0:T(8,128)(2,1)S(1)} %shard_map.148), channel_id=1, source_target_pairs={{1,0},{2,1},{3,2},{4,3},{5,4},{6,5},{7,6},{0,7},{9,8},{10,9},{11,1... | collective-permute-start | bytes 165896 | tf_op jit(solution)/shard_map/ppermute | solution.py:315
  28.2 3.4 %shard_map.150.bias_b = f32[3,144,144]{2,1,0:T(8,128)S(1)} custom-call(s32[168,128]{1,0:T(8,128)S(1)} %get-tuple-element.29.packed, f32[156,128]{1,0:T(8,128)S(1)} %reshape.30.table, s32[144,1]{1,0:T(8,128)S(1)} %reshape.36.col, s32[1,144]{1,0:T(1,128)S(1)} %reshape.32.row), custom_call_target="tpu_custom_call" | custom-call | flops 3000000000 | bytes 1048576 | tf_op jit(solution)/shard_map/pallas_call | solution.py:294
  31.6 0.0 collective-permute-done.1.lat
  31.6 0.0 copy-done
  31.6 0.0 copy-done.2
  31.6 0.0 copy-done.3
  31.6 4.4 %shard_map.151 = (bf16[1152,128]{1,0:T(8,128)(2,1)}, f32[6,168,128]{2,1,0:T(8,128)S(1)}, bf16[144,576]{1,0:T(8,128)(2,1)S(1)}, f32[144,192]{1,0:T(8,128)S(1)}, f...) custom-call(bf16[144,192]{1,0:T(8,128)(2,1)S(1)} %get-tuple-element.25.kept, ...), custom_call_target="tpu_custom_call" | custom-call | flops 10000000000 | bytes 1048576 | tf_op jit(solution)/shard_map/pallas_call | solution.py:294
  36.0 4.1 %all-to-all-start = ((bf16[8,144,128]{2,1,0:T(8,128)(2,1)}), bf16[8,144,128]{2,1,0:T(8,128)(2,1)S(1)}, u32[]{:S(2)}, u32[]{:S(2)}) async-start(bf16[8,144,128]{2,1,0:T(8,128)(2,1)} %bitcast.3), calls=%async_computation | async-start | bytes 589824 | tf_op jit(solution)/shard_map/all_to_all | solution.py:305
  40.2 5.7 %shard_map.152.scattered = f32[192,128]{1,0:T(8,128)S(1)} custom-call(s32[168,128]{1,0:T(8,128)S(1)} %get-tuple-element.29.packed, f32[6,168,128]{2,1,0:T(8,128)S(1)} %get-tuple-element.31.ds), custom_call_target="tpu_custom_call" | custom-call | flops 5000000000 | bytes 1048576 | tf_op jit(solution)/shard_map/pallas_call | solution.py:294
  45.9 1.0 all-to-all-done.parts
  46.9 0.1 shard_map.153
  47.0 10.1 %all_to_all.25.parts = bf16[8,42,128]{2,1,0:T(8,128)(2,1)S(1)} all-to-all(bf16[8,42,128]{2,1,0:T(8,128)(2,1)S(1)} %shard_map.153), channel_id=1, replica_groups={{0,8,16,24,32,40,48,56},{64,72,80,88,96,104,112,120},{128,136,144,152,1..., dimensions={0} | all-to-all | bytes 172032 | tf_op jit(solution)/shard_map/all_to_all | solution.py:305
  57.1 15.6 %all_to_all.26.parts = bf16[12,42,128]{2,1,0:T(8,128)(2,1)S(1)} all-to-all(bf16[12,42,128]{2,1,0:T(8,128)(2,1)S(1)} %shard_map.154), channel_id=1, replica_groups={{0,64,128,192,256,320,384,448,512,576,640,704},{8,72,136,200,264,328,39..., dimensions={0} | all-to-all | bytes 258048 | tf_op jit(solution)/shard_map/all_to_all | solution.py:305
  72.7 0.7 shard_map.155
  73.3 0.0 copy-start.1
  73.3 3.5 %all-to-all-start.3 = ((bf16[8,42,128]{2,1,0:T(8,128)(2,1)}), bf16[8,42,128]{2,1,0:T(8,128)(2,1)S(1)}, u32[]{:S(2)}, u32[]{:S(2)}) async-start(bf16[8,42,128]{2,1,0:T(8,128)(2,1)} %shard_map.155), calls=%async_computation.3 | async-start | bytes 196608 | tf_op jit(solution)/shard_map/all_to_all | solution.py:305
  76.8 0.0 copy-done.1
  76.8 0.5 shard_map.156
  77.4 2.3 %collective-permute-start.2 = (bf16[2,40,192]{2,1,0:T(8,128)(2,1)S(1)}, bf16[2,40,192]{2,1,0:T(8,128)(2,1)S(1)}, u32[]{:S(2)}, u32[]{:S(2)}) collective-permute-start(bf16[2,40,192]{2,1,0:T(8,128)(2,1)S(1)} %get-tuple-element.40), channel_id=1, source_target_pairs={{7,0},{0,1},{1,2},{2,3},{3,4},{4,5},{5,6},{6,7},{15,8},{8,9},{9,10... | collective-permute-start | bytes 92168 | tf_op jit(solution)/shard_map/ppermute | solution.py:315
  79.7 4.6 %all-to-all-done.3.parts = bf16[8,42,128]{2,1,0:T(8,128)(2,1)S(1)} async-done(((bf16[8,42,128]{2,1,0:T(8,128)(2,1)}), bf16[8,42,128]{2,1,0:T(8,128)(2,1)S(1)}, u32[]{:S(2)}, u32[]{:S(2)}) %all-to-all-start.3) | async-done | bytes 86048 | tf_op jit(solution)/shard_map/all_to_all | solution.py:305
  84.3 0.8 shard_map.157
  85.1 0.2 collective-permute-done.2.first
  85.3 8.0 %all-to-all-start.4 = ((bf16[8,144,128]{2,1,0:T(8,128)(2,1)}), bf16[8,144,128]{2,1,0:T(8,128)(2,1)S(1)}, u32[]{:S(2)}, u32[]{:S(2)}) async-start(bf16[8,144,128]{2,1,0:T(8,128)(2,1)} %get-tuple-element.42), calls=%async_computation.4 | async-start | bytes 589824 | tf_op jit(solution)/shard_map/all_to_all | solution.py:305
  93.3 2.2 %collective-permute-start.3 = (bf16[2,40,192]{2,1,0:T(8,128)(2,1)S(1)}, bf16[2,40,192]{2,1,0:T(8,128)(2,1)S(1)}, u32[]{:S(2)}, u32[]{:S(2)}) collective-permute-start(bf16[2,40,192]{2,1,0:T(8,128)(2,1)S(1)} %pad_maximum_fusion), channel_id=1, source_target_pairs={{760,0},{0,8},{8,16},{16,24},{24,32},{32,40},{40,48},{48,56},{56,6... | collective-permute-start | bytes 92168 | tf_op jit(solution)/shard_map/ppermute | solution.py:315
  95.6 0.0 copy-start.5
  95.6 0.7 reshape.35
  96.3 5.1 %collective-permute-done.3.second = bf16[2,40,192]{2,1,0:T(8,128)(2,1)S(1)} collective-permute-done((bf16[2,40,192]{2,1,0:T(8,128)(2,1)S(1)}, bf16[2,40,192]{2,1,0:T(8,128)(2,1)S(1)}, u32[]{:S(2)}, u32[]{:S(2)}) %collective-permute-start.3) | collective-permute-done | bytes 30752 | tf_op jit(solution)/shard_map/ppermute | solution.py:315
  101.4 0.0 copy-done.5
  101.4 0.9 shard_map.158
  102.3 0.0 all-to-all-done.4.parts
  102.3 0.9 shard_map.159
  (10 shorter events, 0.1 us)
Async XLA Ops:
  0.6 19.6 %copy-start.7 = (s32[2,6,12]{2,0,1:T(2,128)S(1)}, s32[2,6,12]{2,0,1:T(2,128)}, u32[]{:S(2)}) copy-start(s32[2,6,12]{2,0,1:T(2,128)} %param.14) | copy-start | bytes 1732
  2.0 18.4 %copy-start.6 = (f32[3312,1,6]{0,1,2:T(1,128)S(1)}, f32[3312,1,6]{0,1,2:T(1,128)}, u32[]{:S(2)}) copy-start(f32[3312,1,6]{0,1,2:T(1,128)} %param.18) | copy-start | bytes 238468
  2.0 21.8 %collective-permute-start = (bf16[144,192]{1,0:T(8,128)(2,1)S(1)}, bf16[144,192]{1,0:T(8,128)(2,1)S(1)}, u32[]{:S(2)}, u32[]{:S(2)}) collective-permute-start(bf16[144,192]{1,0:T(8,128)(2,1)S(1)} %get-tuple-element.26), channel_id=1, source_target_pairs={{8,0},{16,8},{24,16},{32,24},{40,32},{48,40},{56,48},{64,56},{72,6... | collective-permute-start | bytes 165896 | tf_op jit(solution)/shard_map/ppermute | solution.py:315
  20.5 3.4 %copy-start.4 = (bf16[2,144,144]{2,1,0:T(8,128)(2,1)S(1)}, bf16[2,144,144]{2,1,0:T(8,128)(2,1)}, u32[]{:S(2)}) copy-start(bf16[2,144,144]{2,1,0:T(8,128)(2,1)} %constant.14.clone.sel) | copy-start | bytes 248836
  24.1 7.5 %copy-start = (bf16[192,576]{1,0:T(8,128)(2,1)S(1)}, bf16[192,576]{1,0:T(8,128)(2,1)}, u32[]{:S(2)}) copy-start(bf16[192,576]{1,0:T(8,128)(2,1)} %wqkv.3) | copy-start | bytes 663556
  24.1 7.5 %copy-start.2 = (bf16[192,192]{1,0:T(8,128)(2,1)S(1)}, bf16[192,192]{1,0:T(8,128)(2,1)}, u32[]{:S(2)}) copy-start(bf16[192,192]{1,0:T(8,128)(2,1)} %wproj.1) | copy-start | bytes 221188
  24.1 7.5 %copy-start.3 = (bf16[3,288,144]{2,1,0:T(8,128)(2,1)S(1)}, bf16[3,288,144]{2,1,0:T(8,128)(2,1)}, u32[]{:S(2)}) copy-start(bf16[3,288,144]{2,1,0:T(8,128)(2,1)} %constant.15.clone.sel) | copy-start | bytes 746500
  24.1 7.5 %collective-permute-start.1 = (bf16[144,192]{1,0:T(8,128)(2,1)S(1)}, bf16[144,192]{1,0:T(8,128)(2,1)S(1)}, u32[]{:S(2)}, u32[]{:S(2)}) collective-permute-start(bf16[144,192]{1,0:T(8,128)(2,1)S(1)} %shard_map.148), channel_id=1, source_target_pairs={{1,0},{2,1},{3,2},{4,3},{5,4},{6,5},{7,6},{0,7},{9,8},{10,9},{11,1... | collective-permute-start | bytes 165896 | tf_op jit(solution)/shard_map/ppermute | solution.py:315
  36.0 10.9 %all-to-all-start = ((bf16[8,144,128]{2,1,0:T(8,128)(2,1)}), bf16[8,144,128]{2,1,0:T(8,128)(2,1)S(1)}, u32[]{:S(2)}, u32[]{:S(2)}) async-start(bf16[8,144,128]{2,1,0:T(8,128)(2,1)} %bitcast.3), calls=%async_computation | async-start | bytes 589824 | tf_op jit(solution)/shard_map/all_to_all | solution.py:305
  73.3 3.5 %copy-start.1 = (bf16[160,144]{1,0:T(8,128)(2,1)S(1)}, bf16[160,144]{1,0:T(8,128)(2,1)}, u32[]{:S(2)}) copy-start(bf16[160,144]{1,0:T(8,128)(2,1)} %constant.16.clone.leave) | copy-start | bytes 138244
  73.3 11.0 %all-to-all-start.3 = ((bf16[8,42,128]{2,1,0:T(8,128)(2,1)}), bf16[8,42,128]{2,1,0:T(8,128)(2,1)S(1)}, u32[]{:S(2)}, u32[]{:S(2)}) async-start(bf16[8,42,128]{2,1,0:T(8,128)(2,1)} %shard_map.155), calls=%async_computation.3 | async-start | bytes 196608 | tf_op jit(solution)/shard_map/all_to_all | solution.py:305
  77.4 7.9 %collective-permute-start.2 = (bf16[2,40,192]{2,1,0:T(8,128)(2,1)S(1)}, bf16[2,40,192]{2,1,0:T(8,128)(2,1)S(1)}, u32[]{:S(2)}, u32[]{:S(2)}) collective-permute-start(bf16[2,40,192]{2,1,0:T(8,128)(2,1)S(1)} %get-tuple-element.40), channel_id=1, source_target_pairs={{7,0},{0,1},{1,2},{2,3},{3,4},{4,5},{5,6},{6,7},{15,8},{8,9},{9,10... | collective-permute-start | bytes 92168 | tf_op jit(solution)/shard_map/ppermute | solution.py:315
  85.3 17.0 %all-to-all-start.4 = ((bf16[8,144,128]{2,1,0:T(8,128)(2,1)}), bf16[8,144,128]{2,1,0:T(8,128)(2,1)S(1)}, u32[]{:S(2)}, u32[]{:S(2)}) async-start(bf16[8,144,128]{2,1,0:T(8,128)(2,1)} %get-tuple-element.42), calls=%async_computation.4 | async-start | bytes 589824 | tf_op jit(solution)/shard_map/all_to_all | solution.py:305
  93.3 8.1 %collective-permute-start.3 = (bf16[2,40,192]{2,1,0:T(8,128)(2,1)S(1)}, bf16[2,40,192]{2,1,0:T(8,128)(2,1)S(1)}, u32[]{:S(2)}, u32[]{:S(2)}) collective-permute-start(bf16[2,40,192]{2,1,0:T(8,128)(2,1)S(1)} %pad_maximum_fusion), channel_id=1, source_target_pairs={{760,0},{0,8},{8,16},{16,24},{24,32},{32,40},{40,48},{48,56},{56,6... | collective-permute-start | bytes 92168 | tf_op jit(solution)/shard_map/ppermute | solution.py:315
  95.6 5.8 %copy-start.5 = (bf16[4,144,40]{2,1,0:T(8,128)(2,1)S(1)}, bf16[4,144,40]{2,1,0:T(8,128)(2,1)}, u32[]{:S(2)}) copy-start(bf16[4,144,40]{2,1,0:T(8,128)(2,1)} %constant.17.clone.sel) | copy-start | bytes 138244

commit v6 on v4

--- a/solution.py
+++ b/solution.py
@@ -159,7 +159,7 @@
             flat[h, at, :] = totals[h]
         return carry
 
-    lax.fori_loop(0, PACK // 8, block, 0)
+    lax.fori_loop(0, PACK // 8, block, 0, unroll=7)
     same = col[...] == row[...]
     for h in range(HALF):
         bias[h, :, 0:128] = jnp.where(same[:, 0:128], flat[h, 0:T, :], -1e9)
@@ -204,19 +204,23 @@
     key_t = []
     value_t = []
     lane = lax.broadcasted_iota(jnp.int32, (24, 128), 1)
+    masks = [head == h for h in range(HEADS)]
+    scores = [dot(jnp.where(m, query, zero), key, 1, 1) * scale for m in masks]
+    grad_probs = [dot(jnp.where(m, att, zero), value, 1, 1) for m in masks]
+    probs = []
     for h in range(HEADS):
-        mine = head == h
-        scores = dot(jnp.where(mine, query, zero), key, 1, 1) * scale
-        scores = scores + (bias_a[h] if h < HALF else bias_b[h - HALF])
-        exponent = jnp.exp(scores - jnp.max(scores, axis=-1, keepdims=True))
-        prob = exponent * (1.0 / jnp.sum(exponent, axis=-1, keepdims=True))
-        prob_half = prob.astype(BF16)
-        attended = attended + dot(prob_half, jnp.where(mine, value, zero))
-        grad_prob = dot(jnp.where(mine, att, zero), value, 1, 1)
+        score = scores[h] + (bias_a[h] if h < HALF else bias_b[h - HALF])
+        exponent = jnp.exp(score - jnp.max(score, axis=-1, keepdims=True))
+        probs.append(exponent * (1.0 / jnp.sum(exponent, axis=-1, keepdims=True)))
+    for h in range(HEADS):
+        prob_half = probs[h].astype(BF16)
+        attended = attended + dot(prob_half, jnp.where(masks[h], value, zero))
         value_t.append(dot(att_t[HD * h : HD * h + HD], prob_half))
+    for h in range(HEADS):
+        prob, grad_prob = probs[h], grad_probs[h]
         ds = prob * (grad_prob - jnp.sum(grad_prob * prob, axis=-1, keepdims=True))
         ds_half = ds.astype(BF16)
-        grad_query = grad_query + dot(ds_half, jnp.where(mine, key, zero))
+        grad_query = grad_query + dot(ds_half, jnp.where(masks[h], key, zero))
         key_t.append(dot(query_t[HD * h : HD * h + HD], ds_half))
         ds_out[h, 0:T, :] = ds[:, 0:128]
         ds_tail[:, 0:16] = ds[:, 128:T]
@@ -258,28 +262,40 @@
 
 def scatter_kernel(packed, ds, out, total):
     total[...] = jnp.zeros_like(total)
-    blocks = lax.broadcasted_iota(jnp.int32, (32, 128), 0)
-    lows = lax.broadcasted_iota(jnp.int32, (128, 128), 0)
+    blocks = lax.broadcasted_iota(jnp.int32, (32, 128), 0).astype(F32).astype(BF16)
+    lows = lax.broadcasted_iota(jnp.int32, (128, 128), 0).astype(F32).astype(BF16)
+    one = jnp.ones((128, 128), BF16)
+    none = jnp.zeros((128, 128), BF16)
 
     def block(i, carry):
         at = pl.ds(pl.multiple_of(i * 8, 8), 8)
         position = packed[at, :]
-        low = position & 127
-        high = position >> 7
+        low = (position & 127).astype(F32)
+        high = (position >> 7).astype(F32)
         left = []
         right = []
         for r in range(8):
-            right.append(jnp.where(lows == low[r : r + 1], 1.0, 0.0).astype(BF16))
-            mine = blocks == high[r : r + 1]
+            low_row = jnp.broadcast_to(low[r : r + 1], (16, 128)).astype(BF16)
+            high_row = jnp.broadcast_to(high[r : r + 1], (16, 128)).astype(BF16)
+            right.append(
+                jnp.concatenate(
+                    [
+                        jnp.where(lows[16 * k : 16 * k + 16] == low_row, one[0:16], none[0:16])
+                        for k in range(8)
+                    ],
+                    axis=0,
+                )
+            )
+            mine = [blocks[16 * k : 16 * k + 16] == high_row for k in range(2)]
             parts = []
             for h in range(HEADS):
-                row = ds[h, at, :][r : r + 1]
-                parts.append(jnp.where(mine, row, 0.0).astype(BF16))
+                row = jnp.broadcast_to(ds[h, at, :][r : r + 1], (16, 128)).astype(BF16)
+                parts += [jnp.where(m, row, none[0:16]) for m in mine]
             left.append(jnp.concatenate(parts, axis=0))
         total[...] += dot(jnp.concatenate(left, axis=1), jnp.concatenate(right, axis=1), 1, 1)
         return carry
 
-    lax.fori_loop(0, PACK // 8, block, 0)
+    lax.fori_loop(0, PACK // 8, block, 0, unroll=7)
     out[...] = total[...]
 
 
@@ -289,11 +305,13 @@
     if copies:
         scratch.append(pltpu.SemaphoreType.DMA((copies,)))
         specs["in_specs"] = [pl.BlockSpec(memory_space=pltpu.MemorySpace.HBM)] * copies
+    if copies:
+        args = [pltpu.with_memory_space_constraint(a, pltpu.MemorySpace.HBM) for a in args]
     return pl.pallas_call(
         kernel,
         out_shape=[jax.ShapeDtypeStruct(s, d) for s, d in shapes],
         scratch_shapes=scratch,
-        compiler_params=pltpu.CompilerParams(vmem_limit_bytes=(56 if copies else 48) << 20),
+        compiler_params=pltpu.CompilerParams(vmem_limit_bytes=(48 if copies else 48) << 20),
         cost_estimate=pl.CostEstimate(flops=cost, bytes_accessed=1 << 20, transcendentals=0),
         **specs,
     )(*args)

time: 103 us -> 101 us (0.981)
  Pallas kernels: 23.5 us -> 15.8 us
  waiting for transfers between devices: 18 us -> 21.2 us
  starting transfers between devices: 48.1 us -> 51.1 us
    pallas_call x13, Pallas kernels: 23.5 us -> 15.8 us  [call(): pl.pallas_call(kernel, out_shape=[jax.ShapeDtypeStruct(s, d) for s, d in...]
    all_to_all x4, waiting for transfers between devices: 18 us -> 21.2 us  [exchange(): lax.all_to_all(block, axes, 0, 0, axis_index_groups=groups, tiled=False)]
    all_to_all x4, starting transfers between devices: 20.3 us -> 23.4 us  [exchange(): lax.all_to_all(block, axes, 0, 0, axis_index_groups=groups, tiled=False)]
  transfers between devices with their start and end apart: 8 -> 8, of which waited for: 4 -> 4; matrix products, arithmetic and copies ran while one was open for 1% -> 1% of each run, Pallas kernels for 15% -> 10%
where the time goes in v6:
time: 101 us; the launch traced here: 100 us
  starting transfers between devices  51.1 us (51%)
  waiting for transfers between devices  21.2 us (21%)
  Pallas kernels  15.8 us (16%)
  blocking collectives  10.1 us (10%)
  local copies, waits for them, and re-layouts  1.17 us (1%)
    ppermute x4, starting transfers between devices, moved(): lax.ppermute(block, axes, [((i + distance) % n, i) for i in range(n)])  27.7 us
    all_to_all x4, starting transfers between devices, exchange(): lax.all_to_all(block, axes, 0, 0, axis_index_groups=groups, tiled=False)  23.4 us
    all_to_all x4, waiting for transfers between devices, exchange(): lax.all_to_all(block, axes, 0, 0, axis_index_groups=groups, tiled=False)  21.2 us
    pallas_call x13, Pallas kernels, call(): pl.pallas_call(kernel, out_shape=[jax.ShapeDtypeStruct(s, d) for s, d in...  15.8 us
    all_to_all x1, blocking collectives, exchange(): lax.all_to_all(block, axes, 0, 0, axis_index_groups=groups, tiled=False)  10.1 us
  transfers between devices with their start and end apart: 8, of which 4 were waited for; matrix products, arithmetic and copies ran while one was open for 1% of the time, Pallas kernels for 10%

profile of v6, /device:TPU:1, one launch (start us, length us, event | category | flops | bytes accessed | tf_op | source)
XLA Modules:
  0.0 100.2 jit_solution(12126437802831264441)
XLA Ops:
  0.6 0.0 copy-start.7
  0.6 1.4 %shard_map.147 = (bf16[144,192]{1,0:T(8,128)(2,1)S(1)}, bf16[144,192]{1,0:T(8,128)(2,1)S(1)}, s32[168,128]{1,0:T(8,128)S(1)}) custom-call(bf16[6,12,2,192]{3,2,1,0:T(2,128)(2,1)} %bitcast.14, bf16[6,12,2,192]{3,2,1,0:T(2,128)(2,1)} %bitcast.15, bf16[288,288]{1,0:T(8,128)(2,1)} %constant.13.clone.sel, s32[144,144]{1,0:T(8,128)} %idx.1), custom_call_target="tpu_custom_call" | custom-call | flops 100000000 | bytes 1048576 | tf_op jit(solution)/shard_map/pallas_call | solution.py:310
  2.0 0.0 copy-start.6
  2.0 18.2 %collective-permute-start = (bf16[144,192]{1,0:T(8,128)(2,1)S(1)}, bf16[144,192]{1,0:T(8,128)(2,1)S(1)}, u32[]{:S(2)}, u32[]{:S(2)}) collective-permute-start(bf16[144,192]{1,0:T(8,128)(2,1)S(1)} %get-tuple-element.28), channel_id=1, source_target_pairs={{8,0},{16,8},{24,16},{32,24},{40,32},{48,40},{56,48},{64,56},{72,6... | collective-permute-start | bytes 165896 | tf_op jit(solution)/shard_map/ppermute | solution.py:331
  20.2 0.0 copy-done.7
  20.2 0.1 reshape.32.row
  20.3 0.1 reshape.36.col
  20.4 0.0 copy-done.6
  20.5 0.0 copy-start.4
  20.5 2.1 %shard_map.149.bias_a = f32[3,144,144]{2,1,0:T(8,128)S(1)} custom-call(s32[168,128]{1,0:T(8,128)S(1)} %get-tuple-element.31.packed, f32[156,128]{1,0:T(8,128)S(1)} %reshape.30.table, s32[144,1]{1,0:T(8,128)S(1)} %reshape.36.col, s32[1,144]{1,0:T(1,128)S(1)} %reshape.32.row), custom_call_target="tpu_custom_call" | custom-call | flops 3000000000 | bytes 1048576 | tf_op jit(solution)/shard_map/pallas_call | solution.py:310
  22.6 0.0 collective-permute-done.arrived.lon
  22.6 0.0 copy-done.4
  22.7 0.2 shard_map.148
  22.8 0.0 copy-start
  22.9 0.0 copy-start.2
  22.9 0.0 copy-start.3
  22.9 4.1 %collective-permute-start.1 = (bf16[144,192]{1,0:T(8,128)(2,1)S(1)}, bf16[144,192]{1,0:T(8,128)(2,1)S(1)}, u32[]{:S(2)}, u32[]{:S(2)}) collective-permute-start(bf16[144,192]{1,0:T(8,128)(2,1)S(1)} %shard_map.148), channel_id=1, source_target_pairs={{1,0},{2,1},{3,2},{4,3},{5,4},{6,5},{7,6},{0,7},{9,8},{10,9},{11,1... | collective-permute-start | bytes 165896 | tf_op jit(solution)/shard_map/ppermute | solution.py:331
  27.0 2.1 %shard_map.150.bias_b = f32[3,144,144]{2,1,0:T(8,128)S(1)} custom-call(s32[168,128]{1,0:T(8,128)S(1)} %get-tuple-element.31.packed, f32[156,128]{1,0:T(8,128)S(1)} %reshape.30.table, s32[144,1]{1,0:T(8,128)S(1)} %reshape.36.col, s32[1,144]{1,0:T(1,128)S(1)} %reshape.32.row), custom_call_target="tpu_custom_call" | custom-call | flops 3000000000 | bytes 1048576 | tf_op jit(solution)/shard_map/pallas_call | solution.py:310
  29.1 0.0 collective-permute-done.1.lat
  29.1 0.0 copy-done
  29.1 0.0 copy-done.2
  29.2 0.0 copy-done.3
  29.2 2.9 %shard_map.151 = (bf16[1152,128]{1,0:T(8,128)(2,1)}, f32[6,168,128]{2,1,0:T(8,128)S(1)}, bf16[144,576]{1,0:T(8,128)(2,1)S(1)}, f32[144,192]{1,0:T(8,128)S(1)}, f...) custom-call(bf16[144,192]{1,0:T(8,128)(2,1)S(1)} %get-tuple-element.27.kept, ...), custom_call_target="tpu_custom_call" | custom-call | flops 10000000000 | bytes 1048576 | tf_op jit(solution)/shard_map/pallas_call | solution.py:310
  32.0 5.4 %all-to-all-start = ((bf16[8,144,128]{2,1,0:T(8,128)(2,1)}), bf16[8,144,128]{2,1,0:T(8,128)(2,1)S(1)}, u32[]{:S(2)}, u32[]{:S(2)}) async-start(bf16[8,144,128]{2,1,0:T(8,128)(2,1)} %bitcast.3), calls=%async_computation | async-start | bytes 589824 | tf_op jit(solution)/shard_map/all_to_all | solution.py:321
  37.4 2.7 %shard_map.152.scattered = f32[192,128]{1,0:T(8,128)S(1)} custom-call(s32[168,128]{1,0:T(8,128)S(1)} %get-tuple-element.31.packed, f32[6,168,128]{2,1,0:T(8,128)S(1)} %get-tuple-element.33.ds), custom_call_target="tpu_custom_call" | custom-call | flops 5000000000 | bytes 1048576 | tf_op jit(solution)/shard_map/pallas_call | solution.py:310
  40.0 4.1 %all-to-all-done.parts = bf16[8,144,128]{2,1,0:T(8,128)(2,1)S(1)} async-done(((bf16[8,144,128]{2,1,0:T(8,128)(2,1)}), bf16[8,144,128]{2,1,0:T(8,128)(2,1)S(1)}, u32[]{:S(2)}, u32[]{:S(2)}) %all-to-all-start) | async-done | bytes 294944 | tf_op jit(solution)/shard_map/all_to_all | solution.py:321
  44.1 0.1 shard_map.153
  44.2 10.1 %all_to_all.25.parts = bf16[8,42,128]{2,1,0:T(8,128)(2,1)S(1)} all-to-all(bf16[8,42,128]{2,1,0:T(8,128)(2,1)S(1)} %shard_map.153), channel_id=1, replica_groups={{0,8,16,24,32,40,48,56},{64,72,80,88,96,104,112,120},{128,136,144,152,1..., dimensions={0} | all-to-all | bytes 172032 | tf_op jit(solution)/shard_map/all_to_all | solution.py:321
  54.2 0.7 shard_map.155
  54.9 0.0 copy-start.1
  54.9 6.4 %all-to-all-start.2 = ((bf16[12,42,128]{2,1,0:T(8,128)(2,1)}), bf16[12,42,128]{2,1,0:T(8,128)(2,1)S(1)}, u32[]{:S(2)}, u32[]{:S(2)}) async-start(bf16[12,42,128]{2,1,0:T(8,128)(2,1)} %shard_map.155), calls=%async_computation.2 | async-start | bytes 294912 | tf_op jit(solution)/shard_map/all_to_all | solution.py:321
  61.3 0.0 copy-done.1
  61.4 0.5 shard_map.154
  61.9 2.2 %collective-permute-start.2 = (bf16[2,40,192]{2,1,0:T(8,128)(2,1)S(1)}, bf16[2,40,192]{2,1,0:T(8,128)(2,1)S(1)}, u32[]{:S(2)}, u32[]{:S(2)}) collective-permute-start(bf16[2,40,192]{2,1,0:T(8,128)(2,1)S(1)} %get-tuple-element.41), channel_id=1, source_target_pairs={{7,0},{0,1},{1,2},{2,3},{3,4},{4,5},{5,6},{6,7},{15,8},{8,9},{9,10... | collective-permute-start | bytes 92168 | tf_op jit(solution)/shard_map/ppermute | solution.py:331
  64.1 8.0 %all-to-all-done.2.parts = bf16[12,42,128]{2,1,0:T(8,128)(2,1)S(1)} async-done(((bf16[12,42,128]{2,1,0:T(8,128)(2,1)}), bf16[12,42,128]{2,1,0:T(8,128)(2,1)S(1)}, u32[]{:S(2)}, u32[]{:S(2)}) %all-to-all-start.2) | async-done | bytes 129056 | tf_op jit(solution)/shard_map/all_to_all | solution.py:321
  72.1 0.7 shard_map.156
  72.8 0.0 collective-permute-done.2.first
  72.8 3.4 %all-to-all-start.3 = ((bf16[8,42,128]{2,1,0:T(8,128)(2,1)}), bf16[8,42,128]{2,1,0:T(8,128)(2,1)S(1)}, u32[]{:S(2)}, u32[]{:S(2)}) async-start(bf16[8,42,128]{2,1,0:T(8,128)(2,1)} %shard_map.156), calls=%async_computation.3 | async-start | bytes 196608 | tf_op jit(solution)/shard_map/all_to_all | solution.py:321
  76.2 3.3 %collective-permute-start.3 = (bf16[2,40,192]{2,1,0:T(8,128)(2,1)S(1)}, bf16[2,40,192]{2,1,0:T(8,128)(2,1)S(1)}, u32[]{:S(2)}, u32[]{:S(2)}) collective-permute-start(bf16[2,40,192]{2,1,0:T(8,128)(2,1)S(1)} %pad_maximum_fusion), channel_id=1, source_target_pairs={{760,0},{0,8},{8,16},{16,24},{24,32},{32,40},{40,48},{48,56},{56,6... | collective-permute-start | bytes 92168 | tf_op jit(solution)/shard_map/ppermute | solution.py:331
  79.4 4.2 %all-to-all-done.3.parts = bf16[8,42,128]{2,1,0:T(8,128)(2,1)S(1)} async-done(((bf16[8,42,128]{2,1,0:T(8,128)(2,1)}), bf16[8,42,128]{2,1,0:T(8,128)(2,1)S(1)}, u32[]{:S(2)}, u32[]{:S(2)}) %all-to-all-start.3) | async-done | bytes 86048 | tf_op jit(solution)/shard_map/all_to_all | solution.py:321
  83.6 0.8 shard_map.157
  84.4 0.0 collective-permute-done.3.second
  84.4 8.2 %all-to-all-start.4 = ((bf16[8,144,128]{2,1,0:T(8,128)(2,1)}), bf16[8,144,128]{2,1,0:T(8,128)(2,1)S(1)}, u32[]{:S(2)}, u32[]{:S(2)}) async-start(bf16[8,144,128]{2,1,0:T(8,128)(2,1)} %get-tuple-element.46), calls=%async_computation.4 | async-start | bytes 589824 | tf_op jit(solution)/shard_map/all_to_all | solution.py:321
  92.6 0.0 copy-start.5
  92.6 0.7 reshape.35
  93.3 0.2 copy-done.5
  93.5 0.9 shard_map.158
  94.4 4.9 %all-to-all-done.4.parts = bf16[8,144,128]{2,1,0:T(8,128)(2,1)S(1)} async-done(((bf16[8,144,128]{2,1,0:T(8,128)(2,1)}), bf16[8,144,128]{2,1,0:T(8,128)(2,1)S(1)}, u32[]{:S(2)}, u32[]{:S(2)}) %all-to-all-start.4) | async-done | bytes 294944 | tf_op jit(solution)/shard_map/all_to_all | solution.py:321
  99.3 0.9 shard_map.159
  (9 shorter events, 0.1 us)
Async XLA Ops:
  0.6 19.6 %copy-start.7 = (s32[2,6,12]{2,0,1:T(2,128)S(1)}, s32[2,6,12]{2,0,1:T(2,128)}, u32[]{:S(2)}) copy-start(s32[2,6,12]{2,0,1:T(2,128)} %param.14) | copy-start | bytes 1732
  2.0 18.4 %copy-start.6 = (f32[3312,1,6]{0,1,2:T(1,128)S(1)}, f32[3312,1,6]{0,1,2:T(1,128)}, u32[]{:S(2)}) copy-start(f32[3312,1,6]{0,1,2:T(1,128)} %param.18) | copy-start | bytes 238468
  2.0 20.6 %collective-permute-start = (bf16[144,192]{1,0:T(8,128)(2,1)S(1)}, bf16[144,192]{1,0:T(8,128)(2,1)S(1)}, u32[]{:S(2)}, u32[]{:S(2)}) collective-permute-start(bf16[144,192]{1,0:T(8,128)(2,1)S(1)} %get-tuple-element.28), channel_id=1, source_target_pairs={{8,0},{16,8},{24,16},{32,24},{40,32},{48,40},{56,48},{64,56},{72,6... | collective-permute-start | bytes 165896 | tf_op jit(solution)/shard_map/ppermute | solution.py:331
  20.5 2.2 %copy-start.4 = (bf16[2,144,144]{2,1,0:T(8,128)(2,1)S(1)}, bf16[2,144,144]{2,1,0:T(8,128)(2,1)}, u32[]{:S(2)}) copy-start(bf16[2,144,144]{2,1,0:T(8,128)(2,1)} %constant.14.clone.sel) | copy-start | bytes 248836
  22.8 6.3 %copy-start = (bf16[192,576]{1,0:T(8,128)(2,1)S(1)}, bf16[192,576]{1,0:T(8,128)(2,1)}, u32[]{:S(2)}) copy-start(bf16[192,576]{1,0:T(8,128)(2,1)} %wqkv.3) | copy-start | bytes 663556
  22.9 6.3 %copy-start.2 = (bf16[192,192]{1,0:T(8,128)(2,1)S(1)}, bf16[192,192]{1,0:T(8,128)(2,1)}, u32[]{:S(2)}) copy-start(bf16[192,192]{1,0:T(8,128)(2,1)} %wproj.1) | copy-start | bytes 221188
  22.9 6.3 %copy-start.3 = (bf16[3,288,144]{2,1,0:T(8,128)(2,1)S(1)}, bf16[3,288,144]{2,1,0:T(8,128)(2,1)}, u32[]{:S(2)}) copy-start(bf16[3,288,144]{2,1,0:T(8,128)(2,1)} %constant.15.clone.sel) | copy-start | bytes 746500
  22.9 6.2 %collective-permute-start.1 = (bf16[144,192]{1,0:T(8,128)(2,1)S(1)}, bf16[144,192]{1,0:T(8,128)(2,1)S(1)}, u32[]{:S(2)}, u32[]{:S(2)}) collective-permute-start(bf16[144,192]{1,0:T(8,128)(2,1)S(1)} %shard_map.148), channel_id=1, source_target_pairs={{1,0},{2,1},{3,2},{4,3},{5,4},{6,5},{7,6},{0,7},{9,8},{10,9},{11,1... | collective-permute-start | bytes 165896 | tf_op jit(solution)/shard_map/ppermute | solution.py:331
  32.0 12.1 %all-to-all-start = ((bf16[8,144,128]{2,1,0:T(8,128)(2,1)}), bf16[8,144,128]{2,1,0:T(8,128)(2,1)S(1)}, u32[]{:S(2)}, u32[]{:S(2)}) async-start(bf16[8,144,128]{2,1,0:T(8,128)(2,1)} %bitcast.3), calls=%async_computation | async-start | bytes 589824 | tf_op jit(solution)/shard_map/all_to_all | solution.py:321
  54.9 6.4 %copy-start.1 = (bf16[160,144]{1,0:T(8,128)(2,1)S(1)}, bf16[160,144]{1,0:T(8,128)(2,1)}, u32[]{:S(2)}) copy-start(bf16[160,144]{1,0:T(8,128)(2,1)} %constant.16.clone.leave) | copy-start | bytes 138244
  54.9 17.2 %all-to-all-start.2 = ((bf16[12,42,128]{2,1,0:T(8,128)(2,1)}), bf16[12,42,128]{2,1,0:T(8,128)(2,1)S(1)}, u32[]{:S(2)}, u32[]{:S(2)}) async-start(bf16[12,42,128]{2,1,0:T(8,128)(2,1)} %shard_map.155), calls=%async_computation.2 | async-start | bytes 294912 | tf_op jit(solution)/shard_map/all_to_all | solution.py:321
  61.9 10.9 %collective-permute-start.2 = (bf16[2,40,192]{2,1,0:T(8,128)(2,1)S(1)}, bf16[2,40,192]{2,1,0:T(8,128)(2,1)S(1)}, u32[]{:S(2)}, u32[]{:S(2)}) collective-permute-start(bf16[2,40,192]{2,1,0:T(8,128)(2,1)S(1)} %get-tuple-element.41), channel_id=1, source_target_pairs={{7,0},{0,1},{1,2},{2,3},{3,4},{4,5},{5,6},{6,7},{15,8},{8,9},{9,10... | collective-permute-start | bytes 92168 | tf_op jit(solution)/shard_map/ppermute | solution.py:331
  72.8 10.9 %all-to-all-start.3 = ((bf16[8,42,128]{2,1,0:T(8,128)(2,1)}), bf16[8,42,128]{2,1,0:T(8,128)(2,1)S(1)}, u32[]{:S(2)}, u32[]{:S(2)}) async-start(bf16[8,42,128]{2,1,0:T(8,128)(2,1)} %shard_map.156), calls=%async_computation.3 | async-start | bytes 196608 | tf_op jit(solution)/shard_map/all_to_all | solution.py:321
  76.2 8.2 %collective-permute-start.3 = (bf16[2,40,192]{2,1,0:T(8,128)(2,1)S(1)}, bf16[2,40,192]{2,1,0:T(8,128)(2,1)S(1)}, u32[]{:S(2)}, u32[]{:S(2)}) collective-permute-start(bf16[2,40,192]{2,1,0:T(8,128)(2,1)S(1)} %pad_maximum_fusion), channel_id=1, source_target_pairs={{760,0},{0,8},{8,16},{16,24},{24,32},{32,40},{40,48},{48,56},{56,6... | collective-permute-start | bytes 92168 | tf_op jit(solution)/shard_map/ppermute | solution.py:331
  84.4 15.0 %all-to-all-start.4 = ((bf16[8,144,128]{2,1,0:T(8,128)(2,1)}), bf16[8,144,128]{2,1,0:T(8,128)(2,1)S(1)}, u32[]{:S(2)}, u32[]{:S(2)}) async-start(bf16[8,144,128]{2,1,0:T(8,128)(2,1)} %get-tuple-element.46), calls=%async_computation.4 | async-start | bytes 589824 | tf_op jit(solution)/shard_map/all_to_all | solution.py:321
  92.6 0.9 copy-start.5

commit v7 on v6

--- a/solution.py
+++ b/solution.py
@@ -179,7 +179,7 @@
 
 
 def main_kernel(kept, lon, lat, sel, bias_a, bias_b, wqkv, wproj,
-                grads, ds_out, grad_in_out, normed_out, inv_std_out, cot_out, ds_tail):
+                grads, ds_out, grad_in_out, normed_out, inv_std_out, cot_out):
     scale = HD ** (-0.5)
     both = dot(sel[0], kept[...]) + dot(sel[1], lon[...]) + dot(sel[2], lat[...])
     values = both[0:T]
@@ -203,7 +203,6 @@
     grad_query = jnp.zeros((T, C), F32)
     key_t = []
     value_t = []
-    lane = lax.broadcasted_iota(jnp.int32, (24, 128), 1)
     masks = [head == h for h in range(HEADS)]
     scores = [dot(jnp.where(m, query, zero), key, 1, 1) * scale for m in masks]
     grad_probs = [dot(jnp.where(m, att, zero), value, 1, 1) for m in masks]
@@ -222,14 +221,7 @@
         ds_half = ds.astype(BF16)
         grad_query = grad_query + dot(ds_half, jnp.where(masks[h], key, zero))
         key_t.append(dot(query_t[HD * h : HD * h + HD], ds_half))
-        ds_out[h, 0:T, :] = ds[:, 0:128]
-        ds_tail[:, 0:16] = ds[:, 128:T]
-        packed = jnp.zeros((24, 128), F32)
-        for c in range(6):
-            part = ds_tail[24 * c : 24 * c + 24, :]
-            part = pltpu.roll(part, 16 * c, 1) if c else part
-            packed = jnp.where((lane >= 16 * c) & (lane < 16 * c + 16), part, packed)
-        ds_out[h, T:PACK, :] = packed
+        ds_out[h] = ds
     grad_key = jnp.concatenate(key_t, axis=0).T
     grad_value = jnp.concatenate(value_t, axis=0).T
     grad_in = jnp.concatenate((grad_query * scale, grad_key * scale, grad_value), axis=1)
@@ -260,7 +252,18 @@
         ret_strip[k] = parts[80 + 40 * k : 120 + 40 * k]
 
 
-def scatter_kernel(packed, ds, out, total):
+def scatter_kernel(packed, ds_in, out, total, ds, raw):
+    lane = lax.broadcasted_iota(jnp.int32, (24, 128), 1)
+    for h in range(HEADS):
+        ds[h, 0:T, :] = ds_in[h, :, 0:128]
+        raw[h, :, 0:16] = ds_in[h, :, 128:T]
+    for h in range(HEADS):
+        tail = jnp.zeros((24, 128), F32)
+        for c in range(6):
+            part = raw[h, 24 * c : 24 * c + 24, :]
+            part = pltpu.roll(part, 16 * c, 1) if c else part
+            tail = jnp.where((lane >= 16 * c) & (lane < 16 * c + 16), part, tail)
+        ds[h, T:PACK, :] = tail
     total[...] = jnp.zeros_like(total)
     blocks = lax.broadcasted_iota(jnp.int32, (32, 128), 0).astype(F32).astype(BF16)
     lows = lax.broadcasted_iota(jnp.int32, (128, 128), 0).astype(F32).astype(BF16)
@@ -361,13 +364,13 @@
         main_kernel,
         [
             ((6 * C, 128), BF16),
-            ((HEADS, PACK, 128), F32),
+            ((HEADS, T, T), F32),
             ((T, 3 * C), BF16),
             ((T, C), F32),
             ((T, 1), F32),
             block,
         ],
-        [((T, 128), F32)],
+        [],
         10**10,
         kept, lon, lat, gather, bias_a, bias_b, w_qkv, w_proj,
     )
@@ -376,24 +379,28 @@
     rows = 6 * C // n_lat
     grads = exchange(grads.reshape(n_lat, rows, 128), across)
     (scattered,) = call(
-        scatter_kernel, [((192, 128), F32)], [((192, 128), F32)], 5 * 10**9, packed, ds
-    )
+        scatter_kernel, [((192, 128), F32)],
+        [((192, 128), F32), ((HEADS, PACK, 128), F32), ((HEADS, T, 128), F32)],
+        5 * 10**9,
+        packed, ds,
+    )
+    quarter = ((2, 40, C), BF16)
+    ret_kept, ret_strip = call(
+        norm_kernel, [quarter] * 2, [], 10**8, grad_in, normed, inv_std, cot, w_qkv, leave
+    )
+    scattered, ret_strip = lax.optimization_barrier((scattered, ret_strip))
+    ret_first = moved(ret_strip, across, n_lat, -1)
     mixed_rows = (rows + 192) // n_y
     wide = [((rows, 128), F32)]
     (mixed,) = call(
         mix_kernel, [((n_y, mixed_rows, 128), BF16)], wide, 10**7, grads, scattered
     )
-    mixed, grad_in = lax.optimization_barrier((mixed, grad_in))
-    quarter = ((2, 40, C), BF16)
-    ret_kept, ret_strip = call(
-        norm_kernel, [quarter] * 2, [], 10**8, grad_in, normed, inv_std, cot, w_qkv, leave
-    )
-    ret_first = moved(ret_strip, across, n_lat, -1)
+    mixed, ret_first = lax.optimization_barrier((mixed, ret_first))
     mixed = exchange(mixed, "lon", rows_y)
     (mixed,) = call(sum_kernel, [((n_z, mixed_rows, 128), BF16)], [], 10**7, mixed)
     mixed = exchange(mixed, "lon", rows_z)
     (mixed,) = call(sum_kernel, [((n_y, mixed_rows, 128), BF16)], [], 10**7, mixed)
-    mixed, ret_first = lax.optimization_barrier((mixed, ret_first))
+    mixed, ret_kept = lax.optimization_barrier((mixed, ret_kept))
     ret_second = moved(jnp.stack((ret_kept[1], ret_first[1])), "lon", n_lon, -1)
     mixed = exchange(mixed, "lon", rows_y)
     grads, scattered = call(

time: 101 us -> 103 us (1.020)
  blocking collectives: 10.1 us -> 26.9 us
  waiting for transfers between devices: 21.2 us -> 11.2 us
  starting transfers between devices: 51.1 us -> 46.3 us
    all_to_all x1 -> x2, blocking collectives: 10.1 us -> 26.9 us  [exchange(): lax.all_to_all(block, axes, 0, 0, axis_index_groups=groups, tiled=False)]
    all_to_all x4 -> x3, waiting for transfers between devices: 21.2 us -> 8.45 us  [exchange(): lax.all_to_all(block, axes, 0, 0, axis_index_groups=groups, tiled=False)]
    all_to_all x4 -> x3, starting transfers between devices: 23.4 us -> 17.5 us  [exchange(): lax.all_to_all(block, axes, 0, 0, axis_index_groups=groups, tiled=False)]
    ppermute x4, waiting for transfers between devices: 0.01 us -> 2.76 us  [moved(): lax.ppermute(block, axes, [((i + distance) % n, i) for i in range(n)])]
    ppermute x4, starting transfers between devices: 27.7 us -> 28.8 us  [moved(): lax.ppermute(block, axes, [((i + distance) % n, i) for i in range(n)])]
  transfers between devices with their start and end apart: 8 -> 7, of which waited for: 4 -> 5; matrix products, arithmetic and copies ran while one was open for 1% -> 1% of each run, Pallas kernels for 10% -> 9%
where the time goes in v7:
time: 103 us; the launch traced here: 102 us
  starting transfers between devices  46.3 us (45%)
  blocking collectives  26.9 us (26%)
  Pallas kernels  15.2 us (15%)
  waiting for transfers between devices  11.2 us (11%)
  local copies, waits for them, and re-layouts  1.88 us (2%)
    ppermute x4, starting transfers between devices, moved(): lax.ppermute(block, axes, [((i + distance) % n, i) for i in range(n)])  28.8 us
    all_to_all x2, blocking collectives, exchange(): lax.all_to_all(block, axes, 0, 0, axis_index_groups=groups, tiled=False)  26.9 us
    all_to_all x3, starting transfers between devices, exchange(): lax.all_to_all(block, axes, 0, 0, axis_index_groups=groups, tiled=False)  17.5 us
    pallas_call x13, Pallas kernels, call(): pl.pallas_call(kernel, out_shape=[jax.ShapeDtypeStruct(s, d) for s, d in...  15.2 us
    all_to_all x3, waiting for transfers between devices, exchange(): lax.all_to_all(block, axes, 0, 0, axis_index_groups=groups, tiled=False)  8.45 us
    ppermute x4, waiting for transfers between devices, moved(): lax.ppermute(block, axes, [((i + distance) % n, i) for i in range(n)])  2.76 us
  transfers between devices with their start and end apart: 7, of which 5 were waited for; matrix products, arithmetic and copies ran while one was open for 1% of the time, Pallas kernels for 9%

profile of v7, /device:TPU:1, one launch (start us, length us, event | category | flops | bytes accessed | tf_op | source)
XLA Modules:
  0.0 102.4 jit_solution(14559834759376504458)
XLA Ops:
  0.6 0.0 copy-start.9
  0.6 1.4 %shard_map.147 = (bf16[144,192]{1,0:T(8,128)(2,1)S(1)}, bf16[144,192]{1,0:T(8,128)(2,1)S(1)}, s32[168,128]{1,0:T(8,128)S(1)}) custom-call(bf16[6,12,2,192]{3,2,1,0:T(2,128)(2,1)} %bitcast.14, bf16[6,12,2,192]{3,2,1,0:T(2,128)(2,1)} %bitcast.15, bf16[288,288]{1,0:T(8,128)(2,1)} %constant.13.clone.sel, s32[144,144]{1,0:T(8,128)} %idx.1), custom_call_target="tpu_custom_call" | custom-call | flops 100000000 | bytes 1048576 | tf_op jit(solution)/shard_map/pallas_call | solution.py:313
  2.0 0.0 copy-start.8
  2.0 18.2 %collective-permute-start = (bf16[144,192]{1,0:T(8,128)(2,1)S(1)}, bf16[144,192]{1,0:T(8,128)(2,1)S(1)}, u32[]{:S(2)}, u32[]{:S(2)}) collective-permute-start(bf16[144,192]{1,0:T(8,128)(2,1)S(1)} %get-tuple-element.30), channel_id=1, source_target_pairs={{8,0},{16,8},{24,16},{32,24},{40,32},{48,40},{56,48},{64,56},{72,6... | collective-permute-start | bytes 165896 | tf_op jit(solution)/shard_map/ppermute | solution.py:334
  20.2 0.0 copy-done.9
  20.2 0.1 reshape.32.row
  20.3 0.1 reshape.36.col
  20.4 0.0 copy-done.8
  20.5 0.0 copy-start.6
  20.5 2.1 %shard_map.149.bias_a = f32[3,144,144]{2,1,0:T(8,128)S(1)} custom-call(s32[168,128]{1,0:T(8,128)S(1)} %get-tuple-element.33.packed, f32[156,128]{1,0:T(8,128)S(1)} %reshape.30.table, s32[144,1]{1,0:T(8,128)S(1)} %reshape.36.col, s32[1,144]{1,0:T(1,128)S(1)} %reshape.32.row), custom_call_target="tpu_custom_call" | custom-call | flops 3000000000 | bytes 1048576 | tf_op jit(solution)/shard_map/pallas_call | solution.py:313
  22.6 0.0 collective-permute-done.arrived.lon
  22.6 0.0 copy-done.6
  22.7 0.2 shard_map.148
  22.8 0.0 copy-start
  22.9 0.0 copy-start.4
  22.9 0.0 copy-start.5
  22.9 4.1 %collective-permute-start.1 = (bf16[144,192]{1,0:T(8,128)(2,1)S(1)}, bf16[144,192]{1,0:T(8,128)(2,1)S(1)}, u32[]{:S(2)}, u32[]{:S(2)}) collective-permute-start(bf16[144,192]{1,0:T(8,128)(2,1)S(1)} %shard_map.148), channel_id=1, source_target_pairs={{1,0},{2,1},{3,2},{4,3},{5,4},{6,5},{7,6},{0,7},{9,8},{10,9},{11,1... | collective-permute-start | bytes 165896 | tf_op jit(solution)/shard_map/ppermute | solution.py:334
  27.0 2.1 %shard_map.150.bias_b = f32[3,144,144]{2,1,0:T(8,128)S(1)} custom-call(s32[168,128]{1,0:T(8,128)S(1)} %get-tuple-element.33.packed, f32[156,128]{1,0:T(8,128)S(1)} %reshape.30.table, s32[144,1]{1,0:T(8,128)S(1)} %reshape.36.col, s32[1,144]{1,0:T(1,128)S(1)} %reshape.32.row), custom_call_target="tpu_custom_call" | custom-call | flops 3000000000 | bytes 1048576 | tf_op jit(solution)/shard_map/pallas_call | solution.py:313
  29.1 0.0 collective-permute-done.1.lat
  29.1 0.0 copy-done
  29.1 0.0 copy-done.4
  29.2 0.0 copy-done.5
  29.2 2.8 %shard_map.151 = (bf16[1152,128]{1,0:T(8,128)(2,1)}, f32[6,144,144]{2,1,0:T(8,128)S(1)}, bf16[144,576]{1,0:T(8,128)(2,1)S(1)}, f32[144,192]{1,0:T(8,128)S(1)}, f...) custom-call(bf16[144,192]{1,0:T(8,128)(2,1)S(1)} %get-tuple-element.29.kept, ...), custom_call_target="tpu_custom_call" | custom-call | flops 10000000000 | bytes 1048576 | tf_op jit(solution)/shard_map/pallas_call | solution.py:313
  32.0 5.4 %all-to-all-start = ((bf16[8,144,128]{2,1,0:T(8,128)(2,1)}), bf16[8,144,128]{2,1,0:T(8,128)(2,1)S(1)}, u32[]{:S(2)}, u32[]{:S(2)}) async-start(bf16[8,144,128]{2,1,0:T(8,128)(2,1)} %bitcast.3), calls=%async_computation | async-start | bytes 589824 | tf_op jit(solution)/shard_map/all_to_all | solution.py:324
  37.3 0.0 copy-start.1
  37.3 2.8 %shard_map.152.scattered = f32[192,128]{1,0:T(8,128)S(1)} custom-call(s32[168,128]{1,0:T(8,128)S(1)} %get-tuple-element.33.packed, f32[6,144,144]{2,1,0:T(8,128)S(1)} %get-tuple-element.35.ds_in), custom_call_target="tpu_custom_call" | custom-call | flops 5000000000 | bytes 1048576 | tf_op jit(solution)/shard_map/pallas_call | solution.py:313
  40.2 0.0 copy-done.1
  40.2 0.5 shard_map.153
  40.7 3.3 %collective-permute-start.2 = (bf16[2,40,192]{2,1,0:T(8,128)(2,1)S(1)}, bf16[2,40,192]{2,1,0:T(8,128)(2,1)S(1)}, u32[]{:S(2)}, u32[]{:S(2)}) collective-permute-start(bf16[2,40,192]{2,1,0:T(8,128)(2,1)S(1)} %get-tuple-element.42), channel_id=1, source_target_pairs={{7,0},{0,1},{1,2},{2,3},{3,4},{4,5},{5,6},{6,7},{15,8},{8,9},{9,10... | collective-permute-start | bytes 92168 | tf_op jit(solution)/shard_map/ppermute | solution.py:334
  44.0 0.1 all-to-all-done.parts
  44.1 0.1 shard_map.154
  44.1 2.2 %collective-permute-done.2.first = bf16[2,40,192]{2,1,0:T(8,128)(2,1)S(1)} collective-permute-done((bf16[2,40,192]{2,1,0:T(8,128)(2,1)S(1)}, bf16[2,40,192]{2,1,0:T(8,128)(2,1)S(1)}, u32[]{:S(2)}, u32[]{:S(2)}) %collective-permute-start.2) | collective-permute-done | bytes 30752 | tf_op jit(solution)/shard_map/ppermute | solution.py:334
  46.3 0.0 copy-start.2
  46.3 10.0 %all_to_all.25.parts = bf16[8,42,128]{2,1,0:T(8,128)(2,1)S(1)} all-to-all(bf16[8,42,128]{2,1,0:T(8,128)(2,1)S(1)} %shard_map.154), channel_id=1, replica_groups={{0,8,16,24,32,40,48,56},{64,72,80,88,96,104,112,120},{128,136,144,152,1..., dimensions={0} | all-to-all | bytes 172032 | tf_op jit(solution)/shard_map/all_to_all | solution.py:324
  56.4 16.9 %all_to_all.26.parts = bf16[12,42,128]{2,1,0:T(8,128)(2,1)S(1)} all-to-all(bf16[12,42,128]{2,1,0:T(8,128)(2,1)S(1)} %shard_map.155), channel_id=1, replica_groups={{0,64,128,192,256,320,384,448,512,576,640,704},{8,72,136,200,264,328,39..., dimensions={0} | all-to-all | bytes 258048 | tf_op jit(solution)/shard_map/all_to_all | solution.py:324
  73.2 0.7 shard_map.156
  73.9 3.4 %all-to-all-start.3 = ((bf16[8,42,128]{2,1,0:T(8,128)(2,1)}), bf16[8,42,128]{2,1,0:T(8,128)(2,1)S(1)}, u32[]{:S(2)}, u32[]{:S(2)}) async-start(bf16[8,42,128]{2,1,0:T(8,128)(2,1)} %shard_map.156), calls=%async_computation.3 | async-start | bytes 196608 | tf_op jit(solution)/shard_map/all_to_all | solution.py:324
  77.3 0.0 copy-done.2
  77.3 0.0 slice-start
  77.3 0.7 slice-done
  78.0 3.3 %collective-permute-start.3 = (bf16[2,40,192]{2,1,0:T(8,128)(2,1)S(1)}, bf16[2,40,192]{2,1,0:T(8,128)(2,1)S(1)}, u32[]{:S(2)}, u32[]{:S(2)}) collective-permute-start(bf16[2,40,192]{2,1,0:T(8,128)(2,1)S(1)} %pad_maximum_fusion), channel_id=1, source_target_pairs={{760,0},{0,8},{8,16},{16,24},{24,32},{32,40},{40,48},{48,56},{56,6... | collective-permute-start | bytes 92168 | tf_op jit(solution)/shard_map/ppermute | solution.py:334
  81.3 3.5 %all-to-all-done.3.parts = bf16[8,42,128]{2,1,0:T(8,128)(2,1)S(1)} async-done(((bf16[8,42,128]{2,1,0:T(8,128)(2,1)}), bf16[8,42,128]{2,1,0:T(8,128)(2,1)S(1)}, u32[]{:S(2)}, u32[]{:S(2)}) %all-to-all-start.3) | async-done | bytes 86048 | tf_op jit(solution)/shard_map/all_to_all | solution.py:324
  84.8 0.8 shard_map.157
  85.5 0.6 collective-permute-done.3.second
  86.1 8.7 %all-to-all-start.4 = ((bf16[8,144,128]{2,1,0:T(8,128)(2,1)}), bf16[8,144,128]{2,1,0:T(8,128)(2,1)S(1)}, u32[]{:S(2)}, u32[]{:S(2)}) async-start(bf16[8,144,128]{2,1,0:T(8,128)(2,1)} %get-tuple-element.50), calls=%async_computation.4 | async-start | bytes 589824 | tf_op jit(solution)/shard_map/all_to_all | solution.py:324
  94.9 0.0 copy-start.7
  94.9 0.0 copy-start.3
  94.9 0.7 reshape.35
  95.6 0.2 copy-done.7
  95.8 0.0 copy-done.3
  95.8 0.9 shard_map.158
  96.6 4.9 %all-to-all-done.4.parts = bf16[8,144,128]{2,1,0:T(8,128)(2,1)S(1)} async-done(((bf16[8,144,128]{2,1,0:T(8,128)(2,1)}), bf16[8,144,128]{2,1,0:T(8,128)(2,1)S(1)}, u32[]{:S(2)}, u32[]{:S(2)}) %all-to-all-start.4) | async-done | bytes 294944 | tf_op jit(solution)/shard_map/all_to_all | solution.py:324
  101.6 0.9 shard_map.159
  (9 shorter events, 0.1 us)
Async XLA Ops:
  0.6 19.6 %copy-start.9 = (s32[2,6,12]{2,0,1:T(2,128)S(1)}, s32[2,6,12]{2,0,1:T(2,128)}, u32[]{:S(2)}) copy-start(s32[2,6,12]{2,0,1:T(2,128)} %param.14) | copy-start | bytes 1732
  2.0 18.4 %copy-start.8 = (f32[3312,1,6]{0,1,2:T(1,128)S(1)}, f32[3312,1,6]{0,1,2:T(1,128)}, u32[]{:S(2)}) copy-start(f32[3312,1,6]{0,1,2:T(1,128)} %param.18) | copy-start | bytes 238468
  2.0 20.6 %collective-permute-start = (bf16[144,192]{1,0:T(8,128)(2,1)S(1)}, bf16[144,192]{1,0:T(8,128)(2,1)S(1)}, u32[]{:S(2)}, u32[]{:S(2)}) collective-permute-start(bf16[144,192]{1,0:T(8,128)(2,1)S(1)} %get-tuple-element.30), channel_id=1, source_target_pairs={{8,0},{16,8},{24,16},{32,24},{40,32},{48,40},{56,48},{64,56},{72,6... | collective-permute-start | bytes 165896 | tf_op jit(solution)/shard_map/ppermute | solution.py:334
  20.5 2.2 %copy-start.6 = (bf16[2,144,144]{2,1,0:T(8,128)(2,1)S(1)}, bf16[2,144,144]{2,1,0:T(8,128)(2,1)}, u32[]{:S(2)}) copy-start(bf16[2,144,144]{2,1,0:T(8,128)(2,1)} %constant.14.clone.sel) | copy-start | bytes 248836
  22.8 6.3 %copy-start = (bf16[192,576]{1,0:T(8,128)(2,1)S(1)}, bf16[192,576]{1,0:T(8,128)(2,1)}, u32[]{:S(2)}) copy-start(bf16[192,576]{1,0:T(8,128)(2,1)} %wqkv.3) | copy-start | bytes 663556
  22.9 6.3 %copy-start.4 = (bf16[192,192]{1,0:T(8,128)(2,1)S(1)}, bf16[192,192]{1,0:T(8,128)(2,1)}, u32[]{:S(2)}) copy-start(bf16[192,192]{1,0:T(8,128)(2,1)} %wproj.1) | copy-start | bytes 221188
  22.9 6.3 %copy-start.5 = (bf16[3,288,144]{2,1,0:T(8,128)(2,1)S(1)}, bf16[3,288,144]{2,1,0:T(8,128)(2,1)}, u32[]{:S(2)}) copy-start(bf16[3,288,144]{2,1,0:T(8,128)(2,1)} %constant.15.clone.sel) | copy-start | bytes 746500
  22.9 6.2 %collective-permute-start.1 = (bf16[144,192]{1,0:T(8,128)(2,1)S(1)}, bf16[144,192]{1,0:T(8,128)(2,1)S(1)}, u32[]{:S(2)}, u32[]{:S(2)}) collective-permute-start(bf16[144,192]{1,0:T(8,128)(2,1)S(1)} %shard_map.148), channel_id=1, source_target_pairs={{1,0},{2,1},{3,2},{4,3},{5,4},{6,5},{7,6},{0,7},{9,8},{10,9},{11,1... | collective-permute-start | bytes 165896 | tf_op jit(solution)/shard_map/ppermute | solution.py:334
  32.0 12.1 %all-to-all-start = ((bf16[8,144,128]{2,1,0:T(8,128)(2,1)}), bf16[8,144,128]{2,1,0:T(8,128)(2,1)S(1)}, u32[]{:S(2)}, u32[]{:S(2)}) async-start(bf16[8,144,128]{2,1,0:T(8,128)(2,1)} %bitcast.3), calls=%async_computation | async-start | bytes 589824 | tf_op jit(solution)/shard_map/all_to_all | solution.py:324
  37.3 2.8 %copy-start.1 = (bf16[160,144]{1,0:T(8,128)(2,1)S(1)}, bf16[160,144]{1,0:T(8,128)(2,1)}, u32[]{:S(2)}) copy-start(bf16[160,144]{1,0:T(8,128)(2,1)} %constant.16.clone.leave) | copy-start | bytes 138244
  40.7 5.6 %collective-permute-start.2 = (bf16[2,40,192]{2,1,0:T(8,128)(2,1)S(1)}, bf16[2,40,192]{2,1,0:T(8,128)(2,1)S(1)}, u32[]{:S(2)}, u32[]{:S(2)}) collective-permute-start(bf16[2,40,192]{2,1,0:T(8,128)(2,1)S(1)} %get-tuple-element.42), channel_id=1, source_target_pairs={{7,0},{0,1},{1,2},{2,3},{3,4},{4,5},{5,6},{6,7},{15,8},{8,9},{9,10... | collective-permute-start | bytes 92168 | tf_op jit(solution)/shard_map/ppermute | solution.py:334
  46.3 31.0 %copy-start.2 = (bf16[2,40,192]{2,1,0:T(8,128)(2,1)}, bf16[2,40,192]{2,1,0:T(8,128)(2,1)S(1)}, u32[]{:S(2)}) copy-start(bf16[2,40,192]{2,1,0:T(8,128)(2,1)S(1)} %collective-permute-done.2.first) | copy-start | bytes 92164
  73.9 10.9 %all-to-all-start.3 = ((bf16[8,42,128]{2,1,0:T(8,128)(2,1)}), bf16[8,42,128]{2,1,0:T(8,128)(2,1)S(1)}, u32[]{:S(2)}, u32[]{:S(2)}) async-start(bf16[8,42,128]{2,1,0:T(8,128)(2,1)} %shard_map.156), calls=%async_computation.3 | async-start | bytes 196608 | tf_op jit(solution)/shard_map/all_to_all | solution.py:324
  77.3 0.7 slice-start
  78.0 8.1 %collective-permute-start.3 = (bf16[2,40,192]{2,1,0:T(8,128)(2,1)S(1)}, bf16[2,40,192]{2,1,0:T(8,128)(2,1)S(1)}, u32[]{:S(2)}, u32[]{:S(2)}) collective-permute-start(bf16[2,40,192]{2,1,0:T(8,128)(2,1)S(1)} %pad_maximum_fusion), channel_id=1, source_target_pairs={{760,0},{0,8},{8,16},{16,24},{24,32},{32,40},{40,48},{48,56},{56,6... | collective-permute-start | bytes 92168 | tf_op jit(solution)/shard_map/ppermute | solution.py:334
  86.1 15.5 %all-to-all-start.4 = ((bf16[8,144,128]{2,1,0:T(8,128)(2,1)}), bf16[8,144,128]{2,1,0:T(8,128)(2,1)S(1)}, u32[]{:S(2)}, u32[]{:S(2)}) async-start(bf16[8,144,128]{2,1,0:T(8,128)(2,1)} %get-tuple-element.50), calls=%async_computation.4 | async-start | bytes 589824 | tf_op jit(solution)/shard_map/all_to_all | solution.py:324
  94.9 0.9 copy-start.7
  94.9 0.9 copy-start.3

commit v8 on v6

--- a/solution.py
+++ b/solution.py
@@ -378,16 +378,16 @@
     (scattered,) = call(
         scatter_kernel, [((192, 128), F32)], [((192, 128), F32)], 5 * 10**9, packed, ds
     )
+    quarter = ((2, 40, C), BF16)
+    ret_kept, ret_strip = call(
+        norm_kernel, [quarter] * 2, [], 10**8, grad_in, normed, inv_std, cot, w_qkv, leave
+    )
     mixed_rows = (rows + 192) // n_y
     wide = [((rows, 128), F32)]
     (mixed,) = call(
         mix_kernel, [((n_y, mixed_rows, 128), BF16)], wide, 10**7, grads, scattered
     )
-    mixed, grad_in = lax.optimization_barrier((mixed, grad_in))
-    quarter = ((2, 40, C), BF16)
-    ret_kept, ret_strip = call(
-        norm_kernel, [quarter] * 2, [], 10**8, grad_in, normed, inv_std, cot, w_qkv, leave
-    )
+    mixed, ret_strip = lax.optimization_barrier((mixed, ret_strip))
     ret_first = moved(ret_strip, across, n_lat, -1)
     mixed = exchange(mixed, "lon", rows_y)
     (mixed,) = call(sum_kernel, [((n_z, mixed_rows, 128), BF16)], [], 10**7, mixed)

time: 101 us -> 101 us (level)
  no operation moved by 1% of the time
where the time goes in v8:
time: 101 us; the launch traced here: 100 us
  starting transfers between devices  51.1 us (51%)
  waiting for transfers between devices  21.2 us (21%)
  Pallas kernels  15.8 us (16%)
  blocking collectives  10.1 us (10%)
  local copies, waits for them, and re-layouts  1.17 us (1%)
    ppermute x4, starting transfers between devices, moved(): lax.ppermute(block, axes, [((i + distance) % n, i) for i in range(n)])  27.7 us
    all_to_all x4, starting transfers between devices, exchange(): lax.all_to_all(block, axes, 0, 0, axis_index_groups=groups, tiled=False)  23.4 us
    all_to_all x4, waiting for transfers between devices, exchange(): lax.all_to_all(block, axes, 0, 0, axis_index_groups=groups, tiled=False)  21.2 us
    pallas_call x13, Pallas kernels, call(): pl.pallas_call(kernel, out_shape=[jax.ShapeDtypeStruct(s, d) for s, d in...  15.8 us
    all_to_all x1, blocking collectives, exchange(): lax.all_to_all(block, axes, 0, 0, axis_index_groups=groups, tiled=False)  10.1 us
  transfers between devices with their start and end apart: 8, of which 4 were waited for; matrix products, arithmetic and copies ran while one was open for 1% of the time, Pallas kernels for 10%

profile of v8, /device:TPU:1, one launch (start us, length us, event | category | flops | bytes accessed | tf_op | source)
XLA Modules:
  0.0 100.2 jit_solution(3280800288905138619)
XLA Ops:
  0.6 0.0 copy-start.7
  0.6 1.4 %shard_map.147 = (bf16[144,192]{1,0:T(8,128)(2,1)S(1)}, bf16[144,192]{1,0:T(8,128)(2,1)S(1)}, s32[168,128]{1,0:T(8,128)S(1)}) custom-call(bf16[6,12,2,192]{3,2,1,0:T(2,128)(2,1)} %bitcast.14, bf16[6,12,2,192]{3,2,1,0:T(2,128)(2,1)} %bitcast.15, bf16[288,288]{1,0:T(8,128)(2,1)} %constant.13.clone.sel, s32[144,144]{1,0:T(8,128)} %idx.1), custom_call_target="tpu_custom_call" | custom-call | flops 100000000 | bytes 1048576 | tf_op jit(solution)/shard_map/pallas_call | solution.py:310
  2.0 0.0 copy-start.6
  2.0 18.2 %collective-permute-start = (bf16[144,192]{1,0:T(8,128)(2,1)S(1)}, bf16[144,192]{1,0:T(8,128)(2,1)S(1)}, u32[]{:S(2)}, u32[]{:S(2)}) collective-permute-start(bf16[144,192]{1,0:T(8,128)(2,1)S(1)} %get-tuple-element.28), channel_id=1, source_target_pairs={{8,0},{16,8},{24,16},{32,24},{40,32},{48,40},{56,48},{64,56},{72,6... | collective-permute-start | bytes 165896 | tf_op jit(solution)/shard_map/ppermute | solution.py:331
  20.2 0.0 copy-done.7
  20.2 0.1 reshape.32.row
  20.3 0.1 reshape.36.col
  20.4 0.0 copy-done.6
  20.5 0.0 copy-start.4
  20.5 2.1 %shard_map.149.bias_a = f32[3,144,144]{2,1,0:T(8,128)S(1)} custom-call(s32[168,128]{1,0:T(8,128)S(1)} %get-tuple-element.31.packed, f32[156,128]{1,0:T(8,128)S(1)} %reshape.30.table, s32[144,1]{1,0:T(8,128)S(1)} %reshape.36.col, s32[1,144]{1,0:T(1,128)S(1)} %reshape.32.row), custom_call_target="tpu_custom_call" | custom-call | flops 3000000000 | bytes 1048576 | tf_op jit(solution)/shard_map/pallas_call | solution.py:310
  22.6 0.0 collective-permute-done.arrived.lon
  22.6 0.0 copy-done.4
  22.7 0.2 shard_map.148
  22.8 0.0 copy-start
  22.9 0.0 copy-start.2
  22.9 0.0 copy-start.3
  22.9 4.1 %collective-permute-start.1 = (bf16[144,192]{1,0:T(8,128)(2,1)S(1)}, bf16[144,192]{1,0:T(8,128)(2,1)S(1)}, u32[]{:S(2)}, u32[]{:S(2)}) collective-permute-start(bf16[144,192]{1,0:T(8,128)(2,1)S(1)} %shard_map.148), channel_id=1, source_target_pairs={{1,0},{2,1},{3,2},{4,3},{5,4},{6,5},{7,6},{0,7},{9,8},{10,9},{11,1... | collective-permute-start | bytes 165896 | tf_op jit(solution)/shard_map/ppermute | solution.py:331
  27.0 2.1 %shard_map.150.bias_b = f32[3,144,144]{2,1,0:T(8,128)S(1)} custom-call(s32[168,128]{1,0:T(8,128)S(1)} %get-tuple-element.31.packed, f32[156,128]{1,0:T(8,128)S(1)} %reshape.30.table, s32[144,1]{1,0:T(8,128)S(1)} %reshape.36.col, s32[1,144]{1,0:T(1,128)S(1)} %reshape.32.row), custom_call_target="tpu_custom_call" | custom-call | flops 3000000000 | bytes 1048576 | tf_op jit(solution)/shard_map/pallas_call | solution.py:310
  29.1 0.0 collective-permute-done.1.lat
  29.1 0.0 copy-done
  29.1 0.0 copy-done.2
  29.2 0.0 copy-done.3
  29.2 2.9 %shard_map.151 = (bf16[1152,128]{1,0:T(8,128)(2,1)}, f32[6,168,128]{2,1,0:T(8,128)S(1)}, bf16[144,576]{1,0:T(8,128)(2,1)S(1)}, f32[144,192]{1,0:T(8,128)S(1)}, f...) custom-call(bf16[144,192]{1,0:T(8,128)(2,1)S(1)} %get-tuple-element.27.kept, ...), custom_call_target="tpu_custom_call" | custom-call | flops 10000000000 | bytes 1048576 | tf_op jit(solution)/shard_map/pallas_call | solution.py:310
  32.0 0.0 copy-start.1
  32.0 5.5 %all-to-all-start = ((bf16[8,144,128]{2,1,0:T(8,128)(2,1)}), bf16[8,144,128]{2,1,0:T(8,128)(2,1)S(1)}, u32[]{:S(2)}, u32[]{:S(2)}) async-start(bf16[8,144,128]{2,1,0:T(8,128)(2,1)} %bitcast.3), calls=%async_computation | async-start | bytes 589824 | tf_op jit(solution)/shard_map/all_to_all | solution.py:321
  37.5 0.0 copy-done.1
  37.5 0.5 shard_map.152
  38.0 2.7 %shard_map.153.scattered = f32[192,128]{1,0:T(8,128)S(1)} custom-call(s32[168,128]{1,0:T(8,128)S(1)} %get-tuple-element.31.packed, f32[6,168,128]{2,1,0:T(8,128)S(1)} %get-tuple-element.38.ds), custom_call_target="tpu_custom_call" | custom-call | flops 5000000000 | bytes 1048576 | tf_op jit(solution)/shard_map/pallas_call | solution.py:310
  40.7 3.5 %all-to-all-done.parts = bf16[8,144,128]{2,1,0:T(8,128)(2,1)S(1)} async-done(((bf16[8,144,128]{2,1,0:T(8,128)(2,1)}), bf16[8,144,128]{2,1,0:T(8,128)(2,1)S(1)}, u32[]{:S(2)}, u32[]{:S(2)}) %all-to-all-start) | async-done | bytes 294944 | tf_op jit(solution)/shard_map/all_to_all | solution.py:321
  44.2 0.1 shard_map.154
  44.3 10.1 %all_to_all.25.parts = bf16[8,42,128]{2,1,0:T(8,128)(2,1)S(1)} all-to-all(bf16[8,42,128]{2,1,0:T(8,128)(2,1)S(1)} %shard_map.154), channel_id=1, replica_groups={{0,8,16,24,32,40,48,56},{64,72,80,88,96,104,112,120},{128,136,144,152,1..., dimensions={0} | all-to-all | bytes 172032 | tf_op jit(solution)/shard_map/all_to_all | solution.py:321
  54.4 0.7 shard_map.155
  55.0 6.3 %all-to-all-start.2 = ((bf16[12,42,128]{2,1,0:T(8,128)(2,1)}), bf16[12,42,128]{2,1,0:T(8,128)(2,1)S(1)}, u32[]{:S(2)}, u32[]{:S(2)}) async-start(bf16[12,42,128]{2,1,0:T(8,128)(2,1)} %shard_map.155), calls=%async_computation.2 | async-start | bytes 294912 | tf_op jit(solution)/shard_map/all_to_all | solution.py:321
  61.3 2.2 %collective-permute-start.2 = (bf16[2,40,192]{2,1,0:T(8,128)(2,1)S(1)}, bf16[2,40,192]{2,1,0:T(8,128)(2,1)S(1)}, u32[]{:S(2)}, u32[]{:S(2)}) collective-permute-start(bf16[2,40,192]{2,1,0:T(8,128)(2,1)S(1)} %get-tuple-element.41), channel_id=1, source_target_pairs={{7,0},{0,1},{1,2},{2,3},{3,4},{4,5},{5,6},{6,7},{15,8},{8,9},{9,10... | collective-permute-start | bytes 92168 | tf_op jit(solution)/shard_map/ppermute | solution.py:331
  63.5 8.5 %all-to-all-done.2.parts = bf16[12,42,128]{2,1,0:T(8,128)(2,1)S(1)} async-done(((bf16[12,42,128]{2,1,0:T(8,128)(2,1)}), bf16[12,42,128]{2,1,0:T(8,128)(2,1)S(1)}, u32[]{:S(2)}, u32[]{:S(2)}) %all-to-all-start.2) | async-done | bytes 129056 | tf_op jit(solution)/shard_map/all_to_all | solution.py:321
  72.1 0.7 shard_map.156
  72.7 0.0 collective-permute-done.2.first
  72.8 3.4 %all-to-all-start.3 = ((bf16[8,42,128]{2,1,0:T(8,128)(2,1)}), bf16[8,42,128]{2,1,0:T(8,128)(2,1)S(1)}, u32[]{:S(2)}, u32[]{:S(2)}) async-start(bf16[8,42,128]{2,1,0:T(8,128)(2,1)} %shard_map.156), calls=%async_computation.3 | async-start | bytes 196608 | tf_op jit(solution)/shard_map/all_to_all | solution.py:321
  76.2 3.3 %collective-permute-start.3 = (bf16[2,40,192]{2,1,0:T(8,128)(2,1)S(1)}, bf16[2,40,192]{2,1,0:T(8,128)(2,1)S(1)}, u32[]{:S(2)}, u32[]{:S(2)}) collective-permute-start(bf16[2,40,192]{2,1,0:T(8,128)(2,1)S(1)} %pad_maximum_fusion), channel_id=1, source_target_pairs={{760,0},{0,8},{8,16},{16,24},{24,32},{32,40},{40,48},{48,56},{56,6... | collective-permute-start | bytes 92168 | tf_op jit(solution)/shard_map/ppermute | solution.py:331
  79.4 4.2 %all-to-all-done.3.parts = bf16[8,42,128]{2,1,0:T(8,128)(2,1)S(1)} async-done(((bf16[8,42,128]{2,1,0:T(8,128)(2,1)}), bf16[8,42,128]{2,1,0:T(8,128)(2,1)S(1)}, u32[]{:S(2)}, u32[]{:S(2)}) %all-to-all-start.3) | async-done | bytes 86048 | tf_op jit(solution)/shard_map/all_to_all | solution.py:321
  83.6 0.8 shard_map.157
  84.4 0.0 collective-permute-done.3.second
  84.4 8.2 %all-to-all-start.4 = ((bf16[8,144,128]{2,1,0:T(8,128)(2,1)}), bf16[8,144,128]{2,1,0:T(8,128)(2,1)S(1)}, u32[]{:S(2)}, u32[]{:S(2)}) async-start(bf16[8,144,128]{2,1,0:T(8,128)(2,1)} %get-tuple-element.46), calls=%async_computation.4 | async-start | bytes 589824 | tf_op jit(solution)/shard_map/all_to_all | solution.py:321
  92.6 0.0 copy-start.5
  92.6 0.7 reshape.35
  93.3 0.2 copy-done.5
  93.5 0.9 shard_map.158
  94.4 4.9 %all-to-all-done.4.parts = bf16[8,144,128]{2,1,0:T(8,128)(2,1)S(1)} async-done(((bf16[8,144,128]{2,1,0:T(8,128)(2,1)}), bf16[8,144,128]{2,1,0:T(8,128)(2,1)S(1)}, u32[]{:S(2)}, u32[]{:S(2)}) %all-to-all-start.4) | async-done | bytes 294944 | tf_op jit(solution)/shard_map/all_to_all | solution.py:321
  99.3 0.9 shard_map.159
  (9 shorter events, 0.1 us)
Async XLA Ops:
  0.6 19.6 %copy-start.7 = (s32[2,6,12]{2,0,1:T(2,128)S(1)}, s32[2,6,12]{2,0,1:T(2,128)}, u32[]{:S(2)}) copy-start(s32[2,6,12]{2,0,1:T(2,128)} %param.14) | copy-start | bytes 1732
  2.0 18.4 %copy-start.6 = (f32[3312,1,6]{0,1,2:T(1,128)S(1)}, f32[3312,1,6]{0,1,2:T(1,128)}, u32[]{:S(2)}) copy-start(f32[3312,1,6]{0,1,2:T(1,128)} %param.18) | copy-start | bytes 238468
  2.0 20.6 %collective-permute-start = (bf16[144,192]{1,0:T(8,128)(2,1)S(1)}, bf16[144,192]{1,0:T(8,128)(2,1)S(1)}, u32[]{:S(2)}, u32[]{:S(2)}) collective-permute-start(bf16[144,192]{1,0:T(8,128)(2,1)S(1)} %get-tuple-element.28), channel_id=1, source_target_pairs={{8,0},{16,8},{24,16},{32,24},{40,32},{48,40},{56,48},{64,56},{72,6... | collective-permute-start | bytes 165896 | tf_op jit(solution)/shard_map/ppermute | solution.py:331
  20.5 2.2 %copy-start.4 = (bf16[2,144,144]{2,1,0:T(8,128)(2,1)S(1)}, bf16[2,144,144]{2,1,0:T(8,128)(2,1)}, u32[]{:S(2)}) copy-start(bf16[2,144,144]{2,1,0:T(8,128)(2,1)} %constant.14.clone.sel) | copy-start | bytes 248836
  22.8 6.3 %copy-start = (bf16[192,576]{1,0:T(8,128)(2,1)S(1)}, bf16[192,576]{1,0:T(8,128)(2,1)}, u32[]{:S(2)}) copy-start(bf16[192,576]{1,0:T(8,128)(2,1)} %wqkv.3) | copy-start | bytes 663556
  22.9 6.3 %copy-start.2 = (bf16[192,192]{1,0:T(8,128)(2,1)S(1)}, bf16[192,192]{1,0:T(8,128)(2,1)}, u32[]{:S(2)}) copy-start(bf16[192,192]{1,0:T(8,128)(2,1)} %wproj.1) | copy-start | bytes 221188
  22.9 6.3 %copy-start.3 = (bf16[3,288,144]{2,1,0:T(8,128)(2,1)S(1)}, bf16[3,288,144]{2,1,0:T(8,128)(2,1)}, u32[]{:S(2)}) copy-start(bf16[3,288,144]{2,1,0:T(8,128)(2,1)} %constant.15.clone.sel) | copy-start | bytes 746500
  22.9 6.2 %collective-permute-start.1 = (bf16[144,192]{1,0:T(8,128)(2,1)S(1)}, bf16[144,192]{1,0:T(8,128)(2,1)S(1)}, u32[]{:S(2)}, u32[]{:S(2)}) collective-permute-start(bf16[144,192]{1,0:T(8,128)(2,1)S(1)} %shard_map.148), channel_id=1, source_target_pairs={{1,0},{2,1},{3,2},{4,3},{5,4},{6,5},{7,6},{0,7},{9,8},{10,9},{11,1... | collective-permute-start | bytes 165896 | tf_op jit(solution)/shard_map/ppermute | solution.py:331
  32.0 5.5 %copy-start.1 = (bf16[160,144]{1,0:T(8,128)(2,1)S(1)}, bf16[160,144]{1,0:T(8,128)(2,1)}, u32[]{:S(2)}) copy-start(bf16[160,144]{1,0:T(8,128)(2,1)} %constant.16.clone.leave) | copy-start | bytes 138244
  32.0 12.2 %all-to-all-start = ((bf16[8,144,128]{2,1,0:T(8,128)(2,1)}), bf16[8,144,128]{2,1,0:T(8,128)(2,1)S(1)}, u32[]{:S(2)}, u32[]{:S(2)}) async-start(bf16[8,144,128]{2,1,0:T(8,128)(2,1)} %bitcast.3), calls=%async_computation | async-start | bytes 589824 | tf_op jit(solution)/shard_map/all_to_all | solution.py:321
  55.0 17.0 %all-to-all-start.2 = ((bf16[12,42,128]{2,1,0:T(8,128)(2,1)}), bf16[12,42,128]{2,1,0:T(8,128)(2,1)S(1)}, u32[]{:S(2)}, u32[]{:S(2)}) async-start(bf16[12,42,128]{2,1,0:T(8,128)(2,1)} %shard_map.155), calls=%async_computation.2 | async-start | bytes 294912 | tf_op jit(solution)/shard_map/all_to_all | solution.py:321
  61.3 11.4 %collective-permute-start.2 = (bf16[2,40,192]{2,1,0:T(8,128)(2,1)S(1)}, bf16[2,40,192]{2,1,0:T(8,128)(2,1)S(1)}, u32[]{:S(2)}, u32[]{:S(2)}) collective-permute-start(bf16[2,40,192]{2,1,0:T(8,128)(2,1)S(1)} %get-tuple-element.41), channel_id=1, source_target_pairs={{7,0},{0,1},{1,2},{2,3},{3,4},{4,5},{5,6},{6,7},{15,8},{8,9},{9,10... | collective-permute-start | bytes 92168 | tf_op jit(solution)/shard_map/ppermute | solution.py:331
  72.8 10.9 %all-to-all-start.3 = ((bf16[8,42,128]{2,1,0:T(8,128)(2,1)}), bf16[8,42,128]{2,1,0:T(8,128)(2,1)S(1)}, u32[]{:S(2)}, u32[]{:S(2)}) async-start(bf16[8,42,128]{2,1,0:T(8,128)(2,1)} %shard_map.156), calls=%async_computation.3 | async-start | bytes 196608 | tf_op jit(solution)/shard_map/all_to_all | solution.py:321
  76.2 8.2 %collective-permute-start.3 = (bf16[2,40,192]{2,1,0:T(8,128)(2,1)S(1)}, bf16[2,40,192]{2,1,0:T(8,128)(2,1)S(1)}, u32[]{:S(2)}, u32[]{:S(2)}) collective-permute-start(bf16[2,40,192]{2,1,0:T(8,128)(2,1)S(1)} %pad_maximum_fusion), channel_id=1, source_target_pairs={{760,0},{0,8},{8,16},{16,24},{24,32},{32,40},{40,48},{48,56},{56,6... | collective-permute-start | bytes 92168 | tf_op jit(solution)/shard_map/ppermute | solution.py:331
  84.4 15.0 %all-to-all-start.4 = ((bf16[8,144,128]{2,1,0:T(8,128)(2,1)}), bf16[8,144,128]{2,1,0:T(8,128)(2,1)S(1)}, u32[]{:S(2)}, u32[]{:S(2)}) async-start(bf16[8,144,128]{2,1,0:T(8,128)(2,1)} %get-tuple-element.46), calls=%async_computation.4 | async-start | bytes 589824 | tf_op jit(solution)/shard_map/all_to_all | solution.py:321
  92.6 0.9 copy-start.5
